TPU v7x, 128 devices: a whole 4x4x4 slice. The times are simulated.
128 devices in a mesh: client: 4 (over x_hi, core), blk: 32 (over z, x_lo, y).
Axes of the slice: x: 4 (x_hi: 2, x_lo: 2; x = x_hi * 2 + x_lo), y: 4, z: 4, core: 2. Of those that a mesh axis runs over, the one named last changes fastest.
Arguments:
- activations: bfloat16 [8, 2, 32, 8, 1280], P('client', None, 'blk'), may hold values from -6 to 6
- sample_count: int32 [8], replicated, may hold values from 1 to 2, as said below
- client_weights: bfloat16 [8, 11520, 1280], P('client', 'blk'), may hold values from -6 to 6
Outputs:
- merged_gram: float32 [11520, 11520], P(('blk', 'client'))
- merged_rhs: float32 [11520, 1280], P(('blk', 'client'))
Inputs may be any that keep to these rules, and one draw needn't show every extreme that they name: `sample_count`: some client has all 2 slots live in every draw.
All inputs are finite; a program needn't handle non-finite values.
Results may differ from a plain program's by a relative error of at most 0.0029.
Values may be sent and summed in bfloat16 or wider, within the bound.
No kernel may reach another device: no remote copies, remote signals or barrier semaphores. Data moves between devices by JAX's collectives and lax.ppermute only.
A program may use at most 128 MiB of HBM per device.

v0:
```python
import jax
import jax.numpy as jnp
import numpy as np
from jax import lax
from jax.sharding import PartitionSpec as P

keep_off = 0.9


def patch_rows(images):
    groups, slots, img_height, img_width, channel_count = images.shape
    padded = jnp.pad(images, [(0, 0), (0, 0), (1, 1), (1, 1), (0, 0)])
    shifted = [
        padded[:, :, row_off : row_off + img_height, col_off : col_off + img_width, :]
        for row_off in range(3)
        for col_off in range(3)
    ]
    joined = jnp.concatenate(shifted, axis=-1)
    joined = joined.reshape(groups, slots * img_height * img_width, 9 * channel_count)
    column_order = (
        np.arange(9 * channel_count).reshape(9, channel_count).T.reshape(-1).astype(np.int32)
    )
    return jnp.take(joined, jnp.asarray(column_order), axis=2)


def body(activations, sample_count, client_weights):
    blk_count = lax.axis_size("blk")
    client_here = lax.axis_index("client")
    blk_here = lax.axis_index("blk")
    group_size = activations.shape[0]
    slot_count = activations.shape[1]
    pixel_count = activations.shape[2] * blk_count * activations.shape[3]
    client_total = sample_count.shape[0]
    mine_counts = lax.dynamic_slice_in_dim(sample_count, client_here * group_size, group_size)
    my_scale = 1.0 / (client_total * mine_counts.astype(jnp.float32) * pixel_count)
    live = lax.broadcasted_iota(jnp.int32, (group_size, slot_count), 1) < mine_counts[:, None]
    masked = jnp.where(live[:, :, None, None, None], activations, jnp.zeros_like(activations))
    tiles = lax.all_to_all(masked, "blk", split_axis=4, concat_axis=2, tiled=True)
    own_patch = patch_rows(tiles)
    tile_rows = own_patch.shape[2]
    partial_out = jnp.einsum(
        "irk,iko->rio", own_patch, client_weights, preferred_element_type=jnp.float32
    )
    summed_out = lax.psum(partial_out, "blk")
    out_bf = summed_out.astype(jnp.bfloat16)
    cross = jnp.einsum("irk,rio->iko", own_patch, out_bf, preferred_element_type=jnp.float32)
    diag_part = jnp.sum(jnp.square(own_patch.astype(jnp.float32)), axis=1)
    rhs_terms = keep_off * cross + (1.0 - keep_off) * diag_part[:, :, None] * client_weights.astype(
        jnp.float32
    )
    rhs_rows = jnp.sum(my_scale[:, None, None] * rhs_terms, axis=0)
    their_patch = patch_rows(lax.all_gather(tiles, "blk", axis=4, tiled=True))
    products = jnp.einsum(
        "irk,irl->ikl", own_patch, their_patch, preferred_element_type=jnp.float32
    )
    gram_rows = jnp.sum(my_scale[:, None, None] * products, axis=0)
    gram_mine, rhs_mine = (
        lax.psum_scatter(gram_rows, "client", scatter_dimension=0, tiled=True),
        lax.psum_scatter(rhs_rows, "client", scatter_dimension=0, tiled=True),
    )
    mine_rows = gram_mine.shape[0]
    first_diag = blk_here * tile_rows + client_here * mine_rows
    on_diag = (
        lax.broadcasted_iota(jnp.int32, gram_mine.shape, 1)
        == lax.broadcasted_iota(jnp.int32, gram_mine.shape, 0) + first_diag
    )
    gram_out = jnp.where(on_diag, gram_mine, keep_off * gram_mine)
    return (gram_out, rhs_mine)


def solution(mesh):
    in_specs = (P("client", None, "blk", None, None), P(), P("client", "blk", None))
    out_specs = (P(("blk", "client"), None), P(("blk", "client"), None))
    return jax.shard_map(body, mesh=mesh, in_specs=in_specs, out_specs=out_specs, check_vma=False)
```

profile of v0, /device:TPU:1, one launch (start us, length us, event | category | flops | bytes accessed | tf_op | source)
XLA Modules:
  0.0 705.3 jit_solution(4371708233687831579)
XLA Ops:
  8.9 1.6 copy.104
  10.6 2.0 reshape.74
  12.6 9.8 %all-to-all-start = ((bf16[32,2,640]{2,1,0:T(2,128)(2,1)}), bf16[32,2,640]{2,1,0:T(2,128)(2,1)S(1)}, u32[]{:S(2)}, u32[]{:S(2)}) async-start(bf16[32,2,640]{2,1,0:T(2,128)(2,1)} %reshape.74), calls=%async_computation | async-start | bytes 163840 | tf_op jit(solution)/shard_map/all_to_all | solution.py:38
  24.0 5.9 all-to-all-done
  31.4 1.7 copy.132
  33.1 2.5 copy.133
  38.8 1.9 copy.107
  42.6 1.7 copy.117
  48.1 1.6 constant_dynamic-update-slice_fusion.6
  54.7 3.4 gather_fusion
  59.0 4.0 convolution_bitcast_fusion
  63.0 218.7 %all-reduce.8 = bf16[512,2,1280]{2,0,1:T(8,128)(2,1)S(1)} all-reduce(f32[512,2,1280]{2,0,1:T(8,128)} %convolution_bitcast_fusion), channel_id=1, replica_groups=mesh['client'=4,'blk'=32] {'blk'}, use_global_device_ids=true, to_apply=%region_2.3 | all-reduce | flops 1310720 | bytes 7864320 | tf_op jit(solution)/shard_map/psum | solution.py:44
  281.7 4.2 fusion.17
  285.9 12.8 %copy.125 = bf16[2,2,32,1,8,1280]{5,4,2,1,0,3:T(8,128)(2,1)S(1)} copy(bf16[2,2,32,1,8,1280]{2,4,3,1,0,5:T(8,128)(2,1)} %all-gather.3.cloned.1.call-done) | data formatting | bytes 5242880 | tf_op jit(solution)/shard_map/all_gather | solution.py:52
  302.8 7.8 %copy-done = bf16[2,2,32,8,11520]{4,3,2,1,0:T(8,128)(2,1)} copy-done((bf16[2,2,32,8,11520]{4,3,2,1,0:T(8,128)(2,1)}, bf16[2,2,32,8,11520]{4,3,2,1,0:T(8,128)(2,1)S(1)}, u32[]{:S(2)}) %copy-start) | copy-done | bytes 23592984
  310.6 56.9 %copy.126 = bf16[2,512,11520]{1,0,2:T(2,128)(2,1)} copy(bf16[2,512,11520]{2,1,0:T(8,128)(2,1)} %bitcast.41) | data formatting | bytes 47185920 | tf_op jit(solution)/shard_map/reshape | solution.py:19
  367.5 72.3 %gather_fusion.1 = bf16[11520,2,512]{2,1,0:T(2,128)(2,1)} fusion(bf16[2,512,11520]{1,0,2:T(2,128)(2,1)} %copy.126, s32[12288]{0:T(1024)S(1)} %pad_clamp_fusion), kind=kCustom, calls=%fused_computation.1 | custom fusion | bytes 47232000 | tf_op jit(solution)/shard_map/jit(_take)/gather | solution.py:23
  439.8 32.9 %multiply_reduce_fusion = f32[360,11520]{1,0:T(8,128)} fusion(f32[2]{0:T(128)S(1)} %get-tuple-element.6, bf16[2,512,11520]{1,0,2:T(2,128)(2,1)} %bitcast.42, bf16[2,512,360]{1,0,2:T(2,128)(2,1)S(1)} %bitcast.47), kind=kOutput, calls=%fused_computation.2 | convolution fusion | flops 8505907200 | bytes 40919048 | tf_op jit(solution)/shard_map/irk,irl->ikl/dot_general | solution.py:53
  472.6 181.7 %fusion.23 = (f32[96,11520]{1,0:T(8,128)}, f32[96,1280]{1,0:T(8,128)S(1)}) fusion(f32[360,11520]{1,0:T(8,128)} %multiply_reduce_fusion, f32[360,1280]{1,0:T(8,128)S(1)} %copy-done.2), kind=kCustom, calls=%all-reduce-scatter.2 | all-reduce-scatter fusion | flops 4915201 | bytes 23347712
  655.7 5.9 collective-permute-start
  662.9 1.9 collective-permute-start.1
  664.8 10.4 %collective-permute-done.1 = f32[18,1280]{1,0:T(8,128)S(1)} collective-permute-done((f32[18,1280]{1,0:T(8,128)S(1)}, f32[18,1280]{1,0:T(8,128)S(1)}, u32[]{:S(2)}, u32[]{:S(2)}) %collective-permute-start.1) | collective-permute-done | bytes 92192
  676.5 16.8 %concatenate.36 = f32[114,11520]{1,0:T(8,128)} concatenate(f32[18,11520]{1,0:T(8,128)S(1)} %collective-permute-done, f32[96,11520]{1,0:T(8,128)} %get-tuple-element.4), dimensions={0} | concatenate | bytes 10506240
  693.3 5.2 multiply_select_fusion
  (60 shorter events, 26.9 us)
Async XLA Ops:
  12.6 17.2 %all-to-all-start = ((bf16[32,2,640]{2,1,0:T(2,128)(2,1)}), bf16[32,2,640]{2,1,0:T(2,128)(2,1)S(1)}, u32[]{:S(2)}, u32[]{:S(2)}) async-start(bf16[32,2,640]{2,1,0:T(2,128)(2,1)} %reshape.74), calls=%async_computation | async-start | bytes 163840 | tf_op jit(solution)/shard_map/all_to_all | solution.py:38
  22.4 263.4 %all-gather.3.cloned.1.call-start = ((), (), s32[]{:S(2)}) async-start(), calls=%async_computation.1 | async-start | bytes 10813440 | tf_op jit(solution)/shard_map/all_gather | solution.py:52
  38.8 20.2 %copy-start.1 = (bf16[2,360,1280]{2,1,0:T(8,128)(2,1)S(1)}, bf16[2,360,1280]{2,1,0:T(8,128)(2,1)}, u32[]{:S(2)}) copy-start(bf16[2,360,1280]{2,1,0:T(8,128)(2,1)} %param.7) | copy-start | bytes 5529604
  302.8 7.8 %copy-start = (bf16[2,2,32,8,11520]{4,3,2,1,0:T(8,128)(2,1)}, bf16[2,2,32,8,11520]{4,3,2,1,0:T(8,128)(2,1)S(1)}, u32[]{:S(2)}) copy-start(bf16[2,2,32,8,11520]{4,3,2,1,0:T(8,128)(2,1)S(1)} %fusion.15) | copy-start | bytes 70778880
  439.8 32.9 %copy-start.2 = (f32[360,1280]{1,0:T(8,128)S(1)}, f32[360,1280]{1,0:T(8,128)}, u32[]{:S(2)}) copy-start(f32[360,1280]{1,0:T(8,128)} %fusion.17) | copy-start | bytes 5529604
  472.6 189.0 %copy-start.3 = (u32[128]{0:T(128)S(1)}, u32[128]{0:T(128)}, u32[]{:S(2)}) copy-start(u32[128]{0:T(128)} %constant.95) | copy-start | bytes 1540
  655.7 20.8 %collective-permute-start = (f32[18,11520]{1,0:T(8,128)S(1)}, f32[18,11520]{1,0:T(8,128)S(1)}, u32[]{:S(2)}, u32[]{:S(2)}) collective-permute-start(f32[18,11520]{1,0:T(8,128)S(1)} %slice.70), channel_id=1, source_target_pairs={{0,32},{32,64},{64,96},{1,33},{33,65},{65,97},{2,34},{34,66},{66,9... | collective-permute-start | bytes 2488328
  662.9 12.4 %collective-permute-start.1 = (f32[18,1280]{1,0:T(8,128)S(1)}, f32[18,1280]{1,0:T(8,128)S(1)}, u32[]{:S(2)}, u32[]{:S(2)}) collective-permute-start(f32[18,1280]{1,0:T(8,128)S(1)} %slice.71), channel_id=1, source_target_pairs={{0,32},{32,64},{64,96},{1,33},{33,65},{65,97},{2,34},{34,66},{66,9... | collective-permute-start | bytes 276488
Sparse Core Ops, SparseCore 0:
  36.9 213.6 all-gather.2
where the time goes:
time: 708 us; the launch traced here: 705 us
  blocking collectives  400 us (56%)
  local copies, waits for them, and re-layouts  206 us (29%)
  matrix products  41 us (6%)
  starting transfers between devices  17.7 us (2%)
  waiting for transfers between devices  16.3 us (2%)
  between operations  15 us (2%)
  other arithmetic  9.34 us (1%)
    psum x1, blocking collectives, body(): summed_out = lax.psum(partial_out, 'blk')  219 us
    unnamed x1, blocking collectives  182 us
    gather x2, local copies, waits for them, and re-layouts, patch_rows(): return jnp.take(joined, jnp.asarray(column_order), axis=2)  75.6 us
    reshape x1, local copies, waits for them, and re-layouts, patch_rows(): joined.reshape(groups, slots * img_height * img_width, 9 * channel_count)  56.9 us
    unnamed x32, local copies, waits for them, and re-layouts  42.1 us
    dot_general x1, matrix products, body(): jnp.einsum('irk,irl->ikl', own_patch, their_patch, preferred_element_type...  32.9 us
  transfers between devices with their start and end apart: 4, of which 2 were waited for; matrix products, arithmetic and copies ran while one was open for 5% of the time, Pallas kernels for 0%

commit v1 on v0

v1 whole, which is shorter than its diff:
```python
import jax
import jax.numpy as jnp
import numpy as np
from jax import lax
from jax.experimental import pallas as pl
from jax.experimental.pallas import tpu as pltpu
from jax.sharding import PartitionSpec as P

keep_off = 0.9
AXES = ("client", "blk")
CHIPS = 4
ROWS = 32
CH = 1280
LANES = 1024
TAPS = 9
OWN = 10
MPAD = 96


def split_device(index):
    client, blk = divmod(index, 32)
    x_hi, core = divmod(client, 2)
    z, rest = divmod(blk, 8)
    x_lo, y = divmod(rest, 4)
    return x_hi * 2 + x_lo, y, z, core


def join_device(x, y, z, core):
    return ((x // 2) * 2 + core) * 32 + z * 8 + (x % 2) * 4 + y


def take_from(value, offset):
    pairs = []
    for dst in range(128):
        x, y, z, core = split_device(dst)
        src = join_device((x + offset[0]) % 4, (y + offset[1]) % 4, (z + offset[2]) % 4, core)
        pairs.append((src, dst))
    return lax.ppermute(value, AXES, pairs)


def vec_add(*vectors):
    return tuple(sum(parts) % 4 for parts in zip(*vectors))


STEP = (1, 0, 1)
FIRST = [tuple(k * s % 4 for s in STEP) for k in range(4)]
SECOND = [(0, 0, 0), (1, 1, 3), (0, 2, 0), (3, 3, 1)]
HEAD = [vec_add(g, f) for g in SECOND[:2] for f in FIRST]
TAIL = [vec_add(g, f) for g in SECOND[2:] for f in FIRST]
LAST = [((1, 0, 0), 0), ((0, 0, 3), 1), ((3, 0, 0), 0), ((0, 0, 1), 1), ((0, 1, 0), 0), ((0, 3, 0), 0)]
SOURCES = list(HEAD) + list(TAIL)
for away, part in LAST:
    SOURCES += [vec_add(away, o) for o in (TAIL if part else HEAD)]
assert len(set(SOURCES)) == 64


def gather_chips(block):
    level = jnp.concatenate([block] + [take_from(block, o) for o in FIRST[1:]], axis=0)
    level = jnp.concatenate([level] + [take_from(level, o) for o in SECOND[1:]], axis=0)
    halves = (level[:256], level[256:])
    return [level] + [take_from(halves[part], away) for away, part in LAST]


def assemble_kernel(slots, *refs):
    sources, out, sems = refs[:7], refs[7], refs[8]
    copies = []
    for t in range(64):
        if t < 16:
            src = sources[0].at[pl.ds(t * ROWS, ROWS)]
        else:
            piece, row = divmod(t - 16, 8)
            src = sources[1 + piece].at[pl.ds(row * ROWS, ROWS)]
        copies.append(pltpu.make_async_copy(src, out.at[slots[t]], sems.at[t]))
    for copy in copies:
        copy.start()
    for copy in copies:
        copy.wait()


def assemble(slots, pieces):
    return pl.pallas_call(
        assemble_kernel,
        out_shape=jax.ShapeDtypeStruct((64, ROWS, CH), jnp.bfloat16),
        grid_spec=pltpu.PrefetchScalarGridSpec(
            num_scalar_prefetch=1,
            grid=(1,),
            in_specs=[pl.BlockSpec(memory_space=pl.ANY)] * 7,
            out_specs=pl.BlockSpec(memory_space=pl.ANY),
            scratch_shapes=[pltpu.SemaphoreType.DMA((64,))],
        ),
        name="assemble",
    )(slots, *pieces)


def shift_lanes(value, row_off, col_off):
    amount = 32 * row_off + col_off
    moved = pltpu.roll(value, (-amount) % LANES, 1) if amount else value
    lane = lax.broadcasted_iota(jnp.int32, (1, LANES), 1)
    row = lane // 32 + row_off
    col = lane % 8 + col_off
    inside = (row >= 0) & (row < 32) & (col >= 0) & (col < 8)
    return jnp.where(inside, moved, 0.0)


def gram_kernel(first_ref, own_ref, other_ref, pick_ref, order_ref, spread_ref, scale_ref, out_ref, left, acc, high):
    pick = pick_ref[...]
    order = order_ref[...]
    for group in range(4):
        source = own_ref if group < 2 else other_ref
        pixels = source[pl.ds((group % 2) * LANES, LANES), :]
        slab = lax.dot_general(pick, pixels, (((1,), (1,)), ((), ())), preferred_element_type=jnp.float32)
        shifted = [shift_lanes(slab, t // 3 - 1, t % 3 - 1) for t in range(TAPS)]
        stacked = jnp.concatenate(shifted, axis=0).astype(jnp.bfloat16)
        patch = jnp.dot(order, stacked, preferred_element_type=jnp.float32)
        patch = patch * scale_ref[pl.ds(group, 1), :]
        for t in range(TAPS):
            left[pl.ds(t * MPAD, MPAD), pl.ds(group * LANES, LANES)] = shift_lanes(
                patch, 1 - t // 3, 1 - t % 3
            ).astype(jnp.bfloat16)

    @pl.loop(0, 5)
    def _(n):
        lanes = pl.ds(pl.multiple_of(n * 256, 256), 256)
        total = jnp.dot(left[:, pl.ds(0, 2048)], own_ref[:, lanes], preferred_element_type=jnp.float32)
        total += jnp.dot(left[:, pl.ds(2048, 2048)], other_ref[:, lanes], preferred_element_type=jnp.float32)
        acc[:, lanes] = total

    for block in range(10):
        for t in range(TAPS):
            part = acc[pl.ds(t * MPAD, MPAD), pl.ds(block * 128, 128)]
            top = part.astype(jnp.bfloat16)
            high[pl.ds(block * 2 * MPAD, MPAD), pl.ds(t * 128, 128)] = top
            high[pl.ds((block * 2 + 1) * MPAD, MPAD), pl.ds(t * 128, 128)] = (
                part - top.astype(jnp.float32)
            ).astype(jnp.bfloat16)

    first = first_ref[0]

    @pl.loop(0, 6)
    def _(step):
        half = step // 3
        piece = step % 3
        rows = pl.ds(pl.multiple_of(half * 960, 960), 960)
        cols = pl.ds(pl.multiple_of(piece * 384, 128), 384)
        wide = jnp.dot(high[rows, :], spread_ref[:, cols], preferred_element_type=jnp.float32)
        for b in range(5):
            value = wide[b * 192 : b * 192 + 96] + wide[b * 192 + 96 : b * 192 + 192]
            value = value[:90]
            base = half * 5760 + b * 1152 + piece * 384
            row = lax.broadcasted_iota(jnp.int32, value.shape, 0) + first
            col = lax.broadcasted_iota(jnp.int32, value.shape, 1) + base
            out_ref[:, pl.ds(pl.multiple_of(base, 128), 384)] = jnp.where(row == col, value, keep_off * value)


def gram(first, own, other, pick, order, spread, scale):
    whole = pl.BlockSpec(memory_space=pltpu.VMEM)
    return pl.pallas_call(
        gram_kernel,
        out_shape=jax.ShapeDtypeStruct((90, 11520), jnp.float32),
        in_specs=[pl.BlockSpec(memory_space=pltpu.SMEM)] + [whole] * 6,
        out_specs=whole,
        scratch_shapes=[
            pltpu.VMEM((TAPS * MPAD, 4 * LANES), jnp.bfloat16),
            pltpu.VMEM((TAPS * MPAD, CH), jnp.float32),
            pltpu.VMEM((20 * MPAD, TAPS * 128), jnp.bfloat16),
        ],
        compiler_params=pltpu.CompilerParams(vmem_limit_bytes=58 * 1024 * 1024),
        cost_estimate=pl.CostEstimate(flops=20_000_000_000, bytes_accessed=20_000_000, transcendentals=0),
        name="gram",
    )(first, own, other, pick, order, spread, scale)


def body(activations, sample_count, client_weights):
    client_here = lax.axis_index("client")
    blk_here = lax.axis_index("blk")
    x_hi, core = client_here // 2, client_here % 2
    z, x_lo, y = blk_here // 8, (blk_here // 4) % 2, blk_here % 4
    x = x_hi * 2 + x_lo

    counts = sample_count.astype(jnp.float32)
    all_scale = 1.0 / (8 * counts * 256)
    mine = lax.dynamic_slice_in_dim(sample_count, client_here * 2, 2)
    my_scale = lax.dynamic_slice_in_dim(all_scale, client_here * 2, 2)

    packed = client_weights.reshape(2, 40, TAPS, 32, 40).transpose(3, 1, 0, 2, 4).reshape(32, 40, 720)
    tiles = lax.all_to_all(packed, "blk", split_axis=0, concat_axis=0, tiled=True)
    tiles = tiles.reshape(CH, 2, 3, 3, 40)

    live = lax.broadcasted_iota(jnp.int32, (2, 2), 1) < mine[:, None]
    masked = jnp.where(live[:, :, None, None, None], activations, jnp.zeros_like(activations))
    pieces = gather_chips(masked.reshape(ROWS, CH))
    offs = np.array(SOURCES, np.int32)
    src_x, src_y, src_z = (x + offs[:, 0]) % 4, (y + offs[:, 1]) % 4, (z + offs[:, 2]) % 4
    away = (src_x // 2 != x_hi).astype(jnp.int32)
    slots = (away * 32 + src_z * 8 + (src_x % 2) * 4 + src_y).astype(jnp.int32)
    own = assemble(slots, pieces)
    other = lax.ppermute(own, AXES, [(d, d ^ 32) for d in range(128)])

    pixels = own[:32].reshape(32, 2, 2, 8, CH)
    outs = []
    for c in range(2):
        out = lax.conv_general_dilated(
            pixels[:, c], tiles[:, c], (1, 1), ((1, 1), (1, 1)),
            dimension_numbers=("HNWC", "IHWO", "HNWC"), preferred_element_type=jnp.float32,
        ).astype(jnp.bfloat16)
        outs.append(out * my_scale[c].astype(jnp.bfloat16))
    outs = jnp.stack(outs, axis=1).reshape(32, 4, 8, 40)
    cross = lax.conv_general_dilated(
        pixels.reshape(32, 4, 8, CH), outs, (1, 1), ((1, 1), (1, 1)),
        dimension_numbers=("HCWN", "HIWO", "NHWC"), preferred_element_type=jnp.float32,
    )
    square = jnp.square(pixels.astype(jnp.float32))
    by_col = jnp.sum(square, axis=(0, 2))
    top, bottom = jnp.sum(square[0], axis=1), jnp.sum(square[31], axis=1)
    by_row = jnp.stack([by_col - bottom, by_col, by_col - top], axis=1)
    full = jnp.sum(by_row, axis=2)
    diag = jnp.stack([full - by_row[:, :, 7], full, full - by_row[:, :, 0]], axis=2)
    weight = ((1.0 - keep_off) * my_scale)[:, None, None, None] * diag
    weight = weight.transpose(3, 0, 1, 2)
    rhs = keep_off * cross + jnp.sum(weight[..., None] * tiles.astype(jnp.float32), axis=1)
    sent = lax.all_to_all(
        rhs.reshape(128, OWN, TAPS, 40), ("blk", "client"), split_axis=0, concat_axis=0, tiled=True
    )
    rhs_out = jnp.sum(sent.reshape(32, 4, OWN, TAPS, 40), axis=1).transpose(1, 2, 0, 3).reshape(90, CH)

    first_channel = blk_here * 40 + client_here * OWN
    chan = lax.broadcasted_iota(jnp.int32, (16, CH), 1) - first_channel
    lane = lax.broadcasted_iota(jnp.int32, (16, CH), 0)
    pick = ((chan == lane) & (lane < OWN)).astype(jnp.bfloat16)
    row = lax.broadcasted_iota(jnp.int32, (MPAD, TAPS * 16), 0)
    col = lax.broadcasted_iota(jnp.int32, (MPAD, TAPS * 16), 1)
    order = ((row // TAPS == col % 16) & (row % TAPS == col // 16)).astype(jnp.bfloat16)
    row = lax.broadcasted_iota(jnp.int32, (1152, 1152), 0)
    col = lax.broadcasted_iota(jnp.int32, (1152, 1152), 1)
    spread = ((row % 128) * TAPS + row // 128 == col).astype(jnp.bfloat16)
    groups = jnp.stack([client_here, client_here ^ 2, client_here ^ 1, client_here ^ 3])
    group_scale = all_scale.reshape(4, 2)[groups]
    img_scale = jnp.repeat(jnp.repeat(group_scale, 16, axis=1)[:, None, :], 32, axis=1).reshape(4, LANES)
    gram_out = gram(
        jnp.reshape(first_channel * TAPS, (1,)), own.reshape(2048, CH), other.reshape(2048, CH),
        pick, order, spread, img_scale,
    )
    return gram_out, rhs_out


def solution(mesh):
    in_specs = (P("client", None, "blk", None, None), P(), P("client", "blk", None))
    out_specs = (P(("blk", "client"), None), P(("blk", "client"), None))
    return jax.shard_map(body, mesh=mesh, in_specs=in_specs, out_specs=out_specs, check_vma=False)
```

time: 708 us -> 455 us (0.64)
  blocking collectives: 400 us -> 0 us
  Pallas kernels: 0 us -> 192 us
  local copies, waits for them, and re-layouts: 206 us -> 99.2 us
  waiting for transfers between devices: 16.3 us -> 62.6 us
  starting transfers between devices: 17.7 us -> 52.7 us
  matrix products: 41 us -> 20.1 us
  other arithmetic: 9.34 us -> 24.6 us
  between operations: 15 us -> 1.21 us
    psum x1 -> x0, blocking collectives: 219 us -> none  [body(): summed_out = lax.psum(partial_out, 'blk')]
    pallas_call x0 -> x2, Pallas kernels: none -> 192 us  [the longest x1 161 us: assemble(): pl.pallas_call(assemble_kernel, out_shape=jax.ShapeDtypeStruct((64, ROWS,...]
    unnamed x1 -> x0, blocking collectives: 182 us -> none
    gather x2 -> x1, local copies, waits for them, and re-layouts: 75.6 us -> 0.56 us  [body(): group_scale = all_scale.reshape(4, 2)[groups]]
    ppermute x0 -> x13, starting transfers between devices: none -> 43.7 us  [the longest x12 22.6 us: take_from(): return lax.ppermute(value, AXES, pairs)]
    dot_general x3 -> x0, matrix products: 41 us -> none  [the longest x1 32.9 us: body(): jnp.einsum('irk,irl->ikl', own_patch, their_patch, preferred_element_type...]
    ppermute x0 -> x13, waiting for transfers between devices: none -> 40.8 us  [the longest x12 40.8 us: take_from(): return lax.ppermute(value, AXES, pairs)]
    unnamed x32 -> x33, local copies, waits for them, and re-layouts: 42.1 us -> 20.2 us
  transfers between devices with their start and end apart: 4 -> 15, of which waited for: 2 -> 7; matrix products, arithmetic and copies ran while one was open for 5% -> 31% of each run, Pallas kernels for 0% -> 36%
where the time goes in v1:
time: 455 us; the launch traced here: 452 us
  Pallas kernels  192 us (42%)
  local copies, waits for them, and re-layouts  99.2 us (22%)
  waiting for transfers between devices  62.6 us (14%)
  starting transfers between devices  52.7 us (12%)
  other arithmetic  24.6 us (5%)
  matrix products  20.1 us (4%)
    pallas_call x1, Pallas kernels, assemble(): pl.pallas_call(assemble_kernel, out_shape=jax.ShapeDtypeStruct((64, ROWS,...  161 us
    ppermute x12, waiting for transfers between devices, take_from(): return lax.ppermute(value, AXES, pairs)  40.8 us
    pallas_call x1, Pallas kernels, gram(): pl.pallas_call(gram_kernel, out_shape=jax.ShapeDtypeStruct((90, 11520), j...  30.9 us
    reshape x3, local copies, waits for them, and re-layouts, body(): client_weights.reshape(2, 40, TAPS, 32, 40).transpose(3, 1, 0, 2, 4)  27.8 us
    ppermute x12, starting transfers between devices, take_from(): return lax.ppermute(value, AXES, pairs)  22.6 us
    all_to_all x1, waiting for transfers between devices, body(): lax.all_to_all(rhs.reshape(128, OWN, TAPS, 40), ('blk', 'client'), split_...  21.8 us
    ppermute x1, starting transfers between devices, body(): other = lax.ppermute(own, AXES, [(d, d ^ 32) for d in range(128)])  21.1 us
    unnamed x33, local copies, waits for them, and re-layouts  20.2 us
  transfers between devices with their start and end apart: 15, of which 7 were waited for; matrix products, arithmetic and copies ran while one was open for 31% of the time, Pallas kernels for 36%

profile of v1, /device:TPU:1, one launch (start us, length us, event | category | flops | bytes accessed | tf_op | source)
XLA Modules:
  0.0 452.5 jit_solution(7948339066408560596)
XLA Ops:
  5.9 5.5 %collective-permute-start.1 = (bf16[32,1280]{1,0:T(8,128)(2,1)S(1)}, bf16[32,1280]{1,0:T(8,128)(2,1)S(1)}, u32[]{:S(2)}, u32[]{:S(2)}) collective-permute-start(bf16[32,1280]{1,0:T(8,128)(2,1)S(1)} %bitcast.86), channel_id=1, source_target_pairs={{80,0},{81,1},{82,2},{83,3},{84,4},{85,5},{86,6},{87,7},{88,8},{89... | collective-permute-start | bytes 245768 | tf_op jit(solution)/shard_map/ppermute | solution.py:38
  12.9 12.7 %reshape.263 = bf16[2,40,9,32,40]{4,3,2,1,0:T(8,128)(2,1)} reshape(bf16[2,360,1280]{2,1,0:T(8,128)(2,1)} %param.8) | data formatting | bytes 3686400 | tf_op jit(solution)/shard_map/reshape | solution.py:185
  25.6 8.8 %copy.51 = bf16[2,40,9,32,40]{1,4,2,0,3:T(8,128)(2,1)} copy(bf16[2,40,9,32,40]{4,3,2,1,0:T(8,128)(2,1)} %reshape.263) | data formatting | bytes 3686400 | tf_op jit(solution)/shard_map/reshape | solution.py:185
  34.4 6.4 %copy.52 = bf16[32,40,720]{2,1,0:T(8,128)(2,1)} copy(bf16[32,40,720]{1,2,0:T(8,128)(2,1)} %bitcast.78) | data formatting | bytes 3686400 | tf_op jit(solution)/shard_map/reshape | solution.py:185
  40.8 5.3 %all-to-all-start = ((bf16[32,40,720]{2,1,0:T(8,128)(2,1)}), bf16[32,40,720]{2,1,0:T(8,128)(2,1)}, u32[]{:S(2)}, u32[]{:S(2)}) async-start(bf16[32,40,720]{2,1,0:T(8,128)(2,1)} %copy.52), calls=%async_computation | async-start | bytes 3932160 | tf_op jit(solution)/shard_map/all_to_all | solution.py:186
  54.4 23.7 %collective-permute-done.3 = bf16[128,1280]{1,0:T(8,128)(2,1)S(1)} collective-permute-done((bf16[128,1280]{1,0:T(8,128)(2,1)S(1)}, bf16[128,1280]{1,0:T(8,128)(2,1)S(1)}, u32[]{:S(2)}, u32[]{:S(2)}) %collective-permute-start.3) | collective-permute-done | bytes 327712 | tf_op jit(solution)/shard_map/ppermute | solution.py:38
  82.0 7.6 %collective-permute-done.5 = bf16[128,1280]{1,0:T(8,128)(2,1)S(1)} collective-permute-done((bf16[128,1280]{1,0:T(8,128)(2,1)S(1)}, bf16[128,1280]{1,0:T(8,128)(2,1)S(1)}, u32[]{:S(2)}, u32[]{:S(2)}) %collective-permute-start.5) | collective-permute-done | bytes 327712 | tf_op jit(solution)/shard_map/ppermute | solution.py:38
  94.5 6.1 %collective-permute-done.7.refs_2_ = bf16[256,1280]{1,0:T(8,128)(2,1)S(1)} collective-permute-done((bf16[256,1280]{1,0:T(8,128)(2,1)S(1)}, bf16[256,1280]{1,0:T(8,128)(2,1)S(1)}, u32[]{:S(2)}, u32[]{:S(2)}) %collective-permute-start.7) | collective-permute-done | bytes 655392 | tf_op jit(solution)/shard_map/ppermute | solution.py:38
  104.0 161.2 %assemble.1 = bf16[64,32,1280]{2,1,0:T(8,128)(2,1)} custom-call(s32[64]{0:T(128)} %fusion.25.slots, bf16[512,1280]{1,0:T(8,128)(2,1)} %copy-done.1, bf16[256,1280]{1,0:T(8,128)(2,1)} %copy-done.4, bf16[256,1280]{1,0:T(8,128)(2,1)} %copy-done.6, bf16[256,1280]{1,0:T(8,128)(2,1)} %copy-done.5, bf16[256,1280]{1,0:T(8,128)(2,1)} %collective-permute-done.9.refs_4_, ...), custom_call_target="tpu_custom_call" | custom-call | tf_op jit(solution)/shard_map/assemble/pallas_call | solution.py:81
  265.2 21.1 %collective-permute-start.12 = (bf16[64,32,1280]{2,1,0:T(8,128)(2,1)}, bf16[64,32,1280]{2,1,0:T(8,128)(2,1)}, u32[]{:S(2)}, u32[]{:S(2)}) collective-permute-start(bf16[64,32,1280]{2,1,0:T(8,128)(2,1)} %assemble.1), channel_id=1, source_target_pairs={{0,32},{1,33},{2,34},{3,35},{4,36},{5,37},{6,38},{7,39},{8,40},{9,... | collective-permute-start | bytes 15728648 | tf_op jit(solution)/shard_map/ppermute | solution.py:197
  286.4 4.0 slice_bitcast_fusion.4
  297.3 9.8 %copy.53 = bf16[32,40,720]{1,0,2:T(8,128)(2,1)} copy(bf16[32,40,720]{2,1,0:T(8,128)(2,1)} %all-to-all-done) | data formatting | bytes 3686400 | tf_op jit(solution)/shard_map/all_to_all | solution.py:186
  307.1 9.3 %reshape.265 = bf16[1280,2,3,3,40]{0,4,3,2,1:T(8,128)(2,1)S(1)} reshape(bf16[32,40,720]{1,0,2:T(8,128)(2,1)} %copy.53) | data formatting | bytes 3686400 | tf_op jit(solution)/shard_map/reshape | solution.py:187
  316.5 7.2 %fusion.10 = bf16[32,1,2,8,40]{4,2,3,0,1:T(2,128)(2,1)S(1)} fusion(bf16[32,1,2,8,1280]{4,3,2,1,0:T(8,128)(2,1)S(1)} %copy-done.3, bf16[1280,2,3,3,40]{0,4,3,2,1:T(8,128)(2,1)S(1)} %reshape.265, bf16[]{:T(256)} %bitcast.19), kind=kOutput, calls=%fused_computation.19 | convolution fusion | flops 423567360 | bytes 2273282 | tf_op jit(solution)/shard_map/conv_general_dilated | solution.py:202
  323.7 7.1 %fusion.8 = bf16[32,1,2,8,40]{4,2,3,0,1:T(2,128)(2,1)S(1)} fusion(bf16[32,1,2,8,1280]{4,3,2,1,0:T(8,128)(2,1)S(1)} %copy-done.2, bf16[1280,2,3,3,40]{0,4,3,2,1:T(8,128)(2,1)S(1)} %reshape.265, bf16[]{:T(256)} %bitcast.15), kind=kOutput, calls=%fused_computation.17 | convolution fusion | flops 423567360 | bytes 2273282 | tf_op jit(solution)/shard_map/conv_general_dilated | solution.py:202
  333.0 5.8 %fusion.1 = f32[1280,3,3,40]{0,3,2,1:T(8,128)S(1)} fusion(f32[1280,3,3,40]{0,3,2,1:T(8,128)S(1)} %multiply_reduce_fusion.1, bf16[32,4,8,1280]{3,2,1,0:T(8,128)(2,1)S(1)} %copy-done, bf16[32,4,8,40]{3,2,1,0:T(8,128)(2,1)S(1)} %bitcast.92), kind=kOutput, calls=%fused_computation.8 | convolution fusion | flops 847974400 | bytes 6389760 | tf_op jit(solution)/shard_map/conv_general_dilated | solution.py:208
  342.6 8.2 %reshape.267 = f32[128,10,9,40]{3,1,0,2:T(8,128)} reshape(f32[1280,3,3,40]{3,0,2,1:T(8,128)} %copy.62) | data formatting | bytes 3686400 | tf_op jit(solution)/shard_map/reshape | solution.py:222
  350.9 7.9 %copy.96 = f32[128,10,9,40]{3,1,2,0:T(8,128)} copy(f32[128,10,9,40]{3,1,0,2:T(8,128)} %reshape.267) | data formatting | bytes 3686400 | tf_op jit(solution)/shard_map/reshape | solution.py:222
  358.8 8.8 %reshape.278 = f32[128,1,3600]{2,1,0:T(1,128)} reshape(f32[128,9,10,40]{3,2,1,0:T(8,128)} %bitcast.77) | data formatting | bytes 3686400
  377.6 21.8 %all-to-all-done.1 = f32[128,1,3600]{2,1,0:T(1,128)S(1)} async-done(((f32[128,1,3600]{2,1,0:T(1,128)}), f32[128,1,3600]{2,1,0:T(1,128)S(1)}, u32[]{:S(2)}, u32[]{:S(2)}) %all-to-all-start.1) | async-done | bytes 1843232 | tf_op jit(solution)/shard_map/all_to_all | solution.py:221
  399.9 7.0 %reduce.4 = f32[128,3600]{1,0:T(8,128)} reduce(f32[128,1,3600]{2,1,0:T(1,128)S(1)} %all-to-all-done.1, f32[]{:T(128)} %broadcast.198), dimensions={1}, to_apply=%all_to_all.7.reduce_sub_computation | reduce | bytes 3686404 | tf_op jit(solution)/shard_map/all_to_all | solution.py:221
  406.9 7.4 %reshape.279 = f32[128,9,10,40]{3,2,1,0:T(8,128)} reshape(f32[128,3600]{1,0:T(8,128)} %reduce.4) | data formatting | bytes 3686400
  414.2 5.0 %bitcast_reduce_fusion = f32[32,10,9,40]{3,1,2,0:T(8,128)S(1)} fusion(f32[128,9,10,40]{3,2,1,0:T(8,128)} %reshape.279), kind=kLoop, calls=%fused_computation.1 | loop fusion | flops 345600 | bytes 2304000 | tf_op jit(solution)/shard_map/reduce_sum | solution.py:224
  421.4 30.9 %gram.1 = f32[90,11520]{1,0:T(8,128)} custom-call(s32[1]{0:T(128)} %bitcast.first_ref, bf16[2048,1280]{1,0:T(8,128)(2,1)} %bitcast.81, bf16[2048,1280]{1,0:T(8,128)(2,1)} %bitcast.3.other_ref, bf16[16,1280]{1,0:T(8,128)(2,1)} %fusion.16.pick_ref, bf16[96,144]{1,0:T(8,128)(2,1)} %fusion.14.order_ref, bf16[1152,1152]{1,0:T(8,128)(2,1)} %fusion.spread_ref, ...), custom_call_target="tpu_custom_call" | custom-call | flops 20000000000 | bytes 20000000 | tf_op jit(solution)/shard_map/gram/pallas_call | solution.py:157
  (103 shorter events, 52.8 us)
Async XLA Ops:
  2.4 45.2 %collective-permute-start.2 = (bf16[32,1280]{1,0:T(8,128)(2,1)S(1)}, bf16[32,1280]{1,0:T(8,128)(2,1)S(1)}, u32[]{:S(2)}, u32[]{:S(2)}) collective-permute-start(bf16[32,1280]{1,0:T(8,128)(2,1)S(1)} %bitcast.85), channel_id=1, source_target_pairs={{92,0},{93,1},{94,2},{95,3},{24,4},{25,5},{26,6},{27,7},{68,8},{69... | collective-permute-start | bytes 245768 | tf_op jit(solution)/shard_map/ppermute | solution.py:38
  5.9 41.7 %collective-permute-start.1 = (bf16[32,1280]{1,0:T(8,128)(2,1)S(1)}, bf16[32,1280]{1,0:T(8,128)(2,1)S(1)}, u32[]{:S(2)}, u32[]{:S(2)}) collective-permute-start(bf16[32,1280]{1,0:T(8,128)(2,1)S(1)} %bitcast.86), channel_id=1, source_target_pairs={{80,0},{81,1},{82,2},{83,3},{84,4},{85,5},{86,6},{87,7},{88,8},{89... | collective-permute-start | bytes 245768 | tf_op jit(solution)/shard_map/ppermute | solution.py:38
  11.3 36.3 %collective-permute-start = (bf16[32,1280]{1,0:T(8,128)(2,1)S(1)}, bf16[32,1280]{1,0:T(8,128)(2,1)S(1)}, u32[]{:S(2)}, u32[]{:S(2)}) collective-permute-start(bf16[32,1280]{1,0:T(8,128)(2,1)S(1)} %bitcast.87), channel_id=1, source_target_pairs={{12,0},{13,1},{14,2},{15,3},{72,4},{73,5},{74,6},{75,7},{20,8},{21... | collective-permute-start | bytes 245768 | tf_op jit(solution)/shard_map/ppermute | solution.py:38
  40.8 6.0 %copy-start.10 = (s32[8]{0:T(128)S(1)}, s32[8]{0:T(128)}, u32[]{:S(2)}) copy-start(s32[8]{0:T(128)} %param.7) | copy-start | bytes 100
  40.8 256.5 %all-to-all-start = ((bf16[32,40,720]{2,1,0:T(8,128)(2,1)}), bf16[32,40,720]{2,1,0:T(8,128)(2,1)}, u32[]{:S(2)}, u32[]{:S(2)}) async-start(bf16[32,40,720]{2,1,0:T(8,128)(2,1)} %copy.52), calls=%async_computation | async-start | bytes 3932160 | tf_op jit(solution)/shard_map/all_to_all | solution.py:186
  47.7 34.3 %collective-permute-start.4 = (bf16[128,1280]{1,0:T(8,128)(2,1)S(1)}, bf16[128,1280]{1,0:T(8,128)(2,1)S(1)}, u32[]{:S(2)}, u32[]{:S(2)}) collective-permute-start(bf16[128,1280]{1,0:T(8,128)(2,1)S(1)} %pad_maximum_fusion), channel_id=1, source_target_pairs={{2,0},{3,1},{0,2},{1,3},{6,4},{7,5},{4,6},{5,7},{10,8},{11,9},{8,1... | collective-permute-start | bytes 983048 | tf_op jit(solution)/shard_map/ppermute | solution.py:38
  50.4 27.6 %collective-permute-start.3 = (bf16[128,1280]{1,0:T(8,128)(2,1)S(1)}, bf16[128,1280]{1,0:T(8,128)(2,1)S(1)}, u32[]{:S(2)}, u32[]{:S(2)}) collective-permute-start(bf16[128,1280]{1,0:T(8,128)(2,1)S(1)} %pad_maximum_fusion), channel_id=1, source_target_pairs={{29,0},{30,1},{31,2},{28,3},{89,4},{90,5},{91,6},{88,7},{5,8},{6,9... | collective-permute-start | bytes 983048 | tf_op jit(solution)/shard_map/ppermute | solution.py:38
  53.1 40.9 %copy-start.7 = (s32[64]{0:T(128)S(1)}, s32[64]{0:T(128)}, u32[]{:S(2)}) copy-start(s32[64]{0:T(128)} %constant.197.clone) | copy-start | bytes 772
  53.1 40.9 %copy-start.8 = (s32[64]{0:T(128)S(1)}, s32[64]{0:T(128)}, u32[]{:S(2)}) copy-start(s32[64]{0:T(128)} %constant.198.clone) | copy-start | bytes 772
  53.1 40.9 %copy-start.9 = (s32[64]{0:T(128)S(1)}, s32[64]{0:T(128)}, u32[]{:S(2)}) copy-start(s32[64]{0:T(128)} %constant.196.clone) | copy-start | bytes 772
  78.8 14.1 %collective-permute-start.6 = (bf16[256,1280]{1,0:T(8,128)(2,1)}, bf16[256,1280]{1,0:T(8,128)(2,1)S(1)}, u32[]{:S(2)}, u32[]{:S(2)}) collective-permute-start(bf16[256,1280]{1,0:T(8,128)(2,1)} %get-tuple-element.12), channel_id=1, source_target_pairs={{4,0},{5,1},{6,2},{7,3},{64,4},{65,5},{66,6},{67,7},{12,8},{13,9},... | collective-permute-start | bytes 1966088 | tf_op jit(solution)/shard_map/ppermute | solution.py:38
  78.9 10.7 %collective-permute-start.5 = (bf16[128,1280]{1,0:T(8,128)(2,1)S(1)}, bf16[128,1280]{1,0:T(8,128)(2,1)S(1)}, u32[]{:S(2)}, u32[]{:S(2)}) collective-permute-start(bf16[128,1280]{1,0:T(8,128)(2,1)S(1)} %pad_maximum_fusion), channel_id=1, source_target_pairs={{79,0},{76,1},{77,2},{78,3},{11,4},{8,5},{9,6},{10,7},{87,8},{84,9... | collective-permute-start | bytes 983048 | tf_op jit(solution)/shard_map/ppermute | solution.py:38
  81.9 20.4 %collective-permute-start.8 = (bf16[256,1280]{1,0:T(8,128)(2,1)}, bf16[256,1280]{1,0:T(8,128)(2,1)S(1)}, u32[]{:S(2)}, u32[]{:S(2)}) collective-permute-start(bf16[256,1280]{1,0:T(8,128)(2,1)} %get-tuple-element.12), channel_id=1, source_target_pairs={{68,0},{69,1},{70,2},{71,3},{0,4},{1,5},{2,6},{3,7},{76,8},{77,9},... | collective-permute-start | bytes 1966088 | tf_op jit(solution)/shard_map/ppermute | solution.py:38
  89.6 14.4 %copy-start.1 = (bf16[512,1280]{1,0:T(8,128)(2,1)}, bf16[512,1280]{1,0:T(8,128)(2,1)S(1)}, u32[]{:S(2)}) copy-start(bf16[512,1280]{1,0:T(8,128)(2,1)S(1)} %get-tuple-element.9.refs_0_) | copy-start | bytes 3932164
  89.6 11.0 %collective-permute-start.7 = (bf16[256,1280]{1,0:T(8,128)(2,1)S(1)}, bf16[256,1280]{1,0:T(8,128)(2,1)S(1)}, u32[]{:S(2)}, u32[]{:S(2)}) collective-permute-start(bf16[256,1280]{1,0:T(8,128)(2,1)S(1)} %get-tuple-element.8), channel_id=1, source_target_pairs={{24,0},{25,1},{26,2},{27,3},{28,4},{29,5},{30,6},{31,7},{0,8},{1,9... | collective-permute-start | bytes 1966088 | tf_op jit(solution)/shard_map/ppermute | solution.py:38
  89.7 13.1 %collective-permute-start.9 = (bf16[256,1280]{1,0:T(8,128)(2,1)S(1)}, bf16[256,1280]{1,0:T(8,128)(2,1)}, u32[]{:S(2)}, u32[]{:S(2)}) collective-permute-start(bf16[256,1280]{1,0:T(8,128)(2,1)S(1)} %get-tuple-element.8), channel_id=1, source_target_pairs={{8,0},{9,1},{10,2},{11,3},{12,4},{13,5},{14,6},{15,7},{16,8},{17,9... | collective-permute-start | bytes 1966088 | tf_op jit(solution)/shard_map/ppermute | solution.py:38
  92.4 10.4 %collective-permute-start.10 = (bf16[256,1280]{1,0:T(8,128)(2,1)}, bf16[256,1280]{1,0:T(8,128)(2,1)}, u32[]{:S(2)}, u32[]{:S(2)}) collective-permute-start(bf16[256,1280]{1,0:T(8,128)(2,1)} %get-tuple-element.12), channel_id=1, source_target_pairs={{1,0},{2,1},{3,2},{0,3},{5,4},{6,5},{7,6},{4,7},{9,8},{10,9},{11,1... | collective-permute-start | bytes 1966088 | tf_op jit(solution)/shard_map/ppermute | solution.py:38
  92.9 11.2 %copy-start.4 = (bf16[256,1280]{1,0:T(8,128)(2,1)}, bf16[256,1280]{1,0:T(8,128)(2,1)S(1)}, u32[]{:S(2)}) copy-start(bf16[256,1280]{1,0:T(8,128)(2,1)S(1)} %collective-permute-done.6.refs_1_) | copy-start | bytes 1966084
  92.9 11.2 %collective-permute-start.11 = (bf16[256,1280]{1,0:T(8,128)(2,1)}, bf16[256,1280]{1,0:T(8,128)(2,1)}, u32[]{:S(2)}, u32[]{:S(2)}) collective-permute-start(bf16[256,1280]{1,0:T(8,128)(2,1)} %get-tuple-element.12), channel_id=1, source_target_pairs={{3,0},{0,1},{1,2},{2,3},{7,4},{4,5},{5,6},{6,7},{11,8},{8,9},{9,10... | collective-permute-start | bytes 1966088 | tf_op jit(solution)/shard_map/ppermute | solution.py:38
  265.2 156.2 %collective-permute-start.12 = (bf16[64,32,1280]{2,1,0:T(8,128)(2,1)}, bf16[64,32,1280]{2,1,0:T(8,128)(2,1)}, u32[]{:S(2)}, u32[]{:S(2)}) collective-permute-start(bf16[64,32,1280]{2,1,0:T(8,128)(2,1)} %assemble.1), channel_id=1, source_target_pairs={{0,32},{1,33},{2,34},{3,35},{4,36},{5,37},{6,38},{7,39},{8,40},{9,... | collective-permute-start | bytes 15728648 | tf_op jit(solution)/shard_map/ppermute | solution.py:197
  286.4 7.1 %slice-start = ((s8[5242880]{0:T(1024)(128)(4,1)}), s8[1048576]{0:T(1024)(128)(4,1)S(1)}, s32[]{:S(2)}) async-start(s8[5242880]{0:T(1024)(128)(4,1)} %bitcast.82), calls=%async_computation.2 | async-start | bytes 2097152
  307.1 9.3 %copy-start.3 = (bf16[32,1,2,8,1280]{4,3,2,1,0:T(8,128)(2,1)S(1)}, bf16[32,1,2,8,1280]{4,3,2,1,0:T(8,128)(2,1)}, u32[]{:S(2)}) copy-start(bf16[32,1,2,8,1280]{4,3,2,1,0:T(8,128)(2,1)} %get-tuple-element.7) | copy-start | bytes 3932164
  316.4 7.2 %copy-start.2 = (bf16[32,1,2,8,1280]{4,3,2,1,0:T(8,128)(2,1)S(1)}, bf16[32,1,2,8,1280]{4,3,2,1,0:T(8,128)(2,1)}, u32[]{:S(2)}) copy-start(bf16[32,1,2,8,1280]{4,3,2,1,0:T(8,128)(2,1)} %get-tuple-element.6) | copy-start | bytes 3932164
  367.6 31.8 %all-to-all-start.1 = ((f32[128,1,3600]{2,1,0:T(1,128)}), f32[128,1,3600]{2,1,0:T(1,128)S(1)}, u32[]{:S(2)}, u32[]{:S(2)}) async-start(f32[128,1,3600]{2,1,0:T(1,128)} %reshape.278), calls=%async_computation.1 | async-start | bytes 3801088 | tf_op jit(solution)/shard_map/all_to_all | solution.py:221
  (4 other events, 10.3 us)

commit v2 on v1

--- a/solution.py
+++ b/solution.py
@@ -85,9 +85,10 @@
             num_scalar_prefetch=1,
             grid=(1,),
             in_specs=[pl.BlockSpec(memory_space=pl.ANY)] * 7,
-            out_specs=pl.BlockSpec(memory_space=pl.ANY),
+            out_specs=pl.BlockSpec((64, ROWS, CH), lambda i, s: (0, 0, 0), pipeline_mode=pl.Buffered(1)),
             scratch_shapes=[pltpu.SemaphoreType.DMA((64,))],
         ),
+        compiler_params=pltpu.CompilerParams(vmem_limit_bytes=16 * 1024 * 1024),
         name="assemble",
     )(slots, *pieces)
 
@@ -170,6 +171,172 @@
     )(first, own, other, pick, order, spread, scale)
 
 
+def pack_kernel(weights_ref, order_ref, out_ref, ordered):
+    lane = lax.broadcasted_iota(jnp.int32, (1, 128), 1)
+    for c in range(2):
+        ordered[...] = jnp.dot(order_ref[...], weights_ref[c], preferred_element_type=jnp.float32)
+        for dest in range(32):
+            tile, off = divmod(dest * 40, 128)
+            total = jnp.zeros((120, 128), jnp.float32)
+            for b in range(3):
+                rows = pl.ds(b * 120, 120)
+                amount = (b * 40 - off) % 128
+                value = ordered[rows, pl.ds(tile * 128, 128)]
+                value = pltpu.roll(value, amount, 1) if amount else value
+                if off + 40 > 128:
+                    nxt = ordered[rows, pl.ds(tile * 128 + 128, 128)]
+                    nxt = pltpu.roll(nxt, amount, 1) if amount else nxt
+                    value = jnp.where(lane < b * 40 + 128 - off, value, nxt)
+                total = jnp.where((lane >= b * 40) & (lane < b * 40 + 40), value, total)
+            out_ref[dest, pl.ds(c * 120, 120), :] = total.astype(jnp.bfloat16)
+
+
+def pack(weights, order):
+    whole = pl.BlockSpec(memory_space=pltpu.VMEM)
+    return pl.pallas_call(
+        pack_kernel,
+        out_shape=jax.ShapeDtypeStruct((32, 240, 128), jnp.bfloat16),
+        in_specs=[whole] * 2,
+        out_specs=whole,
+        scratch_shapes=[pltpu.VMEM((360, CH), jnp.float32)],
+        compiler_params=pltpu.CompilerParams(vmem_limit_bytes=24 * 1024 * 1024),
+        cost_estimate=pl.CostEstimate(flops=1_000_000_000, bytes_accessed=6_000_000, transcendentals=0),
+        name="pack",
+    )(weights, order)
+
+
+def shift_rows(value, amount):
+    if amount == 0:
+        return value
+    pad = jnp.zeros((abs(amount), value.shape[1]), value.dtype)
+    if amount > 0:
+        return jnp.concatenate([value[amount:], pad], axis=0)
+    return jnp.concatenate([pad, value[:amount]], axis=0)
+
+
+def shift_cols(value, amount):
+    if amount == 0:
+        return value
+    moved = pltpu.roll(value, (-amount) % value.shape[0], 0)
+    col = lax.broadcasted_iota(jnp.int32, (value.shape[0], 1), 0) % 8 + amount
+    return jnp.where((col >= 0) & (col < 8), moved, 0.0)
+
+
+def rhs_kernel(scale_ref, pixels_ref, tiles_ref, out_ref, rhs):
+    lane = lax.broadcasted_iota(jnp.int32, (1, 128), 1)
+    tap_row = lax.broadcasted_iota(jnp.int32, (16, 384), 0)
+    tap_lane = lax.broadcasted_iota(jnp.int32, (16, 384), 1)
+    spread = (tap_row == (tap_lane // 128) * 3 + (tap_lane % 128) // 40).astype(jnp.bfloat16)
+    for c in range(2):
+        scale = scale_ref[c]
+        pixels = pixels_ref[...].reshape(32, 2, 16, CH)[:, c].reshape(512, CH)
+        tiles = jnp.concatenate([tiles_ref[c * 3 + a] for a in range(3)], axis=1)
+        taps = jnp.dot(pixels, tiles, preferred_element_type=jnp.float32)
+        by_col = shift_rows(taps[:, :128], -16) + taps[:, 128:256] + shift_rows(taps[:, 256:], 16)
+        out = shift_cols(by_col, -1)
+        out += pltpu.roll(by_col, 88, 1)
+        out += shift_cols(pltpu.roll(by_col, 48, 1), 1)
+        out = jnp.where(lane < 40, out, 0.0).astype(jnp.bfloat16).astype(jnp.float32) * scale
+        moved = shift_cols(out, 1)
+        moved += pltpu.roll(out, 40, 1)
+        moved += pltpu.roll(shift_cols(out, -1), 80, 1)
+        moved = jnp.concatenate([shift_rows(moved, 16), moved, shift_rows(moved, -16)], axis=1)
+        cross = lax.dot_general(
+            pixels, moved.astype(jnp.bfloat16), (((0,), (0,)), ((), ())), preferred_element_type=jnp.float32
+        )
+        top = bottom = total = None
+        for h in range(32):
+            part = jnp.zeros((8, CH), jnp.float32)
+            for slot in range(2):
+                value = pixels[h * 16 + slot * 8 : h * 16 + slot * 8 + 8].astype(jnp.float32)
+                part += value * value
+            total = part if total is None else total + part
+            if h == 0:
+                top = part
+            if h == 31:
+                bottom = part
+        col = lax.broadcasted_iota(jnp.int32, (8, 1), 0)
+        diag = []
+        for kept in (total - bottom, total, total - top):
+            diag.append(jnp.sum(jnp.where(col < 7, kept, 0.0), axis=0, keepdims=True))
+            diag.append(jnp.sum(kept, axis=0, keepdims=True))
+            diag.append(jnp.sum(jnp.where(col > 0, kept, 0.0), axis=0, keepdims=True))
+        diag = jnp.concatenate(diag + [jnp.zeros((7, CH), jnp.float32)], axis=0)
+        diag = diag * (scale * (1.0 - keep_off))
+        wide = None
+        for _ in range(3):
+            head = diag.astype(jnp.bfloat16)
+            part = lax.dot_general(head, spread, (((0,), (0,)), ((), ())), preferred_element_type=jnp.float32)
+            wide = part if wide is None else wide + part
+            diag = diag - head.astype(jnp.float32)
+        value = keep_off * cross + wide * tiles.astype(jnp.float32)
+        rhs[...] = value if c == 0 else rhs[...] + value
+    for dest in range(128):
+        for a in range(3):
+            out_ref[dest, pl.ds(a * OWN, OWN), :] = rhs[pl.ds(dest * OWN, OWN), pl.ds(a * 128, 128)]
+        out_ref[dest, pl.ds(30, 2), :] = jnp.zeros((2, 128), jnp.float32)
+
+
+def rhs_part(scale, pixels, tiles):
+    whole = pl.BlockSpec(memory_space=pltpu.VMEM)
+    return pl.pallas_call(
+        rhs_kernel,
+        out_shape=jax.ShapeDtypeStruct((128, 32, 128), jnp.float32),
+        in_specs=[pl.BlockSpec(memory_space=pltpu.SMEM), pl.BlockSpec((1024, CH), lambda i: (0, 0)), pl.BlockSpec((6, CH, 128), lambda i: (0, 0, 0))],
+        grid=(1,),
+        out_specs=pl.BlockSpec((128, 32, 128), lambda i: (0, 0, 0)),
+        scratch_shapes=[pltpu.VMEM((CH, 384), jnp.float32)],
+        compiler_params=pltpu.CompilerParams(vmem_limit_bytes=48 * 1024 * 1024),
+        cost_estimate=pl.CostEstimate(flops=4_000_000_000, bytes_accessed=8_000_000, transcendentals=0),
+        name="rhs_part",
+    )(scale, pixels, tiles)
+
+
+def finish_kernel(sent_ref, after_ref, out_ref, rows):
+    del after_ref
+    lane = lax.broadcasted_iota(jnp.int32, (1, 128), 1)
+    for tile in range(10):
+        first = tile * 128 // 40
+        last = (tile * 128 + 127) // 40
+        values = [jnp.zeros((32, 128), jnp.float32)] * 3
+        for b in range(first, last + 1):
+            total = sent_ref[b * 4] + sent_ref[b * 4 + 1] + sent_ref[b * 4 + 2] + sent_ref[b * 4 + 3]
+            start = b * 40 - tile * 128
+            keep = (lane >= start) & (lane < start + 40)
+            for t in range(3):
+                amount = (start - t * 40) % 128
+                moved = pltpu.roll(total, amount, 1) if amount else total
+                values[t] = jnp.where(keep, moved, values[t])
+        for t in range(3):
+            rows[pl.ds(t * 32, 32), pl.ds(tile * 128, 128)] = values[t]
+    dst = lax.broadcasted_iota(jnp.int32, (MPAD, 96), 0)
+    src = lax.broadcasted_iota(jnp.int32, (MPAD, 96), 1)
+    inner = src % 32
+    pick = (dst == (inner % OWN) * TAPS + (inner // OWN) * 3 + src // 32) & (inner < 30)
+    pick = pick.astype(jnp.bfloat16)
+    value = rows[...]
+    result = None
+    for _ in range(3):
+        head = value.astype(jnp.bfloat16)
+        part = jnp.dot(pick, head, preferred_element_type=jnp.float32)
+        result = part if result is None else result + part
+        value = value - head.astype(jnp.float32)
+    out_ref[...] = result[:90]
+
+
+def finish(sent, after):
+    whole = pl.BlockSpec(memory_space=pltpu.VMEM)
+    return pl.pallas_call(
+        finish_kernel,
+        out_shape=jax.ShapeDtypeStruct((90, CH), jnp.float32),
+        in_specs=[whole, pl.BlockSpec(memory_space=pl.ANY)],
+        out_specs=whole,
+        scratch_shapes=[pltpu.VMEM((96, CH), jnp.float32)],
+        compiler_params=pltpu.CompilerParams(vmem_limit_bytes=16 * 1024 * 1024),
+        name="finish",
+    )(sent, after)
+
+
 def body(activations, sample_count, client_weights):
     client_here = lax.axis_index("client")
     blk_here = lax.axis_index("blk")
@@ -182,9 +349,12 @@
     mine = lax.dynamic_slice_in_dim(sample_count, client_here * 2, 2)
     my_scale = lax.dynamic_slice_in_dim(all_scale, client_here * 2, 2)
 
-    packed = client_weights.reshape(2, 40, TAPS, 32, 40).transpose(3, 1, 0, 2, 4).reshape(32, 40, 720)
+    row = lax.broadcasted_iota(jnp.int32, (360, 360), 0)
+    col = lax.broadcasted_iota(jnp.int32, (360, 360), 1)
+    tap_order = (col == (row % 40) * TAPS + (row // 40) % 3 * 3 + row // 120).astype(jnp.bfloat16)
+    packed = pack(client_weights, tap_order)
     tiles = lax.all_to_all(packed, "blk", split_axis=0, concat_axis=0, tiled=True)
-    tiles = tiles.reshape(CH, 2, 3, 3, 40)
+    tiles = tiles.reshape(32, 6, 40, 128).transpose(1, 0, 2, 3).reshape(6, CH, 128)
 
     live = lax.broadcasted_iota(jnp.int32, (2, 2), 1) < mine[:, None]
     masked = jnp.where(live[:, :, None, None, None], activations, jnp.zeros_like(activations))
@@ -196,32 +366,9 @@
     own = assemble(slots, pieces)
     other = lax.ppermute(own, AXES, [(d, d ^ 32) for d in range(128)])
 
-    pixels = own[:32].reshape(32, 2, 2, 8, CH)
-    outs = []
-    for c in range(2):
-        out = lax.conv_general_dilated(
-            pixels[:, c], tiles[:, c], (1, 1), ((1, 1), (1, 1)),
-            dimension_numbers=("HNWC", "IHWO", "HNWC"), preferred_element_type=jnp.float32,
-        ).astype(jnp.bfloat16)
-        outs.append(out * my_scale[c].astype(jnp.bfloat16))
-    outs = jnp.stack(outs, axis=1).reshape(32, 4, 8, 40)
-    cross = lax.conv_general_dilated(
-        pixels.reshape(32, 4, 8, CH), outs, (1, 1), ((1, 1), (1, 1)),
-        dimension_numbers=("HCWN", "HIWO", "NHWC"), preferred_element_type=jnp.float32,
-    )
-    square = jnp.square(pixels.astype(jnp.float32))
-    by_col = jnp.sum(square, axis=(0, 2))
-    top, bottom = jnp.sum(square[0], axis=1), jnp.sum(square[31], axis=1)
-    by_row = jnp.stack([by_col - bottom, by_col, by_col - top], axis=1)
-    full = jnp.sum(by_row, axis=2)
-    diag = jnp.stack([full - by_row[:, :, 7], full, full - by_row[:, :, 0]], axis=2)
-    weight = ((1.0 - keep_off) * my_scale)[:, None, None, None] * diag
-    weight = weight.transpose(3, 0, 1, 2)
-    rhs = keep_off * cross + jnp.sum(weight[..., None] * tiles.astype(jnp.float32), axis=1)
-    sent = lax.all_to_all(
-        rhs.reshape(128, OWN, TAPS, 40), ("blk", "client"), split_axis=0, concat_axis=0, tiled=True
-    )
-    rhs_out = jnp.sum(sent.reshape(32, 4, OWN, TAPS, 40), axis=1).transpose(1, 2, 0, 3).reshape(90, CH)
+    own_rows = own.reshape(2048, CH)
+    part = rhs_part(my_scale, own_rows, tiles)
+    sent = lax.all_to_all(part, ("blk", "client"), split_axis=0, concat_axis=0, tiled=True)
 
     first_channel = blk_here * 40 + client_here * OWN
     chan = lax.broadcasted_iota(jnp.int32, (16, CH), 1) - first_channel
@@ -237,10 +384,10 @@
     group_scale = all_scale.reshape(4, 2)[groups]
     img_scale = jnp.repeat(jnp.repeat(group_scale, 16, axis=1)[:, None, :], 32, axis=1).reshape(4, LANES)
     gram_out = gram(
-        jnp.reshape(first_channel * TAPS, (1,)), own.reshape(2048, CH), other.reshape(2048, CH),
+        jnp.reshape(first_channel * TAPS, (1,)), own_rows, other.reshape(2048, CH),
         pick, order, spread, img_scale,
     )
-    return gram_out, rhs_out
+    return gram_out, finish(sent, gram_out)
 
 
 def solution(mesh):

time: 455 us -> 174 us (0.38)
  Pallas kernels: 192 us -> 54.2 us
  local copies, waits for them, and re-layouts: 99.2 us -> 11.1 us
  matrix products: 20.1 us -> 0 us
  other arithmetic: 24.6 us -> 6.77 us
  starting transfers between devices: 52.7 us -> 40.8 us
    pallas_call x1, Pallas kernels: 161 us -> 9.47 us  [assemble(): pl.pallas_call(assemble_kernel, out_shape=jax.ShapeDtypeStruct((64, ROWS,...]
    reshape x7 -> x1, local copies, waits for them, and re-layouts: 54.9 us -> 0.34 us  [body(): tiles.reshape(32, 6, 40, 128).transpose(1, 0, 2, 3).reshape(6, CH, 128)]
    all_to_all x1, waiting for transfers between devices: 0.01 us -> 22.1 us  [body(): lax.all_to_all(packed, 'blk', split_axis=0, concat_axis=0, tiled=True)]
    all_to_all x1, waiting for transfers between devices: 21.8 us -> 0.01 us  [body(): lax.all_to_all(part, ('blk', 'client'), split_axis=0, concat_axis=0, tile...]
    conv_general_dilated x3 -> x0, matrix products: 20.1 us -> none  [the longest x2 14.3 us: body(): lax.conv_general_dilated(pixels[:, c], tiles[:, c], (1, 1), ((1, 1), (1,...]
    ppermute x1, starting transfers between devices: 21.1 us -> 2.69 us  [body(): other = lax.ppermute(own, AXES, [(d, d ^ 32) for d in range(128)])]
    pallas_call x0 -> x3, Pallas kernels: none -> 13.8 us  [the longest x1 8.66 us: rhs_part(): pl.pallas_call(rhs_kernel, out_shape=jax.ShapeDtypeStruct((128, 32, 128),...]
    unnamed x33 -> x19, local copies, waits for them, and re-layouts: 20.2 us -> 6.93 us
  transfers between devices with their start and end apart: 15 -> 15, of which waited for: 7 -> 9; matrix products, arithmetic and copies ran while one was open for 31% -> 7% of each run, Pallas kernels for 36% -> 25%
where the time goes in v2:
time: 174 us; the launch traced here: 173 us
  waiting for transfers between devices  59.5 us (34%)
  Pallas kernels  54.2 us (31%)
  starting transfers between devices  40.8 us (23%)
  local copies, waits for them, and re-layouts  11.1 us (6%)
  other arithmetic  6.77 us (4%)
    ppermute x12, waiting for transfers between devices, take_from(): return lax.ppermute(value, AXES, pairs)  37.4 us
    pallas_call x1, Pallas kernels, gram(): pl.pallas_call(gram_kernel, out_shape=jax.ShapeDtypeStruct((90, 11520), j...  30.9 us
    ppermute x12, starting transfers between devices, take_from(): return lax.ppermute(value, AXES, pairs)  28 us
    all_to_all x1, waiting for transfers between devices, body(): lax.all_to_all(packed, 'blk', split_axis=0, concat_axis=0, tiled=True)  22.1 us
    pallas_call x1, Pallas kernels, assemble(): pl.pallas_call(assemble_kernel, out_shape=jax.ShapeDtypeStruct((64, ROWS,...  9.47 us
    pallas_call x1, Pallas kernels, rhs_part(): pl.pallas_call(rhs_kernel, out_shape=jax.ShapeDtypeStruct((128, 32, 128),...  8.66 us
    unnamed x19, local copies, waits for them, and re-layouts  6.93 us
    all_to_all x1, starting transfers between devices, body(): lax.all_to_all(part, ('blk', 'client'), split_axis=0, concat_axis=0, tile...  5.75 us
  transfers between devices with their start and end apart: 15, of which 9 were waited for; matrix products, arithmetic and copies ran while one was open for 7% of the time, Pallas kernels for 25%

profile of v2, /device:TPU:1, one launch (start us, length us, event | category | flops | bytes accessed | tf_op | source)
XLA Modules:
  0.0 173.2 jit_solution(16020527088147532672)
XLA Ops:
  2.4 6.8 %collective-permute-start = (bf16[32,1280]{1,0:T(8,128)(2,1)S(1)}, bf16[32,1280]{1,0:T(8,128)(2,1)S(1)}, u32[]{:S(2)}, u32[]{:S(2)}) collective-permute-start(bf16[32,1280]{1,0:T(8,128)(2,1)S(1)} %bitcast.16), channel_id=1, source_target_pairs={{12,0},{13,1},{14,2},{15,3},{72,4},{73,5},{74,6},{75,7},{20,8},{21... | collective-permute-start | bytes 245768 | tf_op jit(solution)/shard_map/ppermute | solution.py:38
  11.6 5.5 %collective-permute-done.1 = bf16[32,1280]{1,0:T(8,128)(2,1)S(1)} collective-permute-done((bf16[32,1280]{1,0:T(8,128)(2,1)S(1)}, bf16[32,1280]{1,0:T(8,128)(2,1)S(1)}, u32[]{:S(2)}, u32[]{:S(2)}) %collective-permute-start.1) | collective-permute-done | bytes 81952 | tf_op jit(solution)/shard_map/ppermute | solution.py:38
  17.1 1.8 %collective-permute-start.3 = (bf16[128,1280]{1,0:T(8,128)(2,1)S(1)}, bf16[128,1280]{1,0:T(8,128)(2,1)S(1)}, u32[]{:S(2)}, u32[]{:S(2)}) collective-permute-start(bf16[128,1280]{1,0:T(8,128)(2,1)S(1)} %pad_maximum_fusion), channel_id=1, source_target_pairs={{29,0},{30,1},{31,2},{28,3},{89,4},{90,5},{91,6},{88,7},{5,8},{6,9... | collective-permute-start | bytes 983048 | tf_op jit(solution)/shard_map/ppermute | solution.py:38
  18.9 1.3 collective-permute-start.4
  20.2 3.8 %collective-permute-start.5 = (bf16[128,1280]{1,0:T(8,128)(2,1)S(1)}, bf16[128,1280]{1,0:T(8,128)(2,1)S(1)}, u32[]{:S(2)}, u32[]{:S(2)}) collective-permute-start(bf16[128,1280]{1,0:T(8,128)(2,1)S(1)} %pad_maximum_fusion), channel_id=1, source_target_pairs={{79,0},{76,1},{77,2},{78,3},{11,4},{8,5},{9,6},{10,7},{87,8},{84,9... | collective-permute-start | bytes 983048 | tf_op jit(solution)/shard_map/ppermute | solution.py:38
  28.6 2.3 %collective-permute-done.5 = bf16[128,1280]{1,0:T(8,128)(2,1)S(1)} collective-permute-done((bf16[128,1280]{1,0:T(8,128)(2,1)S(1)}, bf16[128,1280]{1,0:T(8,128)(2,1)S(1)}, u32[]{:S(2)}, u32[]{:S(2)}) %collective-permute-start.5) | collective-permute-done | bytes 327712 | tf_op jit(solution)/shard_map/ppermute | solution.py:38
  31.7 7.3 %collective-permute-start.7 = (bf16[256,1280]{1,0:T(8,128)(2,1)}, bf16[256,1280]{1,0:T(8,128)(2,1)S(1)}, u32[]{:S(2)}, u32[]{:S(2)}) collective-permute-start(bf16[256,1280]{1,0:T(8,128)(2,1)} %get-tuple-element.2), channel_id=1, source_target_pairs={{24,0},{25,1},{26,2},{27,3},{28,4},{29,5},{30,6},{31,7},{0,8},{1,9... | collective-permute-start | bytes 1966088 | tf_op jit(solution)/shard_map/ppermute | solution.py:38
  39.0 3.6 %collective-permute-start.9 = (bf16[256,1280]{1,0:T(8,128)(2,1)}, bf16[256,1280]{1,0:T(8,128)(2,1)S(1)}, u32[]{:S(2)}, u32[]{:S(2)}) collective-permute-start(bf16[256,1280]{1,0:T(8,128)(2,1)} %get-tuple-element.2), channel_id=1, source_target_pairs={{8,0},{9,1},{10,2},{11,3},{12,4},{13,5},{14,6},{15,7},{16,8},{17,9... | collective-permute-start | bytes 1966088 | tf_op jit(solution)/shard_map/ppermute | solution.py:38
  42.6 1.4 collective-permute-start.11
  44.5 12.2 %collective-permute-done.7.refs_2_ = bf16[256,1280]{1,0:T(8,128)(2,1)S(1)} collective-permute-done((bf16[256,1280]{1,0:T(8,128)(2,1)}, bf16[256,1280]{1,0:T(8,128)(2,1)S(1)}, u32[]{:S(2)}, u32[]{:S(2)}) %collective-permute-start.7) | collective-permute-done | bytes 655392 | tf_op jit(solution)/shard_map/ppermute | solution.py:38
  57.6 1.4 collective-permute-done.11.refs_6_
  59.0 13.8 %collective-permute-done.8.refs_3_ = bf16[256,1280]{1,0:T(8,128)(2,1)} collective-permute-done((bf16[256,1280]{1,0:T(8,128)(2,1)}, bf16[256,1280]{1,0:T(8,128)(2,1)}, u32[]{:S(2)}, u32[]{:S(2)}) %collective-permute-start.8) | collective-permute-done | bytes 655392 | tf_op jit(solution)/shard_map/ppermute | solution.py:38
  72.8 9.5 %assemble.1 = bf16[64,32,1280]{2,1,0:T(8,128)(2,1)} custom-call(s32[64]{0:T(128)S(1)} %fusion.29.slots, bf16[512,1280]{1,0:T(8,128)(2,1)S(1)} %get-tuple-element.3.refs_0_, bf16[256,1280]{1,0:T(8,128)(2,1)} %collective-permute-done.6.refs_1_, bf16[256,1280]{1,0:T(8,128)(2,1)S(1)} %collective-permute-done.7.refs_2_, ...), custom_call_target="tpu_custom_call" | custom-call | tf_op jit(solution)/shard_map/assemble/pallas_call | solution.py:81
  82.3 2.7 %collective-permute-start.12 = (bf16[64,32,1280]{2,1,0:T(8,128)(2,1)}, bf16[64,32,1280]{2,1,0:T(8,128)(2,1)}, u32[]{:S(2)}, u32[]{:S(2)}) collective-permute-start(bf16[64,32,1280]{2,1,0:T(8,128)(2,1)} %assemble.1), channel_id=1, source_target_pairs={{0,32},{1,33},{2,34},{3,35},{4,36},{5,37},{6,38},{7,39},{8,40},{9,... | collective-permute-start | bytes 15728648 | tf_op jit(solution)/shard_map/ppermute | solution.py:367
  85.8 3.6 %pack.1 = bf16[32,240,128]{2,1,0:T(8,128)(2,1)} custom-call(bf16[2,360,1280]{2,1,0:T(8,128)(2,1)S(1)} %copy-done.2, bf16[360,360]{1,0:T(8,128)(2,1)S(1)} %fusion.7.order_ref), custom_call_target="tpu_custom_call" | custom-call | flops 1000000000 | bytes 6000000 | tf_op jit(solution)/shard_map/pack/pallas_call | solution.py:196
  89.4 4.3 %all-to-all-start = ((bf16[32,240,128]{2,1,0:T(8,128)(2,1)}), bf16[32,240,128]{2,1,0:T(8,128)(2,1)S(1)}, u32[]{:S(2)}, u32[]{:S(2)}) async-start(bf16[32,240,128]{2,1,0:T(8,128)(2,1)} %pack.1), calls=%async_computation | async-start | bytes 3932160 | tf_op jit(solution)/shard_map/all_to_all | solution.py:356
  96.2 3.3 %fusion.spread_ref = bf16[1152,1152]{1,0:T(8,128)(2,1)} fusion(s32[1152]{0:T(1024)S(1)} %get-tuple-element.28, s32[1152]{0:T(1024)S(1)} %get-tuple-element.31, s32[1152]{0:T(1024)S(1)} %get-tuple-element.29, s32[1152]{0:T(1024)S(1)} %get-tuple-element.30, pred[1152]{0:T(1024)(128)(4,1)S(1)} %get-tuple-element.32, pred[1152]{0:T(1024)(128)(4,1)S(1)} %get-tuple-element.33), kind=kLoop, calls=%fused_computation.2 | loop fusion | flops 7962624 | bytes 2674944 | tf_op jit(solution)/shard_map/convert_element_type | solution.py:382
  99.5 22.1 %all-to-all-done = bf16[32,240,128]{2,1,0:T(8,128)(2,1)S(1)} async-done(((bf16[32,240,128]{2,1,0:T(8,128)(2,1)}), bf16[32,240,128]{2,1,0:T(8,128)(2,1)S(1)}, u32[]{:S(2)}, u32[]{:S(2)}) %all-to-all-start) | async-done | bytes 1966112 | tf_op jit(solution)/shard_map/all_to_all | solution.py:356
  121.9 8.7 %rhs_part.1 = f32[128,32,128]{2,1,0:T(8,128)S(1)} custom-call(f32[2]{0:T(128)S(1)} %dynamic_slice.7.scale_ref, bf16[2048,1280]{1,0:T(8,128)(2,1)} %bitcast.2.own_ref.pixels_ref, bf16[6,1280,128]{2,1,0:T(8,128)(2,1)S(1)} %bitcast.14), custom_call_target="tpu_custom_call" | custom-call | flops 4000000000 | bytes 8000000 | tf_op jit(solution)/shard_map/rhs_part/pallas_call | solution.py:282
  130.6 1.3 copy-done.1
  131.9 5.8 %all-to-all-start.1 = ((f32[128,32,128]{2,1,0:T(8,128)}), f32[128,32,128]{2,1,0:T(8,128)S(1)}, u32[]{:S(2)}, u32[]{:S(2)}) async-start(f32[128,32,128]{2,1,0:T(8,128)} %copy-done.1), calls=%async_computation.1 | async-start | bytes 4194304 | tf_op jit(solution)/shard_map/all_to_all | solution.py:371
  138.4 30.9 %gram.1.after_ref = f32[90,11520]{1,0:T(8,128)} custom-call(s32[1]{0:T(128)} %bitcast.first_ref, bf16[2048,1280]{1,0:T(8,128)(2,1)} %bitcast.2.own_ref.pixels_ref, bf16[2048,1280]{1,0:T(8,128)(2,1)} %bitcast.3.other_ref, bf16[16,1280]{1,0:T(8,128)(2,1)} %fusion.12.pick_ref, bf16[96,144]{1,0:T(8,128)(2,1)} %fusion.10.order_ref, ...), custom_call_target="tpu_custom_call" | custom-call | flops 20000000000 | bytes 20000000 | tf_op jit(solution)/shard_map/gram/pallas_call | solution.py:158
  169.3 2.3 %copy-done = f32[90,11520]{1,0:T(8,128)S(1)} copy-done((f32[90,11520]{1,0:T(8,128)S(1)}, f32[90,11520]{1,0:T(8,128)}, u32[]{:S(2)}) %copy-start) | copy-done | bytes 4147224
  171.6 1.6 finish.1
  (68 shorter events, 15.3 us)
Async XLA Ops:
  2.4 9.2 %collective-permute-start = (bf16[32,1280]{1,0:T(8,128)(2,1)S(1)}, bf16[32,1280]{1,0:T(8,128)(2,1)S(1)}, u32[]{:S(2)}, u32[]{:S(2)}) collective-permute-start(bf16[32,1280]{1,0:T(8,128)(2,1)S(1)} %bitcast.16), channel_id=1, source_target_pairs={{12,0},{13,1},{14,2},{15,3},{72,4},{73,5},{74,6},{75,7},{20,8},{21... | collective-permute-start | bytes 245768 | tf_op jit(solution)/shard_map/ppermute | solution.py:38
  9.3 7.9 %collective-permute-start.1 = (bf16[32,1280]{1,0:T(8,128)(2,1)S(1)}, bf16[32,1280]{1,0:T(8,128)(2,1)S(1)}, u32[]{:S(2)}, u32[]{:S(2)}) collective-permute-start(bf16[32,1280]{1,0:T(8,128)(2,1)S(1)} %bitcast.17), channel_id=1, source_target_pairs={{80,0},{81,1},{82,2},{83,3},{84,4},{85,5},{86,6},{87,7},{88,8},{89... | collective-permute-start | bytes 245768 | tf_op jit(solution)/shard_map/ppermute | solution.py:38
  9.5 7.7 %collective-permute-start.2 = (bf16[32,1280]{1,0:T(8,128)(2,1)S(1)}, bf16[32,1280]{1,0:T(8,128)(2,1)S(1)}, u32[]{:S(2)}, u32[]{:S(2)}) collective-permute-start(bf16[32,1280]{1,0:T(8,128)(2,1)S(1)} %bitcast.18), channel_id=1, source_target_pairs={{92,0},{93,1},{94,2},{95,3},{24,4},{25,5},{26,6},{27,7},{68,8},{69... | collective-permute-start | bytes 245768 | tf_op jit(solution)/shard_map/ppermute | solution.py:38
  17.1 9.9 %collective-permute-start.3 = (bf16[128,1280]{1,0:T(8,128)(2,1)S(1)}, bf16[128,1280]{1,0:T(8,128)(2,1)S(1)}, u32[]{:S(2)}, u32[]{:S(2)}) collective-permute-start(bf16[128,1280]{1,0:T(8,128)(2,1)S(1)} %pad_maximum_fusion), channel_id=1, source_target_pairs={{29,0},{30,1},{31,2},{28,3},{89,4},{90,5},{91,6},{88,7},{5,8},{6,9... | collective-permute-start | bytes 983048 | tf_op jit(solution)/shard_map/ppermute | solution.py:38
  18.9 8.9 %collective-permute-start.4 = (bf16[128,1280]{1,0:T(8,128)(2,1)S(1)}, bf16[128,1280]{1,0:T(8,128)(2,1)S(1)}, u32[]{:S(2)}, u32[]{:S(2)}) collective-permute-start(bf16[128,1280]{1,0:T(8,128)(2,1)S(1)} %pad_maximum_fusion), channel_id=1, source_target_pairs={{2,0},{3,1},{0,2},{1,3},{6,4},{7,5},{4,6},{5,7},{10,8},{11,9},{8,1... | collective-permute-start | bytes 983048 | tf_op jit(solution)/shard_map/ppermute | solution.py:38
  20.2 10.7 %collective-permute-start.5 = (bf16[128,1280]{1,0:T(8,128)(2,1)S(1)}, bf16[128,1280]{1,0:T(8,128)(2,1)S(1)}, u32[]{:S(2)}, u32[]{:S(2)}) collective-permute-start(bf16[128,1280]{1,0:T(8,128)(2,1)S(1)} %pad_maximum_fusion), channel_id=1, source_target_pairs={{79,0},{76,1},{77,2},{78,3},{11,4},{8,5},{9,6},{10,7},{87,8},{84,9... | collective-permute-start | bytes 983048 | tf_op jit(solution)/shard_map/ppermute | solution.py:38
  27.0 29.9 %copy-start.3 = (s32[64]{0:T(128)S(1)}, s32[64]{0:T(128)}, u32[]{:S(2)}) copy-start(s32[64]{0:T(128)} %constant.219.clone) | copy-start | bytes 772
  27.0 29.9 %copy-start.4 = (s32[64]{0:T(128)S(1)}, s32[64]{0:T(128)}, u32[]{:S(2)}) copy-start(s32[64]{0:T(128)} %constant.220.clone) | copy-start | bytes 772
  27.0 29.9 %copy-start.5 = (s32[64]{0:T(128)S(1)}, s32[64]{0:T(128)}, u32[]{:S(2)}) copy-start(s32[64]{0:T(128)} %constant.221.clone) | copy-start | bytes 772
  31.7 25.0 %collective-permute-start.7 = (bf16[256,1280]{1,0:T(8,128)(2,1)}, bf16[256,1280]{1,0:T(8,128)(2,1)S(1)}, u32[]{:S(2)}, u32[]{:S(2)}) collective-permute-start(bf16[256,1280]{1,0:T(8,128)(2,1)} %get-tuple-element.2), channel_id=1, source_target_pairs={{24,0},{25,1},{26,2},{27,3},{28,4},{29,5},{30,6},{31,7},{0,8},{1,9... | collective-permute-start | bytes 1966088 | tf_op jit(solution)/shard_map/ppermute | solution.py:38
  39.0 18.0 %collective-permute-start.9 = (bf16[256,1280]{1,0:T(8,128)(2,1)}, bf16[256,1280]{1,0:T(8,128)(2,1)S(1)}, u32[]{:S(2)}, u32[]{:S(2)}) collective-permute-start(bf16[256,1280]{1,0:T(8,128)(2,1)} %get-tuple-element.2), channel_id=1, source_target_pairs={{8,0},{9,1},{10,2},{11,3},{12,4},{13,5},{14,6},{15,7},{16,8},{17,9... | collective-permute-start | bytes 1966088 | tf_op jit(solution)/shard_map/ppermute | solution.py:38
  42.5 15.1 %collective-permute-start.10 = (bf16[256,1280]{1,0:T(8,128)(2,1)}, bf16[256,1280]{1,0:T(8,128)(2,1)S(1)}, u32[]{:S(2)}, u32[]{:S(2)}) collective-permute-start(bf16[256,1280]{1,0:T(8,128)(2,1)} %get-tuple-element.6), channel_id=1, source_target_pairs={{1,0},{2,1},{3,2},{0,3},{5,4},{6,5},{7,6},{4,7},{9,8},{10,9},{11,1... | collective-permute-start | bytes 1966088 | tf_op jit(solution)/shard_map/ppermute | solution.py:38
  42.6 16.4 %collective-permute-start.11 = (bf16[256,1280]{1,0:T(8,128)(2,1)}, bf16[256,1280]{1,0:T(8,128)(2,1)}, u32[]{:S(2)}, u32[]{:S(2)}) collective-permute-start(bf16[256,1280]{1,0:T(8,128)(2,1)} %get-tuple-element.6), channel_id=1, source_target_pairs={{3,0},{0,1},{1,2},{2,3},{7,4},{4,5},{5,6},{6,7},{11,8},{8,9},{9,10... | collective-permute-start | bytes 1966088 | tf_op jit(solution)/shard_map/ppermute | solution.py:38
  44.0 15.0 %collective-permute-start.6 = (bf16[256,1280]{1,0:T(8,128)(2,1)}, bf16[256,1280]{1,0:T(8,128)(2,1)}, u32[]{:S(2)}, u32[]{:S(2)}) collective-permute-start(bf16[256,1280]{1,0:T(8,128)(2,1)} %get-tuple-element.6), channel_id=1, source_target_pairs={{4,0},{5,1},{6,2},{7,3},{64,4},{65,5},{66,6},{67,7},{12,8},{13,9},... | collective-permute-start | bytes 1966088 | tf_op jit(solution)/shard_map/ppermute | solution.py:38
  56.7 16.1 %collective-permute-start.8 = (bf16[256,1280]{1,0:T(8,128)(2,1)}, bf16[256,1280]{1,0:T(8,128)(2,1)}, u32[]{:S(2)}, u32[]{:S(2)}) collective-permute-start(bf16[256,1280]{1,0:T(8,128)(2,1)} %get-tuple-element.6), channel_id=1, source_target_pairs={{68,0},{69,1},{70,2},{71,3},{0,4},{1,5},{2,6},{3,7},{76,8},{77,9},... | collective-permute-start | bytes 1966088 | tf_op jit(solution)/shard_map/ppermute | solution.py:38
  72.8 13.0 %copy-start.2 = (bf16[2,360,1280]{2,1,0:T(8,128)(2,1)S(1)}, bf16[2,360,1280]{2,1,0:T(8,128)(2,1)}, u32[]{:S(2)}) copy-start(bf16[2,360,1280]{2,1,0:T(8,128)(2,1)} %weights_ref.1) | copy-start | bytes 5529604
  82.3 56.1 %collective-permute-start.12 = (bf16[64,32,1280]{2,1,0:T(8,128)(2,1)}, bf16[64,32,1280]{2,1,0:T(8,128)(2,1)}, u32[]{:S(2)}, u32[]{:S(2)}) collective-permute-start(bf16[64,32,1280]{2,1,0:T(8,128)(2,1)} %assemble.1), channel_id=1, source_target_pairs={{0,32},{1,33},{2,34},{3,35},{4,36},{5,37},{6,38},{7,39},{8,40},{9,... | collective-permute-start | bytes 15728648 | tf_op jit(solution)/shard_map/ppermute | solution.py:367
  89.4 4.3 %copy-start.6 = (s32[8]{0:T(128)S(1)}, s32[8]{0:T(128)}, u32[]{:S(2)}) copy-start(s32[8]{0:T(128)} %param.7) | copy-start | bytes 100
  89.4 32.2 %all-to-all-start = ((bf16[32,240,128]{2,1,0:T(8,128)(2,1)}), bf16[32,240,128]{2,1,0:T(8,128)(2,1)S(1)}, u32[]{:S(2)}, u32[]{:S(2)}) async-start(bf16[32,240,128]{2,1,0:T(8,128)(2,1)} %pack.1), calls=%async_computation | async-start | bytes 3932160 | tf_op jit(solution)/shard_map/all_to_all | solution.py:356
  130.6 1.3 copy-start.1
  131.9 37.4 %all-to-all-start.1 = ((f32[128,32,128]{2,1,0:T(8,128)}), f32[128,32,128]{2,1,0:T(8,128)S(1)}, u32[]{:S(2)}, u32[]{:S(2)}) async-start(f32[128,32,128]{2,1,0:T(8,128)} %copy-done.1), calls=%async_computation.1 | async-start | bytes 4194304 | tf_op jit(solution)/shard_map/all_to_all | solution.py:371
  169.3 2.3 %copy-start = (f32[90,11520]{1,0:T(8,128)S(1)}, f32[90,11520]{1,0:T(8,128)}, u32[]{:S(2)}) copy-start(f32[90,11520]{1,0:T(8,128)} %gram.1.after_ref) | copy-start | bytes 12441604

commit v3 on v2

--- a/solution.py
+++ b/solution.py
@@ -45,49 +45,39 @@
 STEP = (1, 0, 1)
 FIRST = [tuple(k * s % 4 for s in STEP) for k in range(4)]
 SECOND = [(0, 0, 0), (1, 1, 3), (0, 2, 0), (3, 3, 1)]
-HEAD = [vec_add(g, f) for g in SECOND[:2] for f in FIRST]
-TAIL = [vec_add(g, f) for g in SECOND[2:] for f in FIRST]
-LAST = [((1, 0, 0), 0), ((0, 0, 3), 1), ((3, 0, 0), 0), ((0, 0, 1), 1), ((0, 1, 0), 0), ((0, 3, 0), 0)]
-SOURCES = list(HEAD) + list(TAIL)
-for away, part in LAST:
-    SOURCES += [vec_add(away, o) for o in (TAIL if part else HEAD)]
-assert len(set(SOURCES)) == 64
-
-
-def gather_chips(block):
+LEVEL = [vec_add(g, f) for g in SECOND for f in FIRST]
+LAST = [((1, 0, 0), 0, 8), ((0, 0, 3), 8, 16), ((3, 0, 0), 0, 8), ((0, 0, 1), 8, 16), ((0, 1, 0), 0, 12), ((0, 3, 0), 4, 8)]
+SOURCES = list(LEVEL)
+for away, low, high in LAST:
+    SOURCES += [vec_add(away, o) for o in LEVEL[low:high]]
+assert len(SOURCES) == 64 and len(set(SOURCES)) == 64
+
+
+def gather_chips(block, tiles):
     level = jnp.concatenate([block] + [take_from(block, o) for o in FIRST[1:]], axis=0)
     level = jnp.concatenate([level] + [take_from(level, o) for o in SECOND[1:]], axis=0)
-    halves = (level[:256], level[256:])
-    return [level] + [take_from(halves[part], away) for away, part in LAST]
+    level, tiles = lax.optimization_barrier((level, tiles))
+    parts = [level[low * ROWS : high * ROWS] for _, low, high in LAST]
+    small = take_from(parts[5], LAST[5][0])
+    parts[2], small = lax.optimization_barrier((parts[2], small))
+    return [level] + [take_from(part, last[0]) for part, last in zip(parts[:5], LAST)] + [small], tiles
 
 
 def assemble_kernel(slots, *refs):
-    sources, out, sems = refs[:7], refs[7], refs[8]
-    copies = []
-    for t in range(64):
-        if t < 16:
-            src = sources[0].at[pl.ds(t * ROWS, ROWS)]
-        else:
-            piece, row = divmod(t - 16, 8)
-            src = sources[1 + piece].at[pl.ds(row * ROWS, ROWS)]
-        copies.append(pltpu.make_async_copy(src, out.at[slots[t]], sems.at[t]))
-    for copy in copies:
-        copy.start()
-    for copy in copies:
-        copy.wait()
+    out = refs[-1]
+    spot = 0
+    for ref in refs[:-1]:
+        for row in range(ref.shape[0] // ROWS):
+            out[slots[spot]] = ref[pl.ds(row * ROWS, ROWS), :]
+            spot += 1
 
 
 def assemble(slots, pieces):
     return pl.pallas_call(
         assemble_kernel,
         out_shape=jax.ShapeDtypeStruct((64, ROWS, CH), jnp.bfloat16),
-        grid_spec=pltpu.PrefetchScalarGridSpec(
-            num_scalar_prefetch=1,
-            grid=(1,),
-            in_specs=[pl.BlockSpec(memory_space=pl.ANY)] * 7,
-            out_specs=pl.BlockSpec((64, ROWS, CH), lambda i, s: (0, 0, 0), pipeline_mode=pl.Buffered(1)),
-            scratch_shapes=[pltpu.SemaphoreType.DMA((64,))],
-        ),
+        in_specs=[pl.BlockSpec(memory_space=pltpu.SMEM)] + [pl.BlockSpec(memory_space=pltpu.VMEM)] * 7,
+        out_specs=pl.BlockSpec(memory_space=pltpu.VMEM),
         compiler_params=pltpu.CompilerParams(vmem_limit_bytes=16 * 1024 * 1024),
         name="assemble",
     )(slots, *pieces)
@@ -103,7 +93,7 @@
     return jnp.where(inside, moved, 0.0)
 
 
-def gram_kernel(first_ref, own_ref, other_ref, pick_ref, order_ref, spread_ref, scale_ref, out_ref, left, acc, high):
+def gram_kernel(first_ref, own_ref, other_ref, pick_ref, order_ref, scale_ref, out_ref, left, acc, staged, sems):
     pick = pick_ref[...]
     order = order_ref[...]
     for group in range(4):
@@ -126,49 +116,56 @@
         total += jnp.dot(left[:, pl.ds(2048, 2048)], other_ref[:, lanes], preferred_element_type=jnp.float32)
         acc[:, lanes] = total
 
+    first = first_ref[0]
+    lane = lax.broadcasted_iota(jnp.int32, (MPAD, 128), 1)
+    row = lax.broadcasted_iota(jnp.int32, (MPAD, 128), 0)
+
+    def weave(values, part):
+        spot = lane + 128 * part
+        index = spot // 3
+        result = None
+        for k in range(3):
+            moved = jnp.take_along_axis(values[k], index, axis=1)
+            result = moved if result is None else jnp.where(spot % 3 == k, moved, result)
+        return result
+
+    @pl.loop(0, 10)
+    def _(block):
+        lanes = pl.ds(pl.multiple_of(block * 128, 128), 128)
+        inner = [
+            [weave([acc[pl.ds((3 * a + b) * MPAD, MPAD), lanes] for a in range(3)], part) for part in range(3)]
+            for b in range(3)
+        ]
+        for tile in range(9):
+            value = weave([inner[b][tile // 3] for b in range(3)], tile % 3)
+            base = block * 1152 + tile * 128
+            value = jnp.where(row + first == lane + base, value, keep_off * value)
+            staged[:, pl.ds(pl.multiple_of(base, 128), 128)] = value[:90]
+        wide = pl.ds(pl.multiple_of(block * 1152, 128), 1152)
+        pltpu.make_async_copy(staged.at[:, wide], out_ref.at[:, wide], sems.at[block]).start()
+
     for block in range(10):
-        for t in range(TAPS):
-            part = acc[pl.ds(t * MPAD, MPAD), pl.ds(block * 128, 128)]
-            top = part.astype(jnp.bfloat16)
-            high[pl.ds(block * 2 * MPAD, MPAD), pl.ds(t * 128, 128)] = top
-            high[pl.ds((block * 2 + 1) * MPAD, MPAD), pl.ds(t * 128, 128)] = (
-                part - top.astype(jnp.float32)
-            ).astype(jnp.bfloat16)
-
-    first = first_ref[0]
-
-    @pl.loop(0, 6)
-    def _(step):
-        half = step // 3
-        piece = step % 3
-        rows = pl.ds(pl.multiple_of(half * 960, 960), 960)
-        cols = pl.ds(pl.multiple_of(piece * 384, 128), 384)
-        wide = jnp.dot(high[rows, :], spread_ref[:, cols], preferred_element_type=jnp.float32)
-        for b in range(5):
-            value = wide[b * 192 : b * 192 + 96] + wide[b * 192 + 96 : b * 192 + 192]
-            value = value[:90]
-            base = half * 5760 + b * 1152 + piece * 384
-            row = lax.broadcasted_iota(jnp.int32, value.shape, 0) + first
-            col = lax.broadcasted_iota(jnp.int32, value.shape, 1) + base
-            out_ref[:, pl.ds(pl.multiple_of(base, 128), 384)] = jnp.where(row == col, value, keep_off * value)
-
-
-def gram(first, own, other, pick, order, spread, scale):
+        wide = pl.ds(block * 1152, 1152)
+        pltpu.make_async_copy(staged.at[:, wide], out_ref.at[:, wide], sems.at[block]).wait()
+
+
+def gram(first, own, other, pick, order, scale):
     whole = pl.BlockSpec(memory_space=pltpu.VMEM)
     return pl.pallas_call(
         gram_kernel,
         out_shape=jax.ShapeDtypeStruct((90, 11520), jnp.float32),
-        in_specs=[pl.BlockSpec(memory_space=pltpu.SMEM)] + [whole] * 6,
-        out_specs=whole,
+        in_specs=[pl.BlockSpec(memory_space=pltpu.SMEM)] + [whole] * 5,
+        out_specs=pl.BlockSpec(memory_space=pl.ANY),
         scratch_shapes=[
             pltpu.VMEM((TAPS * MPAD, 4 * LANES), jnp.bfloat16),
             pltpu.VMEM((TAPS * MPAD, CH), jnp.float32),
-            pltpu.VMEM((20 * MPAD, TAPS * 128), jnp.bfloat16),
+            pltpu.VMEM((90, 11520), jnp.float32),
+            pltpu.SemaphoreType.DMA((10,)),
         ],
         compiler_params=pltpu.CompilerParams(vmem_limit_bytes=58 * 1024 * 1024),
         cost_estimate=pl.CostEstimate(flops=20_000_000_000, bytes_accessed=20_000_000, transcendentals=0),
         name="gram",
-    )(first, own, other, pick, order, spread, scale)
+    )(first, own, other, pick, order, scale)
 
 
 def pack_kernel(weights_ref, order_ref, out_ref, ordered):
@@ -353,12 +350,13 @@
     col = lax.broadcasted_iota(jnp.int32, (360, 360), 1)
     tap_order = (col == (row % 40) * TAPS + (row // 40) % 3 * 3 + row // 120).astype(jnp.bfloat16)
     packed = pack(client_weights, tap_order)
-    tiles = lax.all_to_all(packed, "blk", split_axis=0, concat_axis=0, tiled=True)
-    tiles = tiles.reshape(32, 6, 40, 128).transpose(1, 0, 2, 3).reshape(6, CH, 128)
 
     live = lax.broadcasted_iota(jnp.int32, (2, 2), 1) < mine[:, None]
     masked = jnp.where(live[:, :, None, None, None], activations, jnp.zeros_like(activations))
-    pieces = gather_chips(masked.reshape(ROWS, CH))
+    masked, packed = lax.optimization_barrier((masked, packed))
+    tiles = lax.all_to_all(packed, "blk", split_axis=0, concat_axis=0, tiled=True)
+    pieces, tiles = gather_chips(masked.reshape(ROWS, CH), tiles)
+    tiles = tiles.reshape(32, 6, 40, 128).transpose(1, 0, 2, 3).reshape(6, CH, 128)
     offs = np.array(SOURCES, np.int32)
     src_x, src_y, src_z = (x + offs[:, 0]) % 4, (y + offs[:, 1]) % 4, (z + offs[:, 2]) % 4
     away = (src_x // 2 != x_hi).astype(jnp.int32)
@@ -377,15 +375,12 @@
     row = lax.broadcasted_iota(jnp.int32, (MPAD, TAPS * 16), 0)
     col = lax.broadcasted_iota(jnp.int32, (MPAD, TAPS * 16), 1)
     order = ((row // TAPS == col % 16) & (row % TAPS == col // 16)).astype(jnp.bfloat16)
-    row = lax.broadcasted_iota(jnp.int32, (1152, 1152), 0)
-    col = lax.broadcasted_iota(jnp.int32, (1152, 1152), 1)
-    spread = ((row % 128) * TAPS + row // 128 == col).astype(jnp.bfloat16)
     groups = jnp.stack([client_here, client_here ^ 2, client_here ^ 1, client_here ^ 3])
     group_scale = all_scale.reshape(4, 2)[groups]
     img_scale = jnp.repeat(jnp.repeat(group_scale, 16, axis=1)[:, None, :], 32, axis=1).reshape(4, LANES)
     gram_out = gram(
         jnp.reshape(first_channel * TAPS, (1,)), own_rows, other.reshape(2048, CH),
-        pick, order, spread, img_scale,
+        pick, order, img_scale,
     )
     return gram_out, finish(sent, gram_out)
 

time: 174 us -> 159 us (0.914)
  waiting for transfers between devices: 59.5 us -> 50.1 us
  Pallas kernels: 54.2 us -> 45.9 us
  starting transfers between devices: 40.8 us -> 45.4 us
  other arithmetic: 6.77 us -> 3.45 us
  local copies, waits for them, and re-layouts: 11.1 us -> 12.9 us
    all_to_all x1, waiting for transfers between devices: 22.1 us -> 0.01 us  [body(): lax.all_to_all(packed, 'blk', split_axis=0, concat_axis=0, tiled=True)]
    ppermute x12, waiting for transfers between devices: 37.4 us -> 48.9 us  [take_from(): return lax.ppermute(value, AXES, pairs)]
    all_to_all x1, starting transfers between devices: 4.32 us -> 9.81 us  [body(): lax.all_to_all(packed, 'blk', split_axis=0, concat_axis=0, tiled=True)]
    pallas_call x1, Pallas kernels: 9.47 us -> 4.17 us  [assemble(): pl.pallas_call(assemble_kernel, out_shape=jax.ShapeDtypeStruct((64, ROWS,...]
    convert_element_type x1 -> x0, other arithmetic: 3.31 us -> none  [body(): spread = (row % 128 * TAPS + row // 128 == col).astype(jnp.bfloat16)]
    pallas_call x1, Pallas kernels: 30.9 us -> 28 us  [gram(): pl.pallas_call(gram_kernel, out_shape=jax.ShapeDtypeStruct((90, 11520), j...]
    slice x0 -> x3, local copies, waits for them, and re-layouts: none -> 2.2 us  [gather_chips(): parts = [level[low * ROWS:high * ROWS] for _, low, high in LAST]]
    ppermute x12, starting transfers between devices: 28 us -> 25.8 us  [take_from(): return lax.ppermute(value, AXES, pairs)]
  transfers between devices with their start and end apart: 15 -> 15, of which waited for: 9 -> 8; matrix products, arithmetic and copies ran while one was open for 7% -> 4% of each run, Pallas kernels for 25% -> 23%
where the time goes in v3:
time: 159 us
  waiting for transfers between devices  50.1 us (32%)
  Pallas kernels  45.9 us (29%)
  starting transfers between devices  45.4 us (29%)
  local copies, waits for them, and re-layouts  12.9 us (8%)
  other arithmetic  3.45 us (2%)
    ppermute x12, waiting for transfers between devices, take_from(): return lax.ppermute(value, AXES, pairs)  48.9 us
    pallas_call x1, Pallas kernels, gram(): pl.pallas_call(gram_kernel, out_shape=jax.ShapeDtypeStruct((90, 11520), j...  28 us
    ppermute x12, starting transfers between devices, take_from(): return lax.ppermute(value, AXES, pairs)  25.8 us
    all_to_all x1, starting transfers between devices, body(): lax.all_to_all(packed, 'blk', split_axis=0, concat_axis=0, tiled=True)  9.81 us
    pallas_call x1, Pallas kernels, rhs_part(): pl.pallas_call(rhs_kernel, out_shape=jax.ShapeDtypeStruct((128, 32, 128),...  8.66 us
    all_to_all x1, starting transfers between devices, body(): lax.all_to_all(part, ('blk', 'client'), split_axis=0, concat_axis=0, tile...  6.65 us
    unnamed x22, local copies, waits for them, and re-layouts  6.44 us
    pallas_call x1, Pallas kernels, assemble(): pl.pallas_call(assemble_kernel, out_shape=jax.ShapeDtypeStruct((64, ROWS,...  4.17 us
  transfers between devices with their start and end apart: 15, of which 8 were waited for; matrix products, arithmetic and copies ran while one was open for 4% of the time, Pallas kernels for 23%

profile of v3, /device:TPU:1, one launch (start us, length us, event | category | flops | bytes accessed | tf_op | source)
XLA Modules:
  0.0 158.7 jit_solution(6861853363592346898)
XLA Ops:
  3.2 1.5 copy-done.2
  4.7 3.5 %pack.1 = bf16[32,240,128]{2,1,0:T(8,128)(2,1)} custom-call(bf16[2,360,1280]{2,1,0:T(8,128)(2,1)S(1)} %copy-done.2, bf16[360,360]{1,0:T(8,128)(2,1)S(1)} %fusion.6.order_ref), custom_call_target="tpu_custom_call" | custom-call | flops 1000000000 | bytes 6000000 | tf_op jit(solution)/shard_map/pack/pallas_call | solution.py:193
  8.2 9.8 %all-to-all-start = ((bf16[32,240,128]{2,1,0:T(8,128)(2,1)}), bf16[32,240,128]{2,1,0:T(8,128)(2,1)S(1)}, u32[]{:S(2)}, u32[]{:S(2)}) async-start(bf16[32,240,128]{2,1,0:T(8,128)(2,1)} %pack.1), calls=%async_computation | async-start | bytes 3932160 | tf_op jit(solution)/shard_map/all_to_all | solution.py:357
  18.0 4.8 %collective-permute-start = (bf16[32,1280]{1,0:T(8,128)(2,1)S(1)}, bf16[32,1280]{1,0:T(8,128)(2,1)S(1)}, u32[]{:S(2)}, u32[]{:S(2)}) collective-permute-start(bf16[32,1280]{1,0:T(8,128)(2,1)S(1)} %bitcast.16), channel_id=1, source_target_pairs={{12,0},{13,1},{14,2},{15,3},{72,4},{73,5},{74,6},{75,7},{20,8},{21... | collective-permute-start | bytes 245768 | tf_op jit(solution)/shard_map/ppermute | solution.py:38
  24.2 20.3 %collective-permute-done = bf16[32,1280]{1,0:T(8,128)(2,1)S(1)} collective-permute-done((bf16[32,1280]{1,0:T(8,128)(2,1)S(1)}, bf16[32,1280]{1,0:T(8,128)(2,1)S(1)}, u32[]{:S(2)}, u32[]{:S(2)}) %collective-permute-start) | collective-permute-done | bytes 81952 | tf_op jit(solution)/shard_map/ppermute | solution.py:38
  44.5 2.4 %collective-permute-done.1 = bf16[32,1280]{1,0:T(8,128)(2,1)S(1)} collective-permute-done((bf16[32,1280]{1,0:T(8,128)(2,1)S(1)}, bf16[32,1280]{1,0:T(8,128)(2,1)S(1)}, u32[]{:S(2)}, u32[]{:S(2)}) %collective-permute-start.1) | collective-permute-done | bytes 81952 | tf_op jit(solution)/shard_map/ppermute | solution.py:38
  47.0 4.4 %collective-permute-start.3 = (bf16[128,1280]{1,0:T(8,128)(2,1)S(1)}, bf16[128,1280]{1,0:T(8,128)(2,1)S(1)}, u32[]{:S(2)}, u32[]{:S(2)}) collective-permute-start(bf16[128,1280]{1,0:T(8,128)(2,1)S(1)} %pad_maximum_fusion), channel_id=1, source_target_pairs={{29,0},{30,1},{31,2},{28,3},{89,4},{90,5},{91,6},{88,7},{5,8},{6,9... | collective-permute-start | bytes 983048 | tf_op jit(solution)/shard_map/ppermute | solution.py:38
  52.1 4.1 %collective-permute-done.3 = bf16[128,1280]{1,0:T(8,128)(2,1)S(1)} collective-permute-done((bf16[128,1280]{1,0:T(8,128)(2,1)S(1)}, bf16[128,1280]{1,0:T(8,128)(2,1)S(1)}, u32[]{:S(2)}, u32[]{:S(2)}) %collective-permute-start.3) | collective-permute-done | bytes 327712 | tf_op jit(solution)/shard_map/ppermute | solution.py:38
  56.2 3.4 %collective-permute-done.4 = bf16[128,1280]{1,0:T(8,128)(2,1)S(1)} collective-permute-done((bf16[128,1280]{1,0:T(8,128)(2,1)S(1)}, bf16[128,1280]{1,0:T(8,128)(2,1)S(1)}, u32[]{:S(2)}, u32[]{:S(2)}) %collective-permute-start.4) | collective-permute-done | bytes 327712 | tf_op jit(solution)/shard_map/ppermute | solution.py:38
  59.6 3.7 %collective-permute-done.5 = bf16[128,1280]{1,0:T(8,128)(2,1)S(1)} collective-permute-done((bf16[128,1280]{1,0:T(8,128)(2,1)S(1)}, bf16[128,1280]{1,0:T(8,128)(2,1)S(1)}, u32[]{:S(2)}, u32[]{:S(2)}) %collective-permute-start.5) | collective-permute-done | bytes 327712 | tf_op jit(solution)/shard_map/ppermute | solution.py:38
  63.4 1.2 copy-done.3
  65.7 6.0 %collective-permute-start.8 = (bf16[128,1280]{1,0:T(8,128)(2,1)S(1)}, bf16[128,1280]{1,0:T(8,128)(2,1)S(1)}, u32[]{:S(2)}, u32[]{:S(2)}) collective-permute-start(bf16[128,1280]{1,0:T(8,128)(2,1)S(1)} %slice.16), channel_id=1, source_target_pairs={{3,0},{0,1},{1,2},{2,3},{7,4},{4,5},{5,6},{6,7},{11,8},{8,9},{9,10... | collective-permute-start | bytes 983048 | tf_op jit(solution)/shard_map/ppermute | solution.py:38
  73.0 1.4 collective-permute-start.7
  74.4 5.6 %collective-permute-start.10 = (bf16[256,1280]{1,0:T(8,128)(2,1)}, bf16[256,1280]{1,0:T(8,128)(2,1)}, u32[]{:S(2)}, u32[]{:S(2)}) collective-permute-start(bf16[256,1280]{1,0:T(8,128)(2,1)} %get-tuple-element.14), channel_id=1, source_target_pairs={{8,0},{9,1},{10,2},{11,3},{12,4},{13,5},{14,6},{15,7},{16,8},{17,9... | collective-permute-start | bytes 1966088 | tf_op jit(solution)/shard_map/ppermute | solution.py:38
  81.5 13.7 %collective-permute-done.6.refs_1_ = bf16[256,1280]{1,0:T(8,128)(2,1)} collective-permute-done((bf16[256,1280]{1,0:T(8,128)(2,1)}, bf16[256,1280]{1,0:T(8,128)(2,1)}, u32[]{:S(2)}, u32[]{:S(2)}) %collective-permute-start.6) | collective-permute-done | bytes 655392 | tf_op jit(solution)/shard_map/ppermute | solution.py:38
  96.4 4.2 %assemble.1 = bf16[64,32,1280]{2,1,0:T(8,128)(2,1)} custom-call(s32[64]{0:T(128)S(1)} %fusion.22.slots, bf16[512,1280]{1,0:T(8,128)(2,1)S(1)} %constant_dynamic-update-slice_fusion.refs_0_, bf16[256,1280]{1,0:T(8,128)(2,1)} %collective-permute-done.6.refs_1_, bf16[256,1280]{1,0:T(8,128)(2,1)S(1)} %collective-permute-done.7.refs_2_, ...), custom_call_target="tpu_custom_call" | custom-call | tf_op jit(solution)/shard_map/assemble/pallas_call | solution.py:76
  100.6 3.2 %collective-permute-start.12 = (bf16[64,32,1280]{2,1,0:T(8,128)(2,1)}, bf16[64,32,1280]{2,1,0:T(8,128)(2,1)}, u32[]{:S(2)}, u32[]{:S(2)}) collective-permute-start(bf16[64,32,1280]{2,1,0:T(8,128)(2,1)} %assemble.1), channel_id=1, source_target_pairs={{0,32},{1,33},{2,34},{3,35},{4,36},{5,37},{6,38},{7,39},{8,40},{9,... | collective-permute-start | bytes 15728648 | tf_op jit(solution)/shard_map/ppermute | solution.py:365
  106.2 1.9 %copy.9 = bf16[32,6,40,128]{3,2,0,1:T(8,128)(2,1)S(1)} copy(bf16[32,6,40,128]{3,2,1,0:T(8,128)(2,1)} %bitcast.15) | data formatting | bytes 3932160 | tf_op jit(solution)/shard_map/reshape | solution.py:359
  108.1 8.7 %rhs_part.1 = f32[128,32,128]{2,1,0:T(8,128)S(1)} custom-call(f32[2]{0:T(128)S(1)} %dynamic_slice.7.scale_ref, bf16[2048,1280]{1,0:T(8,128)(2,1)} %bitcast.2.own_ref.pixels_ref, bf16[6,1280,128]{2,1,0:T(8,128)(2,1)S(1)} %bitcast.14), custom_call_target="tpu_custom_call" | custom-call | flops 4000000000 | bytes 8000000 | tf_op jit(solution)/shard_map/rhs_part/pallas_call | solution.py:279
  116.8 1.4 copy-done.1
  118.1 6.6 %all-to-all-start.1 = ((f32[128,32,128]{2,1,0:T(8,128)}), f32[128,32,128]{2,1,0:T(8,128)S(1)}, u32[]{:S(2)}, u32[]{:S(2)}) async-start(f32[128,32,128]{2,1,0:T(8,128)} %copy-done.1), calls=%async_computation.1 | async-start | bytes 4194304 | tf_op jit(solution)/shard_map/all_to_all | solution.py:369
  125.6 28.0 %gram.1.after_ref = f32[90,11520]{1,0:T(8,128)} custom-call(s32[1]{0:T(128)} %bitcast.first_ref, bf16[2048,1280]{1,0:T(8,128)(2,1)} %bitcast.2.own_ref.pixels_ref, bf16[2048,1280]{1,0:T(8,128)(2,1)} %bitcast.3.other_ref, bf16[16,1280]{1,0:T(8,128)(2,1)} %fusion.11.pick_ref, bf16[96,144]{1,0:T(8,128)(2,1)} %fusion.9.order_ref, ...), custom_call_target="tpu_custom_call" | custom-call | flops 20000000000 | bytes 20000000 | tf_op jit(solution)/shard_map/gram/pallas_call | solution.py:154
  154.8 2.3 %copy-done = f32[90,11520]{1,0:T(8,128)S(1)} copy-done((f32[90,11520]{1,0:T(8,128)S(1)}, f32[90,11520]{1,0:T(8,128)}, u32[]{:S(2)}) %copy-start) | copy-done | bytes 4147224
  157.1 1.6 %finish.1 = f32[90,1280]{1,0:T(8,128)} custom-call(f32[128,32,128]{2,1,0:T(8,128)S(1)} %all-to-all-done.1.sent_ref, f32[90,11520]{1,0:T(8,128)S(1)} %copy-done), custom_call_target="tpu_custom_call" | custom-call | tf_op jit(solution)/shard_map/finish/pallas_call | solution.py:326
  (69 shorter events, 14.2 us)
Async XLA Ops:
  3.2 1.5 copy-start.2
  8.2 55.2 %all-to-all-start = ((bf16[32,240,128]{2,1,0:T(8,128)(2,1)}), bf16[32,240,128]{2,1,0:T(8,128)(2,1)S(1)}, u32[]{:S(2)}, u32[]{:S(2)}) async-start(bf16[32,240,128]{2,1,0:T(8,128)(2,1)} %pack.1), calls=%async_computation | async-start | bytes 3932160 | tf_op jit(solution)/shard_map/all_to_all | solution.py:357
  18.0 26.5 %collective-permute-start = (bf16[32,1280]{1,0:T(8,128)(2,1)S(1)}, bf16[32,1280]{1,0:T(8,128)(2,1)S(1)}, u32[]{:S(2)}, u32[]{:S(2)}) collective-permute-start(bf16[32,1280]{1,0:T(8,128)(2,1)S(1)} %bitcast.16), channel_id=1, source_target_pairs={{12,0},{13,1},{14,2},{15,3},{72,4},{73,5},{74,6},{75,7},{20,8},{21... | collective-permute-start | bytes 245768 | tf_op jit(solution)/shard_map/ppermute | solution.py:38
  22.8 24.2 %collective-permute-start.1 = (bf16[32,1280]{1,0:T(8,128)(2,1)S(1)}, bf16[32,1280]{1,0:T(8,128)(2,1)S(1)}, u32[]{:S(2)}, u32[]{:S(2)}) collective-permute-start(bf16[32,1280]{1,0:T(8,128)(2,1)S(1)} %bitcast.17), channel_id=1, source_target_pairs={{80,0},{81,1},{82,2},{83,3},{84,4},{85,5},{86,6},{87,7},{88,8},{89... | collective-permute-start | bytes 245768 | tf_op jit(solution)/shard_map/ppermute | solution.py:38
  23.5 23.4 %collective-permute-start.2 = (bf16[32,1280]{1,0:T(8,128)(2,1)S(1)}, bf16[32,1280]{1,0:T(8,128)(2,1)S(1)}, u32[]{:S(2)}, u32[]{:S(2)}) collective-permute-start(bf16[32,1280]{1,0:T(8,128)(2,1)S(1)} %bitcast.18), channel_id=1, source_target_pairs={{92,0},{93,1},{94,2},{95,3},{24,4},{25,5},{26,6},{27,7},{68,8},{69... | collective-permute-start | bytes 245768 | tf_op jit(solution)/shard_map/ppermute | solution.py:38
  47.0 9.2 %collective-permute-start.3 = (bf16[128,1280]{1,0:T(8,128)(2,1)S(1)}, bf16[128,1280]{1,0:T(8,128)(2,1)S(1)}, u32[]{:S(2)}, u32[]{:S(2)}) collective-permute-start(bf16[128,1280]{1,0:T(8,128)(2,1)S(1)} %pad_maximum_fusion), channel_id=1, source_target_pairs={{29,0},{30,1},{31,2},{28,3},{89,4},{90,5},{91,6},{88,7},{5,8},{6,9... | collective-permute-start | bytes 983048 | tf_op jit(solution)/shard_map/ppermute | solution.py:38
  51.4 8.2 %collective-permute-start.4 = (bf16[128,1280]{1,0:T(8,128)(2,1)S(1)}, bf16[128,1280]{1,0:T(8,128)(2,1)S(1)}, u32[]{:S(2)}, u32[]{:S(2)}) collective-permute-start(bf16[128,1280]{1,0:T(8,128)(2,1)S(1)} %pad_maximum_fusion), channel_id=1, source_target_pairs={{2,0},{3,1},{0,2},{1,3},{6,4},{7,5},{4,6},{5,7},{10,8},{11,9},{8,1... | collective-permute-start | bytes 983048 | tf_op jit(solution)/shard_map/ppermute | solution.py:38
  51.6 11.8 %collective-permute-start.5 = (bf16[128,1280]{1,0:T(8,128)(2,1)S(1)}, bf16[128,1280]{1,0:T(8,128)(2,1)S(1)}, u32[]{:S(2)}, u32[]{:S(2)}) collective-permute-start(bf16[128,1280]{1,0:T(8,128)(2,1)S(1)} %pad_maximum_fusion), channel_id=1, source_target_pairs={{79,0},{76,1},{77,2},{78,3},{11,4},{8,5},{9,6},{10,7},{87,8},{84,9... | collective-permute-start | bytes 983048 | tf_op jit(solution)/shard_map/ppermute | solution.py:38
  63.4 1.3 copy-start.3
  65.7 15.8 %copy-start.4 = (s32[64]{0:T(128)S(1)}, s32[64]{0:T(128)}, u32[]{:S(2)}) copy-start(s32[64]{0:T(128)} %constant.192.clone) | copy-start | bytes 772
  65.7 15.8 %copy-start.5 = (s32[64]{0:T(128)S(1)}, s32[64]{0:T(128)}, u32[]{:S(2)}) copy-start(s32[64]{0:T(128)} %constant.193.clone) | copy-start | bytes 772
  65.7 15.8 %copy-start.6 = (s32[64]{0:T(128)S(1)}, s32[64]{0:T(128)}, u32[]{:S(2)}) copy-start(s32[64]{0:T(128)} %constant.191.clone) | copy-start | bytes 772
  65.7 15.0 %collective-permute-start.8 = (bf16[128,1280]{1,0:T(8,128)(2,1)S(1)}, bf16[128,1280]{1,0:T(8,128)(2,1)S(1)}, u32[]{:S(2)}, u32[]{:S(2)}) collective-permute-start(bf16[128,1280]{1,0:T(8,128)(2,1)S(1)} %slice.16), channel_id=1, source_target_pairs={{3,0},{0,1},{1,2},{2,3},{7,4},{4,5},{5,6},{6,7},{11,8},{8,9},{9,10... | collective-permute-start | bytes 983048 | tf_op jit(solution)/shard_map/ppermute | solution.py:38
  71.7 24.8 %collective-permute-start.11 = (bf16[384,1280]{1,0:T(8,128)(2,1)}, bf16[384,1280]{1,0:T(8,128)(2,1)S(1)}, u32[]{:S(2)}, u32[]{:S(2)}) collective-permute-start(bf16[384,1280]{1,0:T(8,128)(2,1)} %slice.17), channel_id=1, source_target_pairs={{1,0},{2,1},{3,2},{0,3},{5,4},{6,5},{7,6},{4,7},{9,8},{10,9},{11,1... | collective-permute-start | bytes 2949128 | tf_op jit(solution)/shard_map/ppermute | solution.py:38
  73.0 22.2 %collective-permute-start.7 = (bf16[256,1280]{1,0:T(8,128)(2,1)}, bf16[256,1280]{1,0:T(8,128)(2,1)S(1)}, u32[]{:S(2)}, u32[]{:S(2)}) collective-permute-start(bf16[256,1280]{1,0:T(8,128)(2,1)} %get-tuple-element.14), channel_id=1, source_target_pairs={{24,0},{25,1},{26,2},{27,3},{28,4},{29,5},{30,6},{31,7},{0,8},{1,9... | collective-permute-start | bytes 1966088 | tf_op jit(solution)/shard_map/ppermute | solution.py:38
  74.4 20.8 %collective-permute-start.10 = (bf16[256,1280]{1,0:T(8,128)(2,1)}, bf16[256,1280]{1,0:T(8,128)(2,1)}, u32[]{:S(2)}, u32[]{:S(2)}) collective-permute-start(bf16[256,1280]{1,0:T(8,128)(2,1)} %get-tuple-element.14), channel_id=1, source_target_pairs={{8,0},{9,1},{10,2},{11,3},{12,4},{13,5},{14,6},{15,7},{16,8},{17,9... | collective-permute-start | bytes 1966088 | tf_op jit(solution)/shard_map/ppermute | solution.py:38
  80.0 15.2 %collective-permute-start.6 = (bf16[256,1280]{1,0:T(8,128)(2,1)}, bf16[256,1280]{1,0:T(8,128)(2,1)}, u32[]{:S(2)}, u32[]{:S(2)}) collective-permute-start(bf16[256,1280]{1,0:T(8,128)(2,1)} %get-tuple-element.11), channel_id=1, source_target_pairs={{4,0},{5,1},{6,2},{7,3},{64,4},{65,5},{66,6},{67,7},{12,8},{13,9},... | collective-permute-start | bytes 1966088 | tf_op jit(solution)/shard_map/ppermute | solution.py:38
  80.7 15.7 %collective-permute-start.9 = (bf16[256,1280]{1,0:T(8,128)(2,1)}, bf16[256,1280]{1,0:T(8,128)(2,1)}, u32[]{:S(2)}, u32[]{:S(2)}) collective-permute-start(bf16[256,1280]{1,0:T(8,128)(2,1)} %get-tuple-element.11), channel_id=1, source_target_pairs={{68,0},{69,1},{70,2},{71,3},{0,4},{1,5},{2,6},{3,7},{76,8},{77,9},... | collective-permute-start | bytes 1966088 | tf_op jit(solution)/shard_map/ppermute | solution.py:38
  81.5 22.2 %copy-start.7 = (s32[8]{0:T(128)S(1)}, s32[8]{0:T(128)}, u32[]{:S(2)}) copy-start(s32[8]{0:T(128)} %param.7) | copy-start | bytes 100
  100.6 25.0 %collective-permute-start.12 = (bf16[64,32,1280]{2,1,0:T(8,128)(2,1)}, bf16[64,32,1280]{2,1,0:T(8,128)(2,1)}, u32[]{:S(2)}, u32[]{:S(2)}) collective-permute-start(bf16[64,32,1280]{2,1,0:T(8,128)(2,1)} %assemble.1), channel_id=1, source_target_pairs={{0,32},{1,33},{2,34},{3,35},{4,36},{5,37},{6,38},{7,39},{8,40},{9,... | collective-permute-start | bytes 15728648 | tf_op jit(solution)/shard_map/ppermute | solution.py:365
  116.8 1.4 copy-start.1
  118.1 36.7 %all-to-all-start.1 = ((f32[128,32,128]{2,1,0:T(8,128)}), f32[128,32,128]{2,1,0:T(8,128)S(1)}, u32[]{:S(2)}, u32[]{:S(2)}) async-start(f32[128,32,128]{2,1,0:T(8,128)} %copy-done.1), calls=%async_computation.1 | async-start | bytes 4194304 | tf_op jit(solution)/shard_map/all_to_all | solution.py:369
  154.8 2.3 %copy-start = (f32[90,11520]{1,0:T(8,128)S(1)}, f32[90,11520]{1,0:T(8,128)}, u32[]{:S(2)}) copy-start(f32[90,11520]{1,0:T(8,128)} %gram.1.after_ref) | copy-start | bytes 12441604

commit v4 on v3

--- a/solution.py
+++ b/solution.py
@@ -53,14 +53,16 @@
 assert len(SOURCES) == 64 and len(set(SOURCES)) == 64
 
 
-def gather_chips(block, tiles):
+def gather_chips(block, tiles, early):
     level = jnp.concatenate([block] + [take_from(block, o) for o in FIRST[1:]], axis=0)
+    level, early = lax.optimization_barrier((level, early))
     level = jnp.concatenate([level] + [take_from(level, o) for o in SECOND[1:]], axis=0)
     level, tiles = lax.optimization_barrier((level, tiles))
     parts = [level[low * ROWS : high * ROWS] for _, low, high in LAST]
     small = take_from(parts[5], LAST[5][0])
-    parts[2], small = lax.optimization_barrier((parts[2], small))
-    return [level] + [take_from(part, last[0]) for part, last in zip(parts[:5], LAST)] + [small], tiles
+    tiles = tiles.reshape(32, 6, 40, 128).transpose(1, 0, 2, 3).reshape(6, CH, 128)
+    parts[2], small, tiles = lax.optimization_barrier((parts[2], small, tiles))
+    return [level] + [take_from(part, last[0]) for part, last in zip(parts[:5], LAST)] + [small], tiles, early
 
 
 def assemble_kernel(slots, *refs):
@@ -93,10 +95,19 @@
     return jnp.where(inside, moved, 0.0)
 
 
-def gram_kernel(first_ref, own_ref, other_ref, pick_ref, order_ref, scale_ref, out_ref, left, acc, staged, sems):
+def gram_kernel(first_ref, own_hbm, other_hbm, pick_ref, order_ref, scale_ref, out_ref, token_ref, left, acc, staged, pixels_own, pixels_other, sems, loads):
+    own_ref, other_ref = pixels_own, pixels_other
+    copies = []
+    for group in range(4):
+        rows = pl.ds((group % 2) * LANES, LANES)
+        source, target = (own_hbm, pixels_own) if group < 2 else (other_hbm, pixels_other)
+        copies.append(pltpu.make_async_copy(source.at[rows], target.at[rows], loads.at[group]))
+        copies[-1].start()
+    token_ref[...] = jnp.zeros_like(token_ref)
     pick = pick_ref[...]
     order = order_ref[...]
     for group in range(4):
+        copies[group].wait()
         source = own_ref if group < 2 else other_ref
         pixels = source[pl.ds((group % 2) * LANES, LANES), :]
         slab = lax.dot_general(pick, pixels, (((1,), (1,)), ((), ())), preferred_element_type=jnp.float32)
@@ -151,16 +162,20 @@
 
 def gram(first, own, other, pick, order, scale):
     whole = pl.BlockSpec(memory_space=pltpu.VMEM)
+    held = pl.BlockSpec(memory_space=pltpu.HBM)
     return pl.pallas_call(
         gram_kernel,
-        out_shape=jax.ShapeDtypeStruct((90, 11520), jnp.float32),
-        in_specs=[pl.BlockSpec(memory_space=pltpu.SMEM)] + [whole] * 5,
-        out_specs=pl.BlockSpec(memory_space=pl.ANY),
+        out_shape=(jax.ShapeDtypeStruct((90, 11520), jnp.float32), jax.ShapeDtypeStruct((8, 128), jnp.float32)),
+        in_specs=[pl.BlockSpec(memory_space=pltpu.SMEM), held, held] + [whole] * 3,
+        out_specs=(held, whole),
         scratch_shapes=[
             pltpu.VMEM((TAPS * MPAD, 4 * LANES), jnp.bfloat16),
             pltpu.VMEM((TAPS * MPAD, CH), jnp.float32),
             pltpu.VMEM((90, 11520), jnp.float32),
+            pltpu.VMEM((2 * LANES, CH), jnp.bfloat16),
+            pltpu.VMEM((2 * LANES, CH), jnp.bfloat16),
             pltpu.SemaphoreType.DMA((10,)),
+            pltpu.SemaphoreType.DMA((4,)),
         ],
         compiler_params=pltpu.CompilerParams(vmem_limit_bytes=58 * 1024 * 1024),
         cost_estimate=pl.CostEstimate(flops=20_000_000_000, bytes_accessed=20_000_000, transcendentals=0),
@@ -219,7 +234,7 @@
     return jnp.where((col >= 0) & (col < 8), moved, 0.0)
 
 
-def rhs_kernel(scale_ref, pixels_ref, tiles_ref, out_ref, rhs):
+def rhs_kernel(scale_ref, pixels_ref, tiles_ref, out_ref, rhs, staged, sems):
     lane = lax.broadcasted_iota(jnp.int32, (1, 128), 1)
     tap_row = lax.broadcasted_iota(jnp.int32, (16, 384), 0)
     tap_lane = lax.broadcasted_iota(jnp.int32, (16, 384), 1)
@@ -268,10 +283,18 @@
             diag = diag - head.astype(jnp.float32)
         value = keep_off * cross + wide * tiles.astype(jnp.float32)
         rhs[...] = value if c == 0 else rhs[...] + value
-    for dest in range(128):
-        for a in range(3):
-            out_ref[dest, pl.ds(a * OWN, OWN), :] = rhs[pl.ds(dest * OWN, OWN), pl.ds(a * 128, 128)]
-        out_ref[dest, pl.ds(30, 2), :] = jnp.zeros((2, 128), jnp.float32)
+    zeros = jnp.zeros((2, 128), jnp.float32)
+    copies = []
+    for part in range(8):
+        for dest in range(part * 16, part * 16 + 16):
+            for a in range(3):
+                staged[dest, pl.ds(a * OWN, OWN), :] = rhs[pl.ds(dest * OWN, OWN), pl.ds(a * 128, 128)]
+            staged[dest, pl.ds(30, 2), :] = zeros
+        some = pl.ds(part * 16, 16)
+        copies.append(pltpu.make_async_copy(staged.at[some], out_ref.at[some], sems.at[part]))
+        copies[-1].start()
+    for copy in copies:
+        copy.wait()
 
 
 def rhs_part(scale, pixels, tiles):
@@ -281,8 +304,12 @@
         out_shape=jax.ShapeDtypeStruct((128, 32, 128), jnp.float32),
         in_specs=[pl.BlockSpec(memory_space=pltpu.SMEM), pl.BlockSpec((1024, CH), lambda i: (0, 0)), pl.BlockSpec((6, CH, 128), lambda i: (0, 0, 0))],
         grid=(1,),
-        out_specs=pl.BlockSpec((128, 32, 128), lambda i: (0, 0, 0)),
-        scratch_shapes=[pltpu.VMEM((CH, 384), jnp.float32)],
+        out_specs=pl.BlockSpec(memory_space=pltpu.HBM),
+        scratch_shapes=[
+            pltpu.VMEM((CH, 384), jnp.float32),
+            pltpu.VMEM((128, 32, 128), jnp.float32),
+            pltpu.SemaphoreType.DMA((8,)),
+        ],
         compiler_params=pltpu.CompilerParams(vmem_limit_bytes=48 * 1024 * 1024),
         cost_estimate=pl.CostEstimate(flops=4_000_000_000, bytes_accessed=8_000_000, transcendentals=0),
         name="rhs_part",
@@ -326,7 +353,7 @@
     return pl.pallas_call(
         finish_kernel,
         out_shape=jax.ShapeDtypeStruct((90, CH), jnp.float32),
-        in_specs=[whole, pl.BlockSpec(memory_space=pl.ANY)],
+        in_specs=[whole, whole],
         out_specs=whole,
         scratch_shapes=[pltpu.VMEM((96, CH), jnp.float32)],
         compiler_params=pltpu.CompilerParams(vmem_limit_bytes=16 * 1024 * 1024),
@@ -352,22 +379,6 @@
     packed = pack(client_weights, tap_order)
 
     live = lax.broadcasted_iota(jnp.int32, (2, 2), 1) < mine[:, None]
-    masked = jnp.where(live[:, :, None, None, None], activations, jnp.zeros_like(activations))
-    masked, packed = lax.optimization_barrier((masked, packed))
-    tiles = lax.all_to_all(packed, "blk", split_axis=0, concat_axis=0, tiled=True)
-    pieces, tiles = gather_chips(masked.reshape(ROWS, CH), tiles)
-    tiles = tiles.reshape(32, 6, 40, 128).transpose(1, 0, 2, 3).reshape(6, CH, 128)
-    offs = np.array(SOURCES, np.int32)
-    src_x, src_y, src_z = (x + offs[:, 0]) % 4, (y + offs[:, 1]) % 4, (z + offs[:, 2]) % 4
-    away = (src_x // 2 != x_hi).astype(jnp.int32)
-    slots = (away * 32 + src_z * 8 + (src_x % 2) * 4 + src_y).astype(jnp.int32)
-    own = assemble(slots, pieces)
-    other = lax.ppermute(own, AXES, [(d, d ^ 32) for d in range(128)])
-
-    own_rows = own.reshape(2048, CH)
-    part = rhs_part(my_scale, own_rows, tiles)
-    sent = lax.all_to_all(part, ("blk", "client"), split_axis=0, concat_axis=0, tiled=True)
-
     first_channel = blk_here * 40 + client_here * OWN
     chan = lax.broadcasted_iota(jnp.int32, (16, CH), 1) - first_channel
     lane = lax.broadcasted_iota(jnp.int32, (16, CH), 0)
@@ -378,11 +389,27 @@
     groups = jnp.stack([client_here, client_here ^ 2, client_here ^ 1, client_here ^ 3])
     group_scale = all_scale.reshape(4, 2)[groups]
     img_scale = jnp.repeat(jnp.repeat(group_scale, 16, axis=1)[:, None, :], 32, axis=1).reshape(4, LANES)
-    gram_out = gram(
+
+    masked = jnp.where(live[:, :, None, None, None], activations, jnp.zeros_like(activations))
+    tiles = lax.all_to_all(packed, "blk", split_axis=0, concat_axis=0, tiled=True)
+    offs = np.array(SOURCES, np.int32)
+    src_x, src_y, src_z = (x + offs[:, 0]) % 4, (y + offs[:, 1]) % 4, (z + offs[:, 2]) % 4
+    away = (src_x // 2 != x_hi).astype(jnp.int32)
+    slots = (away * 32 + src_z * 8 + (src_x % 2) * 4 + src_y).astype(jnp.int32)
+    pieces, tiles, early = gather_chips(masked.reshape(ROWS, CH), tiles, (pick, order, img_scale, slots))
+    pick, order, img_scale, slots = early
+    own = assemble(slots, pieces)
+    other = lax.ppermute(own, AXES, [(d, d ^ 32) for d in range(128)])
+
+    own_rows = own.reshape(2048, CH)
+    part = rhs_part(my_scale, own_rows, tiles)
+    sent = lax.all_to_all(part, ("blk", "client"), split_axis=0, concat_axis=0, tiled=True)
+
+    gram_out, token = gram(
         jnp.reshape(first_channel * TAPS, (1,)), own_rows, other.reshape(2048, CH),
         pick, order, img_scale,
     )
-    return gram_out, finish(sent, gram_out)
+    return gram_out, finish(sent, token)
 
 
 def solution(mesh):

time: 159 us -> 145 us (0.912)
  waiting for transfers between devices: 50.1 us -> 41.2 us
  local copies, waits for them, and re-layouts: 12.9 us -> 6.36 us
    ppermute x12, waiting for transfers between devices: 48.9 us -> 40.1 us  [take_from(): return lax.ppermute(value, AXES, pairs)]
    ppermute x12, starting transfers between devices: 25.8 us -> 32 us  [take_from(): return lax.ppermute(value, AXES, pairs)]
    all_to_all x1, starting transfers between devices: 9.81 us -> 5.2 us  [body(): lax.all_to_all(packed, 'blk', split_axis=0, concat_axis=0, tiled=True)]
    unnamed x22 -> x14, local copies, waits for them, and re-layouts: 6.44 us -> 3.54 us
    slice x3, local copies, waits for them, and re-layouts: 2.2 us -> 0.17 us  [gather_chips(): parts = [level[low * ROWS:high * ROWS] for _, low, high in LAST]]
  transfers between devices with their start and end apart: 15 -> 15, of which waited for: 8 -> 5; matrix products, arithmetic and copies ran while one was open for 4% -> 3% of each run, Pallas kernels for 23% -> 29%
where the time goes in v4:
time: 145 us
  starting transfers between devices  46.7 us (32%)
  Pallas kernels  46.1 us (32%)
  waiting for transfers between devices  41.2 us (28%)
  local copies, waits for them, and re-layouts  6.36 us (4%)
  other arithmetic  3.54 us (2%)
    ppermute x12, waiting for transfers between devices, take_from(): return lax.ppermute(value, AXES, pairs)  40.1 us
    ppermute x12, starting transfers between devices, take_from(): return lax.ppermute(value, AXES, pairs)  32 us
    pallas_call x1, Pallas kernels, gram(): pl.pallas_call(gram_kernel, out_shape=(jax.ShapeDtypeStruct((90, 11520),...  28.9 us
    pallas_call x1, Pallas kernels, rhs_part(): pl.pallas_call(rhs_kernel, out_shape=jax.ShapeDtypeStruct((128, 32, 128),...  8.86 us
    all_to_all x1, starting transfers between devices, body(): lax.all_to_all(part, ('blk', 'client'), split_axis=0, concat_axis=0, tile...  6.72 us
    all_to_all x1, starting transfers between devices, body(): lax.all_to_all(packed, 'blk', split_axis=0, concat_axis=0, tiled=True)  5.2 us
    pallas_call x1, Pallas kernels, pack(): pl.pallas_call(pack_kernel, out_shape=jax.ShapeDtypeStruct((32, 240, 128)...  3.56 us
    unnamed x14, local copies, waits for them, and re-layouts  3.54 us
  transfers between devices with their start and end apart: 15, of which 5 were waited for; matrix products, arithmetic and copies ran while one was open for 3% of the time, Pallas kernels for 29%

profile of v4, /device:TPU:1, one launch (start us, length us, event | category | flops | bytes accessed | tf_op | source)
XLA Modules:
  0.0 144.8 jit_solution(13124062542360227459)
XLA Ops:
  2.4 3.5 %collective-permute-start.2 = (bf16[32,1280]{1,0:T(8,128)(2,1)S(1)}, bf16[32,1280]{1,0:T(8,128)(2,1)S(1)}, u32[]{:S(2)}, u32[]{:S(2)}) collective-permute-start(bf16[32,1280]{1,0:T(8,128)(2,1)S(1)} %bitcast.16), channel_id=1, source_target_pairs={{92,0},{93,1},{94,2},{95,3},{24,4},{25,5},{26,6},{27,7},{68,8},{69... | collective-permute-start | bytes 245768 | tf_op jit(solution)/shard_map/ppermute | solution.py:38
  5.9 5.5 %collective-permute-start.1 = (bf16[32,1280]{1,0:T(8,128)(2,1)S(1)}, bf16[32,1280]{1,0:T(8,128)(2,1)S(1)}, u32[]{:S(2)}, u32[]{:S(2)}) collective-permute-start(bf16[32,1280]{1,0:T(8,128)(2,1)S(1)} %bitcast.17), channel_id=1, source_target_pairs={{80,0},{81,1},{82,2},{83,3},{84,4},{85,5},{86,6},{87,7},{88,8},{89... | collective-permute-start | bytes 245768 | tf_op jit(solution)/shard_map/ppermute | solution.py:38
  11.3 1.6 %collective-permute-start = (bf16[32,1280]{1,0:T(8,128)(2,1)S(1)}, bf16[32,1280]{1,0:T(8,128)(2,1)S(1)}, u32[]{:S(2)}, u32[]{:S(2)}) collective-permute-start(bf16[32,1280]{1,0:T(8,128)(2,1)S(1)} %bitcast.18), channel_id=1, source_target_pairs={{12,0},{13,1},{14,2},{15,3},{72,4},{73,5},{74,6},{75,7},{20,8},{21... | collective-permute-start | bytes 245768 | tf_op jit(solution)/shard_map/ppermute | solution.py:38
  13.7 1.5 %copy-done.1 = bf16[2,360,1280]{2,1,0:T(8,128)(2,1)S(1)} copy-done((bf16[2,360,1280]{2,1,0:T(8,128)(2,1)S(1)}, bf16[2,360,1280]{2,1,0:T(8,128)(2,1)}, u32[]{:S(2)}) %copy-start.1) | copy-done | bytes 1843224
  15.2 3.6 %pack.1 = bf16[32,240,128]{2,1,0:T(8,128)(2,1)} custom-call(bf16[2,360,1280]{2,1,0:T(8,128)(2,1)S(1)} %copy-done.1, bf16[360,360]{1,0:T(8,128)(2,1)S(1)} %fusion.6.order_ref), custom_call_target="tpu_custom_call" | custom-call | flops 1000000000 | bytes 6000000 | tf_op jit(solution)/shard_map/pack/pallas_call | solution.py:208
  18.8 5.2 %all-to-all-start = ((bf16[32,240,128]{2,1,0:T(8,128)(2,1)}), bf16[32,240,128]{2,1,0:T(8,128)(2,1)S(1)}, u32[]{:S(2)}, u32[]{:S(2)}) async-start(bf16[32,240,128]{2,1,0:T(8,128)(2,1)} %pack.1), calls=%async_computation | async-start | bytes 3932160 | tf_op jit(solution)/shard_map/all_to_all | solution.py:394
  27.3 4.4 %collective-permute-start.5 = (bf16[128,1280]{1,0:T(8,128)(2,1)S(1)}, bf16[128,1280]{1,0:T(8,128)(2,1)S(1)}, u32[]{:S(2)}, u32[]{:S(2)}) collective-permute-start(bf16[128,1280]{1,0:T(8,128)(2,1)S(1)} %pad_maximum_fusion.1), channel_id=1, source_target_pairs={{79,0},{76,1},{77,2},{78,3},{11,4},{8,5},{9,6},{10,7},{87,8},{84,9... | collective-permute-start | bytes 983048 | tf_op jit(solution)/shard_map/ppermute | solution.py:38
  31.7 2.4 %collective-permute-start.4 = (bf16[128,1280]{1,0:T(8,128)(2,1)S(1)}, bf16[128,1280]{1,0:T(8,128)(2,1)S(1)}, u32[]{:S(2)}, u32[]{:S(2)}) collective-permute-start(bf16[128,1280]{1,0:T(8,128)(2,1)S(1)} %pad_maximum_fusion.1), channel_id=1, source_target_pairs={{2,0},{3,1},{0,2},{1,3},{6,4},{7,5},{4,6},{5,7},{10,8},{11,9},{8,1... | collective-permute-start | bytes 983048 | tf_op jit(solution)/shard_map/ppermute | solution.py:38
  34.1 1.1 collective-permute-start.3
  35.2 19.6 %collective-permute-done.5 = bf16[128,1280]{1,0:T(8,128)(2,1)S(1)} collective-permute-done((bf16[128,1280]{1,0:T(8,128)(2,1)S(1)}, bf16[128,1280]{1,0:T(8,128)(2,1)S(1)}, u32[]{:S(2)}, u32[]{:S(2)}) %collective-permute-start.5) | collective-permute-done | bytes 327712 | tf_op jit(solution)/shard_map/ppermute | solution.py:38
  54.7 8.3 %collective-permute-done.4 = bf16[128,1280]{1,0:T(8,128)(2,1)S(1)} collective-permute-done((bf16[128,1280]{1,0:T(8,128)(2,1)S(1)}, bf16[128,1280]{1,0:T(8,128)(2,1)S(1)}, u32[]{:S(2)}, u32[]{:S(2)}) %collective-permute-start.4) | collective-permute-done | bytes 327712 | tf_op jit(solution)/shard_map/ppermute | solution.py:38
  63.3 2.2 %collective-permute-start.8 = (bf16[128,1280]{1,0:T(8,128)(2,1)S(1)}, bf16[128,1280]{1,0:T(8,128)(2,1)S(1)}, u32[]{:S(2)}, u32[]{:S(2)}) collective-permute-start(bf16[128,1280]{1,0:T(8,128)(2,1)S(1)} %slice.16), channel_id=1, source_target_pairs={{3,0},{0,1},{1,2},{2,3},{7,4},{4,5},{5,6},{6,7},{11,8},{8,9},{9,10... | collective-permute-start | bytes 983048 | tf_op jit(solution)/shard_map/ppermute | solution.py:38
  66.1 5.0 %collective-permute-start.7 = (bf16[256,1280]{1,0:T(8,128)(2,1)S(1)}, bf16[256,1280]{1,0:T(8,128)(2,1)S(1)}, u32[]{:S(2)}, u32[]{:S(2)}) collective-permute-start(bf16[256,1280]{1,0:T(8,128)(2,1)S(1)} %get-tuple-element.26), channel_id=1, source_target_pairs={{24,0},{25,1},{26,2},{27,3},{28,4},{29,5},{30,6},{31,7},{0,8},{1,9... | collective-permute-start | bytes 1966088 | tf_op jit(solution)/shard_map/ppermute | solution.py:38
  72.1 5.3 %collective-permute-start.9 = (bf16[256,1280]{1,0:T(8,128)(2,1)S(1)}, bf16[256,1280]{1,0:T(8,128)(2,1)S(1)}, u32[]{:S(2)}, u32[]{:S(2)}) collective-permute-start(bf16[256,1280]{1,0:T(8,128)(2,1)S(1)} %get-tuple-element.18), channel_id=1, source_target_pairs={{68,0},{69,1},{70,2},{71,3},{0,4},{1,5},{2,6},{3,7},{76,8},{77,9},... | collective-permute-start | bytes 1966088 | tf_op jit(solution)/shard_map/ppermute | solution.py:38
  77.3 8.6 %collective-permute-done.6.refs_1_ = bf16[256,1280]{1,0:T(8,128)(2,1)S(1)} collective-permute-done((bf16[256,1280]{1,0:T(8,128)(2,1)S(1)}, bf16[256,1280]{1,0:T(8,128)(2,1)S(1)}, u32[]{:S(2)}, u32[]{:S(2)}) %collective-permute-start.6) | collective-permute-done | bytes 655392 | tf_op jit(solution)/shard_map/ppermute | solution.py:38
  85.9 3.6 %collective-permute-done.9.refs_3_ = bf16[256,1280]{1,0:T(8,128)(2,1)S(1)} collective-permute-done((bf16[256,1280]{1,0:T(8,128)(2,1)S(1)}, bf16[256,1280]{1,0:T(8,128)(2,1)S(1)}, u32[]{:S(2)}, u32[]{:S(2)}) %collective-permute-start.9) | collective-permute-done | bytes 655392 | tf_op jit(solution)/shard_map/ppermute | solution.py:38
  89.5 3.2 %assemble.1 = bf16[64,32,1280]{2,1,0:T(8,128)(2,1)} custom-call(s32[64]{0:T(128)S(1)} %fusion.22.slots, bf16[512,1280]{1,0:T(8,128)(2,1)S(1)} %pad_maximum_fusion.refs_0_, bf16[256,1280]{1,0:T(8,128)(2,1)S(1)} %collective-permute-done.6.refs_1_, bf16[256,1280]{1,0:T(8,128)(2,1)S(1)} %collective-permute-done.7.refs_2_, ...), custom_call_target="tpu_custom_call" | custom-call | tf_op jit(solution)/shard_map/assemble/pallas_call | solution.py:78
  92.7 2.8 %collective-permute-start.12 = (bf16[64,32,1280]{2,1,0:T(8,128)(2,1)}, bf16[64,32,1280]{2,1,0:T(8,128)(2,1)}, u32[]{:S(2)}, u32[]{:S(2)}) collective-permute-start(bf16[64,32,1280]{2,1,0:T(8,128)(2,1)} %assemble.1), channel_id=1, source_target_pairs={{0,32},{1,33},{2,34},{3,35},{4,36},{5,37},{6,38},{7,39},{8,40},{9,... | collective-permute-start | bytes 15728648 | tf_op jit(solution)/shard_map/ppermute | solution.py:402
  95.6 8.9 %rhs_part.1 = f32[128,32,128]{2,1,0:T(8,128)S(1)} custom-call(f32[2]{0:T(128)S(1)} %dynamic_slice.7.scale_ref, bf16[2048,1280]{1,0:T(8,128)(2,1)} %bitcast.10.own_hbm.pixels_ref, bf16[6,1280,128]{2,1,0:T(8,128)(2,1)S(1)} %bitcast.14), custom_call_target="tpu_custom_call" | custom-call | flops 4000000000 | bytes 8000000 | tf_op jit(solution)/shard_map/rhs_part/pallas_call | solution.py:302
  104.4 1.4 copy-done
  105.8 6.7 %all-to-all-start.1 = ((f32[128,32,128]{2,1,0:T(8,128)}), f32[128,32,128]{2,1,0:T(8,128)S(1)}, u32[]{:S(2)}, u32[]{:S(2)}) async-start(f32[128,32,128]{2,1,0:T(8,128)} %copy-done), calls=%async_computation.1 | async-start | bytes 4194304 | tf_op jit(solution)/shard_map/all_to_all | solution.py:406
  112.5 28.9 %gram.1 = (f32[90,11520]{1,0:T(8,128)}, f32[8,128]{1,0:T(8,128)}) custom-call(s32[1]{0:T(128)} %bitcast.first_ref, bf16[2048,1280]{1,0:T(8,128)(2,1)} %bitcast.10.own_hbm.pixels_ref, bf16[2048,1280]{1,0:T(8,128)(2,1)} %bitcast.11.other_hbm, bf16[16,1280]{1,0:T(8,128)(2,1)} %fusion.11.pick_ref, bf16[96,144]{1,0:T(8,128)(2,1)} %fusion.9.order_ref, ...), custom_call_target="tpu_custom_call" | custom-call | flops 20000000000 | bytes 20000000 | tf_op jit(solution)/shard_map/gram/pallas_call | solution.py:166
  141.4 1.1 all-to-all-done.1.sent_ref
  143.2 1.6 %finish.1 = f32[90,1280]{1,0:T(8,128)} custom-call(f32[128,32,128]{2,1,0:T(8,128)S(1)} %all-to-all-done.1.sent_ref, f32[8,128]{1,0:T(8,128)S(1)} %copy-done.2), custom_call_target="tpu_custom_call" | custom-call | tf_op jit(solution)/shard_map/finish/pallas_call | solution.py:353
  (61 shorter events, 8.2 us)
Async XLA Ops:
  2.4 24.8 %collective-permute-start.2 = (bf16[32,1280]{1,0:T(8,128)(2,1)S(1)}, bf16[32,1280]{1,0:T(8,128)(2,1)S(1)}, u32[]{:S(2)}, u32[]{:S(2)}) collective-permute-start(bf16[32,1280]{1,0:T(8,128)(2,1)S(1)} %bitcast.16), channel_id=1, source_target_pairs={{92,0},{93,1},{94,2},{95,3},{24,4},{25,5},{26,6},{27,7},{68,8},{69... | collective-permute-start | bytes 245768 | tf_op jit(solution)/shard_map/ppermute | solution.py:38
  5.9 21.4 %collective-permute-start.1 = (bf16[32,1280]{1,0:T(8,128)(2,1)S(1)}, bf16[32,1280]{1,0:T(8,128)(2,1)S(1)}, u32[]{:S(2)}, u32[]{:S(2)}) collective-permute-start(bf16[32,1280]{1,0:T(8,128)(2,1)S(1)} %bitcast.17), channel_id=1, source_target_pairs={{80,0},{81,1},{82,2},{83,3},{84,4},{85,5},{86,6},{87,7},{88,8},{89... | collective-permute-start | bytes 245768 | tf_op jit(solution)/shard_map/ppermute | solution.py:38
  11.3 15.9 %collective-permute-start = (bf16[32,1280]{1,0:T(8,128)(2,1)S(1)}, bf16[32,1280]{1,0:T(8,128)(2,1)S(1)}, u32[]{:S(2)}, u32[]{:S(2)}) collective-permute-start(bf16[32,1280]{1,0:T(8,128)(2,1)S(1)} %bitcast.18), channel_id=1, source_target_pairs={{12,0},{13,1},{14,2},{15,3},{72,4},{73,5},{74,6},{75,7},{20,8},{21... | collective-permute-start | bytes 245768 | tf_op jit(solution)/shard_map/ppermute | solution.py:38
  13.7 1.5 %copy-start.1 = (bf16[2,360,1280]{2,1,0:T(8,128)(2,1)S(1)}, bf16[2,360,1280]{2,1,0:T(8,128)(2,1)}, u32[]{:S(2)}) copy-start(bf16[2,360,1280]{2,1,0:T(8,128)(2,1)} %weights_ref.1) | copy-start | bytes 5529604
  18.8 5.3 %copy-start.6 = (s32[8]{0:T(128)S(1)}, s32[8]{0:T(128)}, u32[]{:S(2)}) copy-start(s32[8]{0:T(128)} %param.7) | copy-start | bytes 100
  18.8 5.5 %copy-start.3 = (s32[64]{0:T(128)S(1)}, s32[64]{0:T(128)}, u32[]{:S(2)}) copy-start(s32[64]{0:T(128)} %constant.192.clone) | copy-start | bytes 772
  18.8 5.5 %copy-start.4 = (s32[64]{0:T(128)S(1)}, s32[64]{0:T(128)}, u32[]{:S(2)}) copy-start(s32[64]{0:T(128)} %constant.193.clone) | copy-start | bytes 772
  18.8 5.5 %copy-start.5 = (s32[64]{0:T(128)S(1)}, s32[64]{0:T(128)}, u32[]{:S(2)}) copy-start(s32[64]{0:T(128)} %constant.191.clone) | copy-start | bytes 772
  18.8 44.4 %all-to-all-start = ((bf16[32,240,128]{2,1,0:T(8,128)(2,1)}), bf16[32,240,128]{2,1,0:T(8,128)(2,1)S(1)}, u32[]{:S(2)}, u32[]{:S(2)}) async-start(bf16[32,240,128]{2,1,0:T(8,128)(2,1)} %pack.1), calls=%async_computation | async-start | bytes 3932160 | tf_op jit(solution)/shard_map/all_to_all | solution.py:394
  27.3 27.4 %collective-permute-start.5 = (bf16[128,1280]{1,0:T(8,128)(2,1)S(1)}, bf16[128,1280]{1,0:T(8,128)(2,1)S(1)}, u32[]{:S(2)}, u32[]{:S(2)}) collective-permute-start(bf16[128,1280]{1,0:T(8,128)(2,1)S(1)} %pad_maximum_fusion.1), channel_id=1, source_target_pairs={{79,0},{76,1},{77,2},{78,3},{11,4},{8,5},{9,6},{10,7},{87,8},{84,9... | collective-permute-start | bytes 983048 | tf_op jit(solution)/shard_map/ppermute | solution.py:38
  31.7 31.4 %collective-permute-start.4 = (bf16[128,1280]{1,0:T(8,128)(2,1)S(1)}, bf16[128,1280]{1,0:T(8,128)(2,1)S(1)}, u32[]{:S(2)}, u32[]{:S(2)}) collective-permute-start(bf16[128,1280]{1,0:T(8,128)(2,1)S(1)} %pad_maximum_fusion.1), channel_id=1, source_target_pairs={{2,0},{3,1},{0,2},{1,3},{6,4},{7,5},{4,6},{5,7},{10,8},{11,9},{8,1... | collective-permute-start | bytes 983048 | tf_op jit(solution)/shard_map/ppermute | solution.py:38
  34.1 29.0 %collective-permute-start.3 = (bf16[128,1280]{1,0:T(8,128)(2,1)S(1)}, bf16[128,1280]{1,0:T(8,128)(2,1)S(1)}, u32[]{:S(2)}, u32[]{:S(2)}) collective-permute-start(bf16[128,1280]{1,0:T(8,128)(2,1)S(1)} %pad_maximum_fusion.1), channel_id=1, source_target_pairs={{29,0},{30,1},{31,2},{28,3},{89,4},{90,5},{91,6},{88,7},{5,8},{6,9... | collective-permute-start | bytes 983048 | tf_op jit(solution)/shard_map/ppermute | solution.py:38
  63.3 8.8 %collective-permute-start.8 = (bf16[128,1280]{1,0:T(8,128)(2,1)S(1)}, bf16[128,1280]{1,0:T(8,128)(2,1)S(1)}, u32[]{:S(2)}, u32[]{:S(2)}) collective-permute-start(bf16[128,1280]{1,0:T(8,128)(2,1)S(1)} %slice.16), channel_id=1, source_target_pairs={{3,0},{0,1},{1,2},{2,3},{7,4},{4,5},{5,6},{6,7},{11,8},{8,9},{9,10... | collective-permute-start | bytes 983048 | tf_op jit(solution)/shard_map/ppermute | solution.py:38
  65.5 24.0 %collective-permute-start.11 = (bf16[384,1280]{1,0:T(8,128)(2,1)S(1)}, bf16[384,1280]{1,0:T(8,128)(2,1)S(1)}, u32[]{:S(2)}, u32[]{:S(2)}) collective-permute-start(bf16[384,1280]{1,0:T(8,128)(2,1)S(1)} %slice.17), channel_id=1, source_target_pairs={{1,0},{2,1},{3,2},{0,3},{5,4},{6,5},{7,6},{4,7},{9,8},{10,9},{11,1... | collective-permute-start | bytes 2949128 | tf_op jit(solution)/shard_map/ppermute | solution.py:38
  66.1 19.8 %collective-permute-start.7 = (bf16[256,1280]{1,0:T(8,128)(2,1)S(1)}, bf16[256,1280]{1,0:T(8,128)(2,1)S(1)}, u32[]{:S(2)}, u32[]{:S(2)}) collective-permute-start(bf16[256,1280]{1,0:T(8,128)(2,1)S(1)} %get-tuple-element.26), channel_id=1, source_target_pairs={{24,0},{25,1},{26,2},{27,3},{28,4},{29,5},{30,6},{31,7},{0,8},{1,9... | collective-permute-start | bytes 1966088 | tf_op jit(solution)/shard_map/ppermute | solution.py:38
  71.1 14.7 %collective-permute-start.10 = (bf16[256,1280]{1,0:T(8,128)(2,1)S(1)}, bf16[256,1280]{1,0:T(8,128)(2,1)S(1)}, u32[]{:S(2)}, u32[]{:S(2)}) collective-permute-start(bf16[256,1280]{1,0:T(8,128)(2,1)S(1)} %get-tuple-element.26), channel_id=1, source_target_pairs={{8,0},{9,1},{10,2},{11,3},{12,4},{13,5},{14,6},{15,7},{16,8},{17,9... | collective-permute-start | bytes 1966088 | tf_op jit(solution)/shard_map/ppermute | solution.py:38
  71.3 14.6 %collective-permute-start.6 = (bf16[256,1280]{1,0:T(8,128)(2,1)S(1)}, bf16[256,1280]{1,0:T(8,128)(2,1)S(1)}, u32[]{:S(2)}, u32[]{:S(2)}) collective-permute-start(bf16[256,1280]{1,0:T(8,128)(2,1)S(1)} %get-tuple-element.18), channel_id=1, source_target_pairs={{4,0},{5,1},{6,2},{7,3},{64,4},{65,5},{66,6},{67,7},{12,8},{13,9},... | collective-permute-start | bytes 1966088 | tf_op jit(solution)/shard_map/ppermute | solution.py:38
  72.1 17.4 %collective-permute-start.9 = (bf16[256,1280]{1,0:T(8,128)(2,1)S(1)}, bf16[256,1280]{1,0:T(8,128)(2,1)S(1)}, u32[]{:S(2)}, u32[]{:S(2)}) collective-permute-start(bf16[256,1280]{1,0:T(8,128)(2,1)S(1)} %get-tuple-element.18), channel_id=1, source_target_pairs={{68,0},{69,1},{70,2},{71,3},{0,4},{1,5},{2,6},{3,7},{76,8},{77,9},... | collective-permute-start | bytes 1966088 | tf_op jit(solution)/shard_map/ppermute | solution.py:38
  92.7 19.8 %collective-permute-start.12 = (bf16[64,32,1280]{2,1,0:T(8,128)(2,1)}, bf16[64,32,1280]{2,1,0:T(8,128)(2,1)}, u32[]{:S(2)}, u32[]{:S(2)}) collective-permute-start(bf16[64,32,1280]{2,1,0:T(8,128)(2,1)} %assemble.1), channel_id=1, source_target_pairs={{0,32},{1,33},{2,34},{3,35},{4,36},{5,37},{6,38},{7,39},{8,40},{9,... | collective-permute-start | bytes 15728648 | tf_op jit(solution)/shard_map/ppermute | solution.py:402
  104.4 1.4 copy-start
  105.8 36.7 %all-to-all-start.1 = ((f32[128,32,128]{2,1,0:T(8,128)}), f32[128,32,128]{2,1,0:T(8,128)S(1)}, u32[]{:S(2)}, u32[]{:S(2)}) async-start(f32[128,32,128]{2,1,0:T(8,128)} %copy-done), calls=%async_computation.1 | async-start | bytes 4194304 | tf_op jit(solution)/shard_map/all_to_all | solution.py:406
  142.5 0.7 copy-start.2

commit v5 on v4

--- a/solution.py
+++ b/solution.py
@@ -53,16 +53,19 @@
 assert len(SOURCES) == 64 and len(set(SOURCES)) == 64
 
 
-def gather_chips(block, tiles, early):
+def gather_chips(block, packed, early):
     level = jnp.concatenate([block] + [take_from(block, o) for o in FIRST[1:]], axis=0)
-    level, early = lax.optimization_barrier((level, early))
+    level, packed = lax.optimization_barrier((level, packed))
+    tiles = lax.all_to_all(packed, "blk", split_axis=0, concat_axis=0, tiled=True)
     level = jnp.concatenate([level] + [take_from(level, o) for o in SECOND[1:]], axis=0)
-    level, tiles = lax.optimization_barrier((level, tiles))
     parts = [level[low * ROWS : high * ROWS] for _, low, high in LAST]
     small = take_from(parts[5], LAST[5][0])
+    parts[2], small, tiles, early = lax.optimization_barrier((parts[2], small, tiles, early))
     tiles = tiles.reshape(32, 6, 40, 128).transpose(1, 0, 2, 3).reshape(6, CH, 128)
-    parts[2], small, tiles = lax.optimization_barrier((parts[2], small, tiles))
-    return [level] + [take_from(part, last[0]) for part, last in zip(parts[:5], LAST)] + [small], tiles, early
+    late = take_from(parts[2], LAST[2][0])
+    late, tiles = lax.optimization_barrier((late, tiles))
+    pieces = [take_from(parts[i], LAST[i][0]) for i in (0, 1, 3, 4)]
+    return [level] + pieces[:2] + [late] + pieces[2:] + [small], tiles, early
 
 
 def assemble_kernel(slots, *refs):
@@ -234,7 +237,7 @@
     return jnp.where((col >= 0) & (col < 8), moved, 0.0)
 
 
-def rhs_kernel(scale_ref, pixels_ref, tiles_ref, out_ref, rhs, staged, sems):
+def rhs_kernel(scale_ref, pixels_ref, tiles_ref, out_ref, rhs, staged):
     lane = lax.broadcasted_iota(jnp.int32, (1, 128), 1)
     tap_row = lax.broadcasted_iota(jnp.int32, (16, 384), 0)
     tap_lane = lax.broadcasted_iota(jnp.int32, (16, 384), 1)
@@ -284,31 +287,26 @@
         value = keep_off * cross + wide * tiles.astype(jnp.float32)
         rhs[...] = value if c == 0 else rhs[...] + value
     zeros = jnp.zeros((2, 128), jnp.float32)
-    copies = []
     for part in range(8):
         for dest in range(part * 16, part * 16 + 16):
             for a in range(3):
                 staged[dest, pl.ds(a * OWN, OWN), :] = rhs[pl.ds(dest * OWN, OWN), pl.ds(a * 128, 128)]
             staged[dest, pl.ds(30, 2), :] = zeros
         some = pl.ds(part * 16, 16)
-        copies.append(pltpu.make_async_copy(staged.at[some], out_ref.at[some], sems.at[part]))
-        copies[-1].start()
-    for copy in copies:
-        copy.wait()
+        out_ref[some] = staged[some].astype(jnp.bfloat16)
 
 
 def rhs_part(scale, pixels, tiles):
     whole = pl.BlockSpec(memory_space=pltpu.VMEM)
     return pl.pallas_call(
         rhs_kernel,
-        out_shape=jax.ShapeDtypeStruct((128, 32, 128), jnp.float32),
+        out_shape=jax.ShapeDtypeStruct((128, 32, 128), jnp.bfloat16),
         in_specs=[pl.BlockSpec(memory_space=pltpu.SMEM), pl.BlockSpec((1024, CH), lambda i: (0, 0)), pl.BlockSpec((6, CH, 128), lambda i: (0, 0, 0))],
         grid=(1,),
-        out_specs=pl.BlockSpec(memory_space=pltpu.HBM),
+        out_specs=pl.BlockSpec((128, 32, 128), lambda i: (0, 0, 0)),
         scratch_shapes=[
             pltpu.VMEM((CH, 384), jnp.float32),
             pltpu.VMEM((128, 32, 128), jnp.float32),
-            pltpu.SemaphoreType.DMA((8,)),
         ],
         compiler_params=pltpu.CompilerParams(vmem_limit_bytes=48 * 1024 * 1024),
         cost_estimate=pl.CostEstimate(flops=4_000_000_000, bytes_accessed=8_000_000, transcendentals=0),
@@ -324,7 +322,7 @@
         last = (tile * 128 + 127) // 40
         values = [jnp.zeros((32, 128), jnp.float32)] * 3
         for b in range(first, last + 1):
-            total = sent_ref[b * 4] + sent_ref[b * 4 + 1] + sent_ref[b * 4 + 2] + sent_ref[b * 4 + 3]
+            total = jnp.sum(sent_ref[pl.ds(b * 4, 4)].astype(jnp.float32), axis=0)
             start = b * 40 - tile * 128
             keep = (lane >= start) & (lane < start + 40)
             for t in range(3):
@@ -391,12 +389,11 @@
     img_scale = jnp.repeat(jnp.repeat(group_scale, 16, axis=1)[:, None, :], 32, axis=1).reshape(4, LANES)
 
     masked = jnp.where(live[:, :, None, None, None], activations, jnp.zeros_like(activations))
-    tiles = lax.all_to_all(packed, "blk", split_axis=0, concat_axis=0, tiled=True)
     offs = np.array(SOURCES, np.int32)
     src_x, src_y, src_z = (x + offs[:, 0]) % 4, (y + offs[:, 1]) % 4, (z + offs[:, 2]) % 4
     away = (src_x // 2 != x_hi).astype(jnp.int32)
     slots = (away * 32 + src_z * 8 + (src_x % 2) * 4 + src_y).astype(jnp.int32)
-    pieces, tiles, early = gather_chips(masked.reshape(ROWS, CH), tiles, (pick, order, img_scale, slots))
+    pieces, tiles, early = gather_chips(masked.reshape(ROWS, CH), packed, (pick, order, img_scale, slots))
     pick, order, img_scale, slots = early
     own = assemble(slots, pieces)
     other = lax.ppermute(own, AXES, [(d, d ^ 32) for d in range(128)])

time: 145 us -> 150 us (1.034)
  waiting for transfers between devices: 41.2 us -> 32.7 us
  local copies, waits for them, and re-layouts: 6.36 us -> 12.3 us
  other arithmetic: 3.54 us -> 9.1 us
    ppermute x12, waiting for transfers between devices: 40.1 us -> 32.7 us  [take_from(): return lax.ppermute(value, AXES, pairs)]
    concatenate x1 -> x2, other arithmetic: 0.09 us -> 3.58 us  [gather_chips(): jnp.concatenate([level] + [take_from(level, o) for o in SECOND[1:]], axis=0)]
    concatenate x0 -> x2, local copies, waits for them, and re-layouts: none -> 3.44 us  [gather_chips(): jnp.concatenate([level] + [take_from(level, o) for o in SECOND[1:]], axis=0)]
    ppermute x1, starting transfers between devices: 2.76 us -> 5.93 us  [body(): other = lax.ppermute(own, AXES, [(d, d ^ 32) for d in range(128)])]
    ppermute x12, starting transfers between devices: 32 us -> 29.6 us  [take_from(): return lax.ppermute(value, AXES, pairs)]
    reshape x1, local copies, waits for them, and re-layouts: 0.34 us -> 1.89 us  [gather_chips(): tiles.reshape(32, 6, 40, 128).transpose(1, 0, 2, 3).reshape(6, CH, 128)]
    unnamed x14 -> x10, local copies, waits for them, and re-layouts: 3.54 us -> 4.68 us
  transfers between devices with their start and end apart: 15 -> 15, of which waited for: 5 -> 5; matrix products, arithmetic and copies ran while one was open for 3% -> 11% of each run, Pallas kernels for 29% -> 28%
where the time goes in v5:
time: 150 us; the launch traced here: 149 us
  Pallas kernels  47.5 us (32%)
  starting transfers between devices  46.4 us (31%)
  waiting for transfers between devices  32.7 us (22%)
  local copies, waits for them, and re-layouts  12.3 us (8%)
  other arithmetic  9.1 us (6%)
    ppermute x12, waiting for transfers between devices, take_from(): return lax.ppermute(value, AXES, pairs)  32.7 us
    ppermute x12, starting transfers between devices, take_from(): return lax.ppermute(value, AXES, pairs)  29.6 us
    pallas_call x1, Pallas kernels, gram(): pl.pallas_call(gram_kernel, out_shape=(jax.ShapeDtypeStruct((90, 11520),...  28.9 us
    pallas_call x1, Pallas kernels, rhs_part(): pl.pallas_call(rhs_kernel, out_shape=jax.ShapeDtypeStruct((128, 32, 128),...  9.78 us
    ppermute x1, starting transfers between devices, body(): other = lax.ppermute(own, AXES, [(d, d ^ 32) for d in range(128)])  5.93 us
    all_to_all x1, starting transfers between devices, body(): lax.all_to_all(part, ('blk', 'client'), split_axis=0, concat_axis=0, tile...  5.83 us
    all_to_all x1, starting transfers between devices, gather_chips(): lax.all_to_all(packed, 'blk', split_axis=0, concat_axis=0, tiled=True)  5.07 us
    unnamed x10, local copies, waits for them, and re-layouts  4.68 us
  transfers between devices with their start and end apart: 15, of which 5 were waited for; matrix products, arithmetic and copies ran while one was open for 11% of the time, Pallas kernels for 28%

profile of v5, /device:TPU:1, one launch (start us, length us, event | category | flops | bytes accessed | tf_op | source)
XLA Modules:
  0.0 148.9 jit_solution(15845932085362924901)
XLA Ops:
  2.4 3.5 %collective-permute-start.2 = (bf16[32,1280]{1,0:T(8,128)(2,1)S(1)}, bf16[32,1280]{1,0:T(8,128)(2,1)S(1)}, u32[]{:S(2)}, u32[]{:S(2)}) collective-permute-start(bf16[32,1280]{1,0:T(8,128)(2,1)S(1)} %bitcast.16), channel_id=1, source_target_pairs={{92,0},{93,1},{94,2},{95,3},{24,4},{25,5},{26,6},{27,7},{68,8},{69... | collective-permute-start | bytes 245768 | tf_op jit(solution)/shard_map/ppermute | solution.py:38
  5.9 5.5 %collective-permute-start.1 = (bf16[32,1280]{1,0:T(8,128)(2,1)S(1)}, bf16[32,1280]{1,0:T(8,128)(2,1)S(1)}, u32[]{:S(2)}, u32[]{:S(2)}) collective-permute-start(bf16[32,1280]{1,0:T(8,128)(2,1)S(1)} %bitcast.17), channel_id=1, source_target_pairs={{80,0},{81,1},{82,2},{83,3},{84,4},{85,5},{86,6},{87,7},{88,8},{89... | collective-permute-start | bytes 245768 | tf_op jit(solution)/shard_map/ppermute | solution.py:38
  11.3 1.6 %collective-permute-start = (bf16[32,1280]{1,0:T(8,128)(2,1)S(1)}, bf16[32,1280]{1,0:T(8,128)(2,1)S(1)}, u32[]{:S(2)}, u32[]{:S(2)}) collective-permute-start(bf16[32,1280]{1,0:T(8,128)(2,1)S(1)} %bitcast.18), channel_id=1, source_target_pairs={{12,0},{13,1},{14,2},{15,3},{72,4},{73,5},{74,6},{75,7},{20,8},{21... | collective-permute-start | bytes 245768 | tf_op jit(solution)/shard_map/ppermute | solution.py:38
  16.7 3.5 %pack.1 = bf16[32,240,128]{2,1,0:T(8,128)(2,1)} custom-call(bf16[2,360,1280]{2,1,0:T(8,128)(2,1)S(1)} %copy-done, bf16[360,360]{1,0:T(8,128)(2,1)S(1)} %fusion.6.order_ref), custom_call_target="tpu_custom_call" | custom-call | flops 1000000000 | bytes 6000000 | tf_op jit(solution)/shard_map/pack/pallas_call | solution.py:211
  21.0 5.1 %all-to-all-start = ((bf16[32,240,128]{2,1,0:T(8,128)(2,1)}), bf16[32,240,128]{2,1,0:T(8,128)(2,1)S(1)}, u32[]{:S(2)}, u32[]{:S(2)}) async-start(bf16[32,240,128]{2,1,0:T(8,128)(2,1)} %pack.1), calls=%async_computation | async-start | bytes 3932160 | tf_op jit(solution)/shard_map/all_to_all | solution.py:59
  27.7 3.6 %collective-permute-start.3 = (bf16[128,1280]{1,0:T(8,128)(2,1)}, bf16[128,1280]{1,0:T(8,128)(2,1)}, u32[]{:S(2)}, u32[]{:S(2)}) collective-permute-start(bf16[128,1280]{1,0:T(8,128)(2,1)} %pad_maximum_fusion.2), channel_id=1, source_target_pairs={{29,0},{30,1},{31,2},{28,3},{89,4},{90,5},{91,6},{88,7},{5,8},{6,9... | collective-permute-start | bytes 983048 | tf_op jit(solution)/shard_map/ppermute | solution.py:38
  33.6 2.7 %collective-permute-start.5 = (bf16[128,1280]{1,0:T(8,128)(2,1)}, bf16[128,1280]{1,0:T(8,128)(2,1)S(1)}, u32[]{:S(2)}, u32[]{:S(2)}) collective-permute-start(bf16[128,1280]{1,0:T(8,128)(2,1)} %pad_maximum_fusion.2), channel_id=1, source_target_pairs={{2,0},{3,1},{0,2},{1,3},{6,4},{7,5},{4,6},{5,7},{10,8},{11,9},{8,1... | collective-permute-start | bytes 983048 | tf_op jit(solution)/shard_map/ppermute | solution.py:38
  36.3 1.8 %constant_dynamic-update-slice_fusion.1 = bf16[256,1280]{1,0:T(8,128)(2,1)} fusion(bf16[128,1280]{1,0:T(8,128)(2,1)} %pad_maximum_fusion.2), kind=kLoop, calls=%fused_computation.23 | loop fusion | bytes 655360
  38.1 22.0 %collective-permute-done.3 = bf16[128,1280]{1,0:T(8,128)(2,1)} collective-permute-done((bf16[128,1280]{1,0:T(8,128)(2,1)}, bf16[128,1280]{1,0:T(8,128)(2,1)}, u32[]{:S(2)}, u32[]{:S(2)}) %collective-permute-start.3) | collective-permute-done | bytes 327712 | tf_op jit(solution)/shard_map/ppermute | solution.py:38
  60.0 1.7 %constant_dynamic-update-slice_fusion = bf16[256,1280]{1,0:T(8,128)(2,1)} fusion(bf16[256,1280]{1,0:T(8,128)(2,1)} %constant_dynamic-update-slice_fusion.1, bf16[128,1280]{1,0:T(8,128)(2,1)} %collective-permute-done.3), kind=kLoop, calls=%fused_computation.22 | loop fusion | bytes 655360 | tf_op jit(solution)/shard_map/concatenate | solution.py:60
  61.8 8.8 %collective-permute-start.4 = (bf16[128,1280]{1,0:T(8,128)(2,1)}, bf16[128,1280]{1,0:T(8,128)(2,1)S(1)}, u32[]{:S(2)}, u32[]{:S(2)}) collective-permute-start(bf16[128,1280]{1,0:T(8,128)(2,1)} %collective-permute-done.3), channel_id=1, source_target_pairs={{3,0},{0,1},{1,2},{2,3},{7,4},{4,5},{5,6},{6,7},{11,8},{8,9},{9,10... | collective-permute-start | bytes 983048 | tf_op jit(solution)/shard_map/ppermute | solution.py:38
  70.5 2.2 %pad_maximum_fusion.1 = bf16[384,1280]{1,0:T(8,128)(2,1)} fusion(bf16[128,1280]{1,0:T(8,128)(2,1)S(1)} %collective-permute-done.5, bf16[128,1280]{1,0:T(8,128)(2,1)} %collective-permute-done.3, bf16[128,1280]{1,0:T(8,128)(2,1)} %pad_maximum_fusion.2), kind=kLoop, calls=%fused_computation.2 | loop fusion | flops 2949120 | bytes 1966080 | tf_op jit(solution)/shard_map/concatenate | solution.py:60
  76.4 1.7 %constant_dynamic-update-slice_fusion.2 = bf16[256,1280]{1,0:T(8,128)(2,1)} fusion(bf16[256,1280]{1,0:T(8,128)(2,1)} %constant_dynamic-update-slice_fusion.3, bf16[128,1280]{1,0:T(8,128)(2,1)} %collective-permute-done.6), kind=kLoop, calls=%fused_computation.24 | loop fusion | bytes 655360 | tf_op jit(solution)/shard_map/concatenate | solution.py:60
  78.1 1.6 %collective-permute-start.10 = (bf16[256,1280]{1,0:T(8,128)(2,1)}, bf16[256,1280]{1,0:T(8,128)(2,1)S(1)}, u32[]{:S(2)}, u32[]{:S(2)}) collective-permute-start(bf16[256,1280]{1,0:T(8,128)(2,1)} %constant_dynamic-update-slice_fusion.2), channel_id=1, source_target_pairs={{8,0},{9,1},{10,2},{11,3},{12,4},{13,5},{14,6},{15,7},{16,8},{17,9... | collective-permute-start | bytes 1966088 | tf_op jit(solution)/shard_map/ppermute | solution.py:38
  81.0 1.9 %copy.9 = bf16[32,6,40,128]{3,2,0,1:T(8,128)(2,1)S(1)} copy(bf16[32,6,40,128]{3,2,1,0:T(8,128)(2,1)} %bitcast.15) | data formatting | bytes 3932160 | tf_op jit(solution)/shard_map/reshape | solution.py:64
  82.9 3.5 %collective-permute-done.9.refs_3_ = bf16[256,1280]{1,0:T(8,128)(2,1)S(1)} collective-permute-done((bf16[256,1280]{1,0:T(8,128)(2,1)}, bf16[256,1280]{1,0:T(8,128)(2,1)S(1)}, u32[]{:S(2)}, u32[]{:S(2)}) %collective-permute-start.9) | collective-permute-done | bytes 655392 | tf_op jit(solution)/shard_map/ppermute | solution.py:38
  86.5 2.8 %collective-permute-done.10.refs_4_ = bf16[256,1280]{1,0:T(8,128)(2,1)S(1)} collective-permute-done((bf16[256,1280]{1,0:T(8,128)(2,1)}, bf16[256,1280]{1,0:T(8,128)(2,1)S(1)}, u32[]{:S(2)}, u32[]{:S(2)}) %collective-permute-start.10) | collective-permute-done | bytes 655392 | tf_op jit(solution)/shard_map/ppermute | solution.py:38
  89.3 3.0 %collective-permute-done.8.refs_2_ = bf16[256,1280]{1,0:T(8,128)(2,1)S(1)} collective-permute-done((bf16[256,1280]{1,0:T(8,128)(2,1)}, bf16[256,1280]{1,0:T(8,128)(2,1)S(1)}, u32[]{:S(2)}, u32[]{:S(2)}) %collective-permute-start.8) | collective-permute-done | bytes 655392 | tf_op jit(solution)/shard_map/ppermute | solution.py:38
  92.3 3.8 %assemble.1 = bf16[64,32,1280]{2,1,0:T(8,128)(2,1)} custom-call(s32[64]{0:T(128)S(1)} %fusion.22.slots, bf16[512,1280]{1,0:T(8,128)(2,1)S(1)} %pad_maximum_fusion.refs_0_, bf16[256,1280]{1,0:T(8,128)(2,1)} %collective-permute-done.7.refs_1_, bf16[256,1280]{1,0:T(8,128)(2,1)S(1)} %collective-permute-done.8.refs_2_, ...), custom_call_target="tpu_custom_call" | custom-call | tf_op jit(solution)/shard_map/assemble/pallas_call | solution.py:81
  96.1 5.9 %collective-permute-start.12 = (bf16[64,32,1280]{2,1,0:T(8,128)(2,1)}, bf16[64,32,1280]{2,1,0:T(8,128)(2,1)}, u32[]{:S(2)}, u32[]{:S(2)}) collective-permute-start(bf16[64,32,1280]{2,1,0:T(8,128)(2,1)} %assemble.1), channel_id=1, source_target_pairs={{0,32},{1,33},{2,34},{3,35},{4,36},{5,37},{6,38},{7,39},{8,40},{9,... | collective-permute-start | bytes 15728648 | tf_op jit(solution)/shard_map/ppermute | solution.py:399
  102.1 9.8 %rhs_part.1 = bf16[128,32,128]{2,1,0:T(8,128)(2,1)} custom-call(f32[2]{0:T(128)S(1)} %dynamic_slice.7.scale_ref, bf16[2048,1280]{1,0:T(8,128)(2,1)} %bitcast.10.own_hbm.pixels_ref, bf16[6,1280,128]{2,1,0:T(8,128)(2,1)S(1)} %bitcast.14), custom_call_target="tpu_custom_call" | custom-call | flops 4000000000 | bytes 8000000 | tf_op jit(solution)/shard_map/rhs_part/pallas_call | solution.py:301
  111.9 5.8 %all-to-all-start.1 = ((bf16[128,32,128]{2,1,0:T(8,128)(2,1)}), bf16[128,32,128]{2,1,0:T(8,128)(2,1)S(1)}, u32[]{:S(2)}, u32[]{:S(2)}) async-start(bf16[128,32,128]{2,1,0:T(8,128)(2,1)} %rhs_part.1), calls=%async_computation.1 | async-start | bytes 2097152 | tf_op jit(solution)/shard_map/all_to_all | solution.py:403
  117.7 28.9 %gram.1 = (f32[90,11520]{1,0:T(8,128)}, f32[8,128]{1,0:T(8,128)}) custom-call(s32[1]{0:T(128)} %bitcast.first_ref, bf16[2048,1280]{1,0:T(8,128)(2,1)} %bitcast.10.own_hbm.pixels_ref, bf16[2048,1280]{1,0:T(8,128)(2,1)} %bitcast.11.other_hbm, bf16[16,1280]{1,0:T(8,128)(2,1)} %fusion.11.pick_ref, bf16[96,144]{1,0:T(8,128)(2,1)} %fusion.9.order_ref, ...), custom_call_target="tpu_custom_call" | custom-call | flops 20000000000 | bytes 20000000 | tf_op jit(solution)/shard_map/gram/pallas_call | solution.py:169
  147.3 1.6 %finish.1 = f32[90,1280]{1,0:T(8,128)} custom-call(bf16[128,32,128]{2,1,0:T(8,128)(2,1)S(1)} %all-to-all-done.1.sent_ref, f32[8,128]{1,0:T(8,128)S(1)} %copy-done.1), custom_call_target="tpu_custom_call" | custom-call | tf_op jit(solution)/shard_map/finish/pallas_call | solution.py:351
  (57 shorter events, 15.9 us)
Async XLA Ops:
  2.4 17.8 %collective-permute-start.2 = (bf16[32,1280]{1,0:T(8,128)(2,1)S(1)}, bf16[32,1280]{1,0:T(8,128)(2,1)S(1)}, u32[]{:S(2)}, u32[]{:S(2)}) collective-permute-start(bf16[32,1280]{1,0:T(8,128)(2,1)S(1)} %bitcast.16), channel_id=1, source_target_pairs={{92,0},{93,1},{94,2},{95,3},{24,4},{25,5},{26,6},{27,7},{68,8},{69... | collective-permute-start | bytes 245768 | tf_op jit(solution)/shard_map/ppermute | solution.py:38
  5.9 14.4 %collective-permute-start.1 = (bf16[32,1280]{1,0:T(8,128)(2,1)S(1)}, bf16[32,1280]{1,0:T(8,128)(2,1)S(1)}, u32[]{:S(2)}, u32[]{:S(2)}) collective-permute-start(bf16[32,1280]{1,0:T(8,128)(2,1)S(1)} %bitcast.17), channel_id=1, source_target_pairs={{80,0},{81,1},{82,2},{83,3},{84,4},{85,5},{86,6},{87,7},{88,8},{89... | collective-permute-start | bytes 245768 | tf_op jit(solution)/shard_map/ppermute | solution.py:38
  11.3 8.9 %collective-permute-start = (bf16[32,1280]{1,0:T(8,128)(2,1)S(1)}, bf16[32,1280]{1,0:T(8,128)(2,1)S(1)}, u32[]{:S(2)}, u32[]{:S(2)}) collective-permute-start(bf16[32,1280]{1,0:T(8,128)(2,1)S(1)} %bitcast.18), channel_id=1, source_target_pairs={{12,0},{13,1},{14,2},{15,3},{72,4},{73,5},{74,6},{75,7},{20,8},{21... | collective-permute-start | bytes 245768 | tf_op jit(solution)/shard_map/ppermute | solution.py:38
  15.2 1.5 %copy-start = (bf16[2,360,1280]{2,1,0:T(8,128)(2,1)S(1)}, bf16[2,360,1280]{2,1,0:T(8,128)(2,1)}, u32[]{:S(2)}) copy-start(bf16[2,360,1280]{2,1,0:T(8,128)(2,1)} %weights_ref.1) | copy-start | bytes 5529604
  21.0 53.9 %all-to-all-start = ((bf16[32,240,128]{2,1,0:T(8,128)(2,1)}), bf16[32,240,128]{2,1,0:T(8,128)(2,1)S(1)}, u32[]{:S(2)}, u32[]{:S(2)}) async-start(bf16[32,240,128]{2,1,0:T(8,128)(2,1)} %pack.1), calls=%async_computation | async-start | bytes 3932160 | tf_op jit(solution)/shard_map/all_to_all | solution.py:59
  27.7 32.4 %collective-permute-start.3 = (bf16[128,1280]{1,0:T(8,128)(2,1)}, bf16[128,1280]{1,0:T(8,128)(2,1)}, u32[]{:S(2)}, u32[]{:S(2)}) collective-permute-start(bf16[128,1280]{1,0:T(8,128)(2,1)} %pad_maximum_fusion.2), channel_id=1, source_target_pairs={{29,0},{30,1},{31,2},{28,3},{89,4},{90,5},{91,6},{88,7},{5,8},{6,9... | collective-permute-start | bytes 983048 | tf_op jit(solution)/shard_map/ppermute | solution.py:38
  32.7 43.6 %collective-permute-start.6 = (bf16[128,1280]{1,0:T(8,128)(2,1)}, bf16[128,1280]{1,0:T(8,128)(2,1)}, u32[]{:S(2)}, u32[]{:S(2)}) collective-permute-start(bf16[128,1280]{1,0:T(8,128)(2,1)} %pad_maximum_fusion.2), channel_id=1, source_target_pairs={{79,0},{76,1},{77,2},{78,3},{11,4},{8,5},{9,6},{10,7},{87,8},{84,9... | collective-permute-start | bytes 983048 | tf_op jit(solution)/shard_map/ppermute | solution.py:38
  33.6 36.9 %collective-permute-start.5 = (bf16[128,1280]{1,0:T(8,128)(2,1)}, bf16[128,1280]{1,0:T(8,128)(2,1)S(1)}, u32[]{:S(2)}, u32[]{:S(2)}) collective-permute-start(bf16[128,1280]{1,0:T(8,128)(2,1)} %pad_maximum_fusion.2), channel_id=1, source_target_pairs={{2,0},{3,1},{0,2},{1,3},{6,4},{7,5},{4,6},{5,7},{10,8},{11,9},{8,1... | collective-permute-start | bytes 983048 | tf_op jit(solution)/shard_map/ppermute | solution.py:38
  61.8 24.7 %collective-permute-start.7 = (bf16[256,1280]{1,0:T(8,128)(2,1)}, bf16[256,1280]{1,0:T(8,128)(2,1)}, u32[]{:S(2)}, u32[]{:S(2)}) collective-permute-start(bf16[256,1280]{1,0:T(8,128)(2,1)} %constant_dynamic-update-slice_fusion), channel_id=1, source_target_pairs={{4,0},{5,1},{6,2},{7,3},{64,4},{65,5},{66,6},{67,7},{12,8},{13,9},... | collective-permute-start | bytes 1966088 | tf_op jit(solution)/shard_map/ppermute | solution.py:38
  61.8 13.1 %collective-permute-start.4 = (bf16[128,1280]{1,0:T(8,128)(2,1)}, bf16[128,1280]{1,0:T(8,128)(2,1)S(1)}, u32[]{:S(2)}, u32[]{:S(2)}) collective-permute-start(bf16[128,1280]{1,0:T(8,128)(2,1)} %collective-permute-done.3), channel_id=1, source_target_pairs={{3,0},{0,1},{1,2},{2,3},{7,4},{4,5},{5,6},{6,7},{11,8},{8,9},{9,10... | collective-permute-start | bytes 983048 | tf_op jit(solution)/shard_map/ppermute | solution.py:38
  70.5 3.0 %copy-start.3 = (bf16[128,1280]{1,0:T(8,128)(2,1)}, bf16[128,1280]{1,0:T(8,128)(2,1)S(1)}, u32[]{:S(2)}) copy-start(bf16[128,1280]{1,0:T(8,128)(2,1)S(1)} %collective-permute-done.5) | copy-start | bytes 983044
  72.8 19.5 %collective-permute-start.11 = (bf16[384,1280]{1,0:T(8,128)(2,1)}, bf16[384,1280]{1,0:T(8,128)(2,1)S(1)}, u32[]{:S(2)}, u32[]{:S(2)}) collective-permute-start(bf16[384,1280]{1,0:T(8,128)(2,1)} %pad_maximum_fusion.1), channel_id=1, source_target_pairs={{1,0},{2,1},{3,2},{0,3},{5,4},{6,5},{7,6},{4,7},{9,8},{10,9},{11,1... | collective-permute-start | bytes 2949128 | tf_op jit(solution)/shard_map/ppermute | solution.py:38
  74.9 6.2 %copy-start.2 = (bf16[32,240,128]{2,1,0:T(8,128)(2,1)}, bf16[32,240,128]{2,1,0:T(8,128)(2,1)S(1)}, u32[]{:S(2)}) copy-start(bf16[32,240,128]{2,1,0:T(8,128)(2,1)S(1)} %all-to-all-done) | copy-start | bytes 5898244
  74.9 11.6 %collective-permute-start.9 = (bf16[256,1280]{1,0:T(8,128)(2,1)}, bf16[256,1280]{1,0:T(8,128)(2,1)S(1)}, u32[]{:S(2)}, u32[]{:S(2)}) collective-permute-start(bf16[256,1280]{1,0:T(8,128)(2,1)} %constant_dynamic-update-slice_fusion), channel_id=1, source_target_pairs={{68,0},{69,1},{70,2},{71,3},{0,4},{1,5},{2,6},{3,7},{76,8},{77,9},... | collective-permute-start | bytes 1966088 | tf_op jit(solution)/shard_map/ppermute | solution.py:38
  78.1 11.2 %collective-permute-start.10 = (bf16[256,1280]{1,0:T(8,128)(2,1)}, bf16[256,1280]{1,0:T(8,128)(2,1)S(1)}, u32[]{:S(2)}, u32[]{:S(2)}) collective-permute-start(bf16[256,1280]{1,0:T(8,128)(2,1)} %constant_dynamic-update-slice_fusion.2), channel_id=1, source_target_pairs={{8,0},{9,1},{10,2},{11,3},{12,4},{13,5},{14,6},{15,7},{16,8},{17,9... | collective-permute-start | bytes 1966088 | tf_op jit(solution)/shard_map/ppermute | solution.py:38
  79.7 12.6 %collective-permute-start.8 = (bf16[256,1280]{1,0:T(8,128)(2,1)}, bf16[256,1280]{1,0:T(8,128)(2,1)S(1)}, u32[]{:S(2)}, u32[]{:S(2)}) collective-permute-start(bf16[256,1280]{1,0:T(8,128)(2,1)} %constant_dynamic-update-slice_fusion.2), channel_id=1, source_target_pairs={{24,0},{25,1},{26,2},{27,3},{28,4},{29,5},{30,6},{31,7},{0,8},{1,9... | collective-permute-start | bytes 1966088 | tf_op jit(solution)/shard_map/ppermute | solution.py:38
  96.1 21.6 %collective-permute-start.12 = (bf16[64,32,1280]{2,1,0:T(8,128)(2,1)}, bf16[64,32,1280]{2,1,0:T(8,128)(2,1)}, u32[]{:S(2)}, u32[]{:S(2)}) collective-permute-start(bf16[64,32,1280]{2,1,0:T(8,128)(2,1)} %assemble.1), channel_id=1, source_target_pairs={{0,32},{1,33},{2,34},{3,35},{4,36},{5,37},{6,38},{7,39},{8,40},{9,... | collective-permute-start | bytes 15728648 | tf_op jit(solution)/shard_map/ppermute | solution.py:399
  111.9 34.8 %all-to-all-start.1 = ((bf16[128,32,128]{2,1,0:T(8,128)(2,1)}), bf16[128,32,128]{2,1,0:T(8,128)(2,1)S(1)}, u32[]{:S(2)}, u32[]{:S(2)}) async-start(bf16[128,32,128]{2,1,0:T(8,128)(2,1)} %rhs_part.1), calls=%async_computation.1 | async-start | bytes 2097152 | tf_op jit(solution)/shard_map/all_to_all | solution.py:403
  146.6 0.7 copy-start.1

commit v6 on v5

--- a/solution.py
+++ b/solution.py
@@ -54,18 +54,15 @@
 
 
 def gather_chips(block, packed, early):
+    tiles = lax.all_to_all(packed, "blk", split_axis=0, concat_axis=0, tiled=True)
     level = jnp.concatenate([block] + [take_from(block, o) for o in FIRST[1:]], axis=0)
-    level, packed = lax.optimization_barrier((level, packed))
-    tiles = lax.all_to_all(packed, "blk", split_axis=0, concat_axis=0, tiled=True)
     level = jnp.concatenate([level] + [take_from(level, o) for o in SECOND[1:]], axis=0)
+    level, tiles = lax.optimization_barrier((level, tiles))
     parts = [level[low * ROWS : high * ROWS] for _, low, high in LAST]
     small = take_from(parts[5], LAST[5][0])
+    tiles = tiles.reshape(32, 6, 40, 128).transpose(1, 0, 2, 3).reshape(6, CH, 128)
     parts[2], small, tiles, early = lax.optimization_barrier((parts[2], small, tiles, early))
-    tiles = tiles.reshape(32, 6, 40, 128).transpose(1, 0, 2, 3).reshape(6, CH, 128)
-    late = take_from(parts[2], LAST[2][0])
-    late, tiles = lax.optimization_barrier((late, tiles))
-    pieces = [take_from(parts[i], LAST[i][0]) for i in (0, 1, 3, 4)]
-    return [level] + pieces[:2] + [late] + pieces[2:] + [small], tiles, early
+    return [level] + [take_from(part, last[0]) for part, last in zip(parts[:5], LAST)] + [small], tiles, early
 
 
 def assemble_kernel(slots, *refs):
@@ -123,13 +120,6 @@
                 patch, 1 - t // 3, 1 - t % 3
             ).astype(jnp.bfloat16)
 
-    @pl.loop(0, 5)
-    def _(n):
-        lanes = pl.ds(pl.multiple_of(n * 256, 256), 256)
-        total = jnp.dot(left[:, pl.ds(0, 2048)], own_ref[:, lanes], preferred_element_type=jnp.float32)
-        total += jnp.dot(left[:, pl.ds(2048, 2048)], other_ref[:, lanes], preferred_element_type=jnp.float32)
-        acc[:, lanes] = total
-
     first = first_ref[0]
     lane = lax.broadcasted_iota(jnp.int32, (MPAD, 128), 1)
     row = lax.broadcasted_iota(jnp.int32, (MPAD, 128), 0)
@@ -143,9 +133,14 @@
             result = moved if result is None else jnp.where(spot % 3 == k, moved, result)
         return result
 
-    @pl.loop(0, 10)
-    def _(block):
-        lanes = pl.ds(pl.multiple_of(block * 128, 128), 128)
+    def multiply(n):
+        lanes = pl.ds(n * 256, 256)
+        total = jnp.dot(left[:, pl.ds(0, 2048)], own_ref[:, lanes], preferred_element_type=jnp.float32)
+        total += jnp.dot(left[:, pl.ds(2048, 2048)], other_ref[:, lanes], preferred_element_type=jnp.float32)
+        acc[:, lanes] = total
+
+    def interleave(block):
+        lanes = pl.ds(block * 128, 128)
         inner = [
             [weave([acc[pl.ds((3 * a + b) * MPAD, MPAD), lanes] for a in range(3)], part) for part in range(3)]
             for b in range(3)
@@ -154,9 +149,20 @@
             value = weave([inner[b][tile // 3] for b in range(3)], tile % 3)
             base = block * 1152 + tile * 128
             value = jnp.where(row + first == lane + base, value, keep_off * value)
-            staged[:, pl.ds(pl.multiple_of(base, 128), 128)] = value[:90]
-        wide = pl.ds(pl.multiple_of(block * 1152, 128), 1152)
+            staged[:, pl.ds(base, 128)] = value[:90]
+
+    def send(block):
+        wide = pl.ds(block * 1152, 1152)
         pltpu.make_async_copy(staged.at[:, wide], out_ref.at[:, wide], sems.at[block]).start()
+
+    multiply(0)
+    for n in range(5):
+        if n < 4:
+            multiply(n + 1)
+        interleave(2 * n)
+        interleave(2 * n + 1)
+        send(2 * n)
+        send(2 * n + 1)
 
     for block in range(10):
         wide = pl.ds(block * 1152, 1152)

time: 150 us -> 140 us (0.933)
  starting transfers between devices: 46.4 us -> 41.8 us
  Pallas kernels: 47.5 us -> 43.6 us
  local copies, waits for them, and re-layouts: 12.3 us -> 9.98 us
    concatenate x2 -> x0, other arithmetic: 3.58 us -> none  [gather_chips(): jnp.concatenate([level] + [take_from(level, o) for o in SECOND[1:]], axis=0)]
    concatenate x2 -> x1, local copies, waits for them, and re-layouts: 3.44 us -> 0.02 us  [gather_chips(): jnp.concatenate([level] + [take_from(level, o) for o in SECOND[1:]], axis=0)]
    ppermute x12, starting transfers between devices: 29.6 us -> 26.7 us  [take_from(): return lax.ppermute(value, AXES, pairs)]
    pallas_call x1, Pallas kernels: 28.9 us -> 26.6 us  [gram(): pl.pallas_call(gram_kernel, out_shape=(jax.ShapeDtypeStruct((90, 11520),...]
    unnamed x10 -> x14, local copies, waits for them, and re-layouts: 4.68 us -> 4.13 us
  transfers between devices with their start and end apart: 15 -> 15, of which waited for: 5 -> 7; matrix products, arithmetic and copies ran while one was open for 11% -> 10% of each run, Pallas kernels for 28% -> 28%
where the time goes in v6:
time: 140 us; the launch traced here: 139 us
  Pallas kernels  43.6 us (31%)
  starting transfers between devices  41.8 us (30%)
  waiting for transfers between devices  33.8 us (24%)
  local copies, waits for them, and re-layouts  9.98 us (7%)
  other arithmetic  9.2 us (7%)
    ppermute x12, waiting for transfers between devices, take_from(): return lax.ppermute(value, AXES, pairs)  33.8 us
    ppermute x12, starting transfers between devices, take_from(): return lax.ppermute(value, AXES, pairs)  26.7 us
    pallas_call x1, Pallas kernels, gram(): pl.pallas_call(gram_kernel, out_shape=(jax.ShapeDtypeStruct((90, 11520),...  26.6 us
    pallas_call x1, Pallas kernels, rhs_part(): pl.pallas_call(rhs_kernel, out_shape=jax.ShapeDtypeStruct((128, 32, 128),...  8.75 us
    ppermute x1, starting transfers between devices, body(): other = lax.ppermute(own, AXES, [(d, d ^ 32) for d in range(128)])  5.62 us
    all_to_all x1, starting transfers between devices, gather_chips(): lax.all_to_all(packed, 'blk', split_axis=0, concat_axis=0, tiled=True)  5.06 us
    all_to_all x1, starting transfers between devices, body(): lax.all_to_all(part, ('blk', 'client'), split_axis=0, concat_axis=0, tile...  4.41 us
    unnamed x14, local copies, waits for them, and re-layouts  4.13 us
  transfers between devices with their start and end apart: 15, of which 7 were waited for; matrix products, arithmetic and copies ran while one was open for 10% of the time, Pallas kernels for 28%

profile of v6, /device:TPU:1, one launch (start us, length us, event | category | flops | bytes accessed | tf_op | source)
XLA Modules:
  0.0 139.4 jit_solution(9991943413083916314)
XLA Ops:
  2.4 3.5 %collective-permute-start.2 = (bf16[32,1280]{1,0:T(8,128)(2,1)S(1)}, bf16[32,1280]{1,0:T(8,128)(2,1)S(1)}, u32[]{:S(2)}, u32[]{:S(2)}) collective-permute-start(bf16[32,1280]{1,0:T(8,128)(2,1)S(1)} %bitcast.16), channel_id=1, source_target_pairs={{92,0},{93,1},{94,2},{95,3},{24,4},{25,5},{26,6},{27,7},{68,8},{69... | collective-permute-start | bytes 245768 | tf_op jit(solution)/shard_map/ppermute | solution.py:38
  5.9 5.5 %collective-permute-start.1 = (bf16[32,1280]{1,0:T(8,128)(2,1)S(1)}, bf16[32,1280]{1,0:T(8,128)(2,1)S(1)}, u32[]{:S(2)}, u32[]{:S(2)}) collective-permute-start(bf16[32,1280]{1,0:T(8,128)(2,1)S(1)} %bitcast.17), channel_id=1, source_target_pairs={{80,0},{81,1},{82,2},{83,3},{84,4},{85,5},{86,6},{87,7},{88,8},{89... | collective-permute-start | bytes 245768 | tf_op jit(solution)/shard_map/ppermute | solution.py:38
  11.3 1.6 %collective-permute-start = (bf16[32,1280]{1,0:T(8,128)(2,1)S(1)}, bf16[32,1280]{1,0:T(8,128)(2,1)}, u32[]{:S(2)}, u32[]{:S(2)}) collective-permute-start(bf16[32,1280]{1,0:T(8,128)(2,1)S(1)} %bitcast.18), channel_id=1, source_target_pairs={{12,0},{13,1},{14,2},{15,3},{72,4},{73,5},{74,6},{75,7},{20,8},{21... | collective-permute-start | bytes 245768 | tf_op jit(solution)/shard_map/ppermute | solution.py:38
  13.7 1.5 %copy-done = bf16[2,360,1280]{2,1,0:T(8,128)(2,1)S(1)} copy-done((bf16[2,360,1280]{2,1,0:T(8,128)(2,1)S(1)}, bf16[2,360,1280]{2,1,0:T(8,128)(2,1)}, u32[]{:S(2)}) %copy-start) | copy-done | bytes 1843224
  15.2 3.5 %pack.1 = bf16[32,240,128]{2,1,0:T(8,128)(2,1)} custom-call(bf16[2,360,1280]{2,1,0:T(8,128)(2,1)S(1)} %copy-done, bf16[360,360]{1,0:T(8,128)(2,1)S(1)} %fusion.6.order_ref), custom_call_target="tpu_custom_call" | custom-call | flops 1000000000 | bytes 6000000 | tf_op jit(solution)/shard_map/pack/pallas_call | solution.py:217
  18.7 5.1 %all-to-all-start = ((bf16[32,240,128]{2,1,0:T(8,128)(2,1)}), bf16[32,240,128]{2,1,0:T(8,128)(2,1)S(1)}, u32[]{:S(2)}, u32[]{:S(2)}) async-start(bf16[32,240,128]{2,1,0:T(8,128)(2,1)} %pack.1), calls=%async_computation | async-start | bytes 3932160 | tf_op jit(solution)/shard_map/all_to_all | solution.py:57
  26.2 1.3 fusion.11.pick_ref
  28.2 1.4 %fusion.9.order_ref = bf16[96,144]{1,0:T(8,128)(2,1)} fusion(s32[144]{0:T(256)S(1)} %get-tuple-element.34, s32[144]{0:T(256)S(1)} %get-tuple-element.43, s32[96]{0:T(128)} %get-tuple-element.41, s32[96]{0:T(128)S(1)} %get-tuple-element.45, s32[144]{0:T(256)S(1)} %get-tuple-element.35, s32[144]{0:T(256)S(1)} %get-tuple-element.42, s32[96]{0:T(128)} %get-tuple-element.40, ...), kind=kLoop, calls=%fused_computation.15 | loop fusion | flops 110592 | bytes 31968 | tf_op jit(solution)/shard_map/convert_element_type | solution.py:392
  31.9 1.5 %broadcast_in_dim.26.scale_ref = f32[4,1024]{1,0:T(4,128)} reshape(f32[4,32,32]{2,1,0:T(8,128)} %broadcast_in_dim.25) | data formatting | bytes 32768 | tf_op jit(solution)/shard_map/broadcast_in_dim | solution.py:395
  34.3 4.4 %collective-permute-start.5 = (bf16[128,1280]{1,0:T(8,128)(2,1)S(1)}, bf16[128,1280]{1,0:T(8,128)(2,1)S(1)}, u32[]{:S(2)}, u32[]{:S(2)}) collective-permute-start(bf16[128,1280]{1,0:T(8,128)(2,1)S(1)} %pad_maximum_fusion), channel_id=1, source_target_pairs={{79,0},{76,1},{77,2},{78,3},{11,4},{8,5},{9,6},{10,7},{87,8},{84,9... | collective-permute-start | bytes 983048 | tf_op jit(solution)/shard_map/ppermute | solution.py:38
  38.7 2.4 %collective-permute-start.4 = (bf16[128,1280]{1,0:T(8,128)(2,1)S(1)}, bf16[128,1280]{1,0:T(8,128)(2,1)S(1)}, u32[]{:S(2)}, u32[]{:S(2)}) collective-permute-start(bf16[128,1280]{1,0:T(8,128)(2,1)S(1)} %pad_maximum_fusion), channel_id=1, source_target_pairs={{2,0},{3,1},{0,2},{1,3},{6,4},{7,5},{4,6},{5,7},{10,8},{11,9},{8,1... | collective-permute-start | bytes 983048 | tf_op jit(solution)/shard_map/ppermute | solution.py:38
  43.1 16.7 %collective-permute-done.3 = bf16[128,1280]{1,0:T(8,128)(2,1)S(1)} collective-permute-done((bf16[128,1280]{1,0:T(8,128)(2,1)S(1)}, bf16[128,1280]{1,0:T(8,128)(2,1)S(1)}, u32[]{:S(2)}, u32[]{:S(2)}) %collective-permute-start.3) | collective-permute-done | bytes 327712 | tf_op jit(solution)/shard_map/ppermute | solution.py:38
  59.8 3.2 %collective-permute-done.4 = bf16[128,1280]{1,0:T(8,128)(2,1)S(1)} collective-permute-done((bf16[128,1280]{1,0:T(8,128)(2,1)S(1)}, bf16[128,1280]{1,0:T(8,128)(2,1)S(1)}, u32[]{:S(2)}, u32[]{:S(2)}) %collective-permute-start.4) | collective-permute-done | bytes 327712 | tf_op jit(solution)/shard_map/ppermute | solution.py:38
  63.2 5.7 %collective-permute-start.6 = (bf16[128,1280]{1,0:T(8,128)(2,1)S(1)}, bf16[128,1280]{1,0:T(8,128)(2,1)S(1)}, u32[]{:S(2)}, u32[]{:S(2)}) collective-permute-start(bf16[128,1280]{1,0:T(8,128)(2,1)S(1)} %slice.15), channel_id=1, source_target_pairs={{3,0},{0,1},{1,2},{2,3},{7,4},{4,5},{5,6},{6,7},{11,8},{8,9},{9,10... | collective-permute-start | bytes 983048 | tf_op jit(solution)/shard_map/ppermute | solution.py:38
  70.5 1.9 %copy.9 = bf16[32,6,40,128]{3,2,0,1:T(8,128)(2,1)S(1)} copy(bf16[32,6,40,128]{3,2,1,0:T(8,128)(2,1)} %bitcast.15) | data formatting | bytes 3932160 | tf_op jit(solution)/shard_map/reshape | solution.py:63
  73.9 7.1 %collective-permute-done.10.refs_4_ = bf16[256,1280]{1,0:T(8,128)(2,1)S(1)} collective-permute-done((bf16[256,1280]{1,0:T(8,128)(2,1)S(1)}, bf16[256,1280]{1,0:T(8,128)(2,1)S(1)}, u32[]{:S(2)}, u32[]{:S(2)}) %collective-permute-start.10) | collective-permute-done | bytes 655392 | tf_op jit(solution)/shard_map/ppermute | solution.py:38
  81.0 3.1 %collective-permute-done.8.refs_2_ = bf16[256,1280]{1,0:T(8,128)(2,1)S(1)} collective-permute-done((bf16[256,1280]{1,0:T(8,128)(2,1)S(1)}, bf16[256,1280]{1,0:T(8,128)(2,1)S(1)}, u32[]{:S(2)}, u32[]{:S(2)}) %collective-permute-start.8) | collective-permute-done | bytes 655392 | tf_op jit(solution)/shard_map/ppermute | solution.py:38
  85.0 2.4 %collective-permute-done.11.refs_5_ = bf16[384,1280]{1,0:T(8,128)(2,1)S(1)} collective-permute-done((bf16[384,1280]{1,0:T(8,128)(2,1)S(1)}, bf16[384,1280]{1,0:T(8,128)(2,1)S(1)}, u32[]{:S(2)}, u32[]{:S(2)}) %collective-permute-start.11) | collective-permute-done | bytes 983072 | tf_op jit(solution)/shard_map/ppermute | solution.py:38
  87.4 3.2 %assemble.1 = bf16[64,32,1280]{2,1,0:T(8,128)(2,1)} custom-call(s32[64]{0:T(128)S(1)} %fusion.22.slots, bf16[512,1280]{1,0:T(8,128)(2,1)S(1)} %constant_dynamic-update-slice_fusion.refs_0_, bf16[256,1280]{1,0:T(8,128)(2,1)S(1)} %collective-permute-done.7.refs_1_, bf16[256,1280]{1,0:T(8,128)(2,1)S(1)} %collective-permute-done.8.refs_2_, ...), custom_call_target="tpu_custom_call" | custom-call | tf_op jit(solution)/shard_map/assemble/pallas_call | solution.py:78
  90.6 5.6 %collective-permute-start.12 = (bf16[64,32,1280]{2,1,0:T(8,128)(2,1)}, bf16[64,32,1280]{2,1,0:T(8,128)(2,1)}, u32[]{:S(2)}, u32[]{:S(2)}) collective-permute-start(bf16[64,32,1280]{2,1,0:T(8,128)(2,1)} %assemble.1), channel_id=1, source_target_pairs={{0,32},{1,33},{2,34},{3,35},{4,36},{5,37},{6,38},{7,39},{8,40},{9,... | collective-permute-start | bytes 15728648 | tf_op jit(solution)/shard_map/ppermute | solution.py:405
  96.3 8.8 %rhs_part.1 = bf16[128,32,128]{2,1,0:T(8,128)(2,1)S(1)} custom-call(f32[2]{0:T(128)S(1)} %dynamic_slice.7.scale_ref, bf16[2048,1280]{1,0:T(8,128)(2,1)} %bitcast.10.own_hbm.pixels_ref, bf16[6,1280,128]{2,1,0:T(8,128)(2,1)S(1)} %bitcast.14), custom_call_target="tpu_custom_call" | custom-call | flops 4000000000 | bytes 8000000 | tf_op jit(solution)/shard_map/rhs_part/pallas_call | solution.py:307
  106.1 4.4 %all-to-all-start.1 = ((bf16[128,32,128]{2,1,0:T(8,128)(2,1)}), bf16[128,32,128]{2,1,0:T(8,128)(2,1)S(1)}, u32[]{:S(2)}, u32[]{:S(2)}) async-start(bf16[128,32,128]{2,1,0:T(8,128)(2,1)} %copy-done.1), calls=%async_computation.1 | async-start | bytes 2097152 | tf_op jit(solution)/shard_map/all_to_all | solution.py:409
  110.5 26.6 %gram.1 = (f32[90,11520]{1,0:T(8,128)}, f32[8,128]{1,0:T(8,128)}) custom-call(s32[1]{0:T(128)} %bitcast.first_ref, bf16[2048,1280]{1,0:T(8,128)(2,1)} %bitcast.10.own_hbm.pixels_ref, bf16[2048,1280]{1,0:T(8,128)(2,1)} %bitcast.11.other_hbm, bf16[16,1280]{1,0:T(8,128)(2,1)} %fusion.11.pick_ref, bf16[96,144]{1,0:T(8,128)(2,1)} %fusion.9.order_ref, ...), custom_call_target="tpu_custom_call" | custom-call | flops 20000000000 | bytes 20000000 | tf_op jit(solution)/shard_map/gram/pallas_call | solution.py:175
  137.8 1.6 %finish.1 = f32[90,1280]{1,0:T(8,128)} custom-call(bf16[128,32,128]{2,1,0:T(8,128)(2,1)S(1)} %all-to-all-done.1.sent_ref, f32[8,128]{1,0:T(8,128)S(1)} %copy-done.2), custom_call_target="tpu_custom_call" | custom-call | tf_op jit(solution)/shard_map/finish/pallas_call | solution.py:357
  (61 shorter events, 16.6 us)
Async XLA Ops:
  2.4 31.0 %collective-permute-start.2 = (bf16[32,1280]{1,0:T(8,128)(2,1)S(1)}, bf16[32,1280]{1,0:T(8,128)(2,1)S(1)}, u32[]{:S(2)}, u32[]{:S(2)}) collective-permute-start(bf16[32,1280]{1,0:T(8,128)(2,1)S(1)} %bitcast.16), channel_id=1, source_target_pairs={{92,0},{93,1},{94,2},{95,3},{24,4},{25,5},{26,6},{27,7},{68,8},{69... | collective-permute-start | bytes 245768 | tf_op jit(solution)/shard_map/ppermute | solution.py:38
  5.9 27.5 %collective-permute-start.1 = (bf16[32,1280]{1,0:T(8,128)(2,1)S(1)}, bf16[32,1280]{1,0:T(8,128)(2,1)S(1)}, u32[]{:S(2)}, u32[]{:S(2)}) collective-permute-start(bf16[32,1280]{1,0:T(8,128)(2,1)S(1)} %bitcast.17), channel_id=1, source_target_pairs={{80,0},{81,1},{82,2},{83,3},{84,4},{85,5},{86,6},{87,7},{88,8},{89... | collective-permute-start | bytes 245768 | tf_op jit(solution)/shard_map/ppermute | solution.py:38
  11.3 22.1 %collective-permute-start = (bf16[32,1280]{1,0:T(8,128)(2,1)S(1)}, bf16[32,1280]{1,0:T(8,128)(2,1)}, u32[]{:S(2)}, u32[]{:S(2)}) collective-permute-start(bf16[32,1280]{1,0:T(8,128)(2,1)S(1)} %bitcast.18), channel_id=1, source_target_pairs={{12,0},{13,1},{14,2},{15,3},{72,4},{73,5},{74,6},{75,7},{20,8},{21... | collective-permute-start | bytes 245768 | tf_op jit(solution)/shard_map/ppermute | solution.py:38
  13.7 1.5 %copy-start = (bf16[2,360,1280]{2,1,0:T(8,128)(2,1)S(1)}, bf16[2,360,1280]{2,1,0:T(8,128)(2,1)}, u32[]{:S(2)}) copy-start(bf16[2,360,1280]{2,1,0:T(8,128)(2,1)} %weights_ref.1) | copy-start | bytes 5529604
  18.7 44.4 %all-to-all-start = ((bf16[32,240,128]{2,1,0:T(8,128)(2,1)}), bf16[32,240,128]{2,1,0:T(8,128)(2,1)S(1)}, u32[]{:S(2)}, u32[]{:S(2)}) async-start(bf16[32,240,128]{2,1,0:T(8,128)(2,1)} %pack.1), calls=%async_computation | async-start | bytes 3932160 | tf_op jit(solution)/shard_map/all_to_all | solution.py:57
  34.3 28.7 %collective-permute-start.5 = (bf16[128,1280]{1,0:T(8,128)(2,1)S(1)}, bf16[128,1280]{1,0:T(8,128)(2,1)S(1)}, u32[]{:S(2)}, u32[]{:S(2)}) collective-permute-start(bf16[128,1280]{1,0:T(8,128)(2,1)S(1)} %pad_maximum_fusion), channel_id=1, source_target_pairs={{79,0},{76,1},{77,2},{78,3},{11,4},{8,5},{9,6},{10,7},{87,8},{84,9... | collective-permute-start | bytes 983048 | tf_op jit(solution)/shard_map/ppermute | solution.py:38
  38.7 24.3 %collective-permute-start.4 = (bf16[128,1280]{1,0:T(8,128)(2,1)S(1)}, bf16[128,1280]{1,0:T(8,128)(2,1)S(1)}, u32[]{:S(2)}, u32[]{:S(2)}) collective-permute-start(bf16[128,1280]{1,0:T(8,128)(2,1)S(1)} %pad_maximum_fusion), channel_id=1, source_target_pairs={{2,0},{3,1},{0,2},{1,3},{6,4},{7,5},{4,6},{5,7},{10,8},{11,9},{8,1... | collective-permute-start | bytes 983048 | tf_op jit(solution)/shard_map/ppermute | solution.py:38
  41.1 18.7 %collective-permute-start.3 = (bf16[128,1280]{1,0:T(8,128)(2,1)S(1)}, bf16[128,1280]{1,0:T(8,128)(2,1)S(1)}, u32[]{:S(2)}, u32[]{:S(2)}) collective-permute-start(bf16[128,1280]{1,0:T(8,128)(2,1)S(1)} %pad_maximum_fusion), channel_id=1, source_target_pairs={{29,0},{30,1},{31,2},{28,3},{89,4},{90,5},{91,6},{88,7},{5,8},{6,9... | collective-permute-start | bytes 983048 | tf_op jit(solution)/shard_map/ppermute | solution.py:38
  63.1 5.9 %copy-start.3 = (bf16[32,240,128]{2,1,0:T(8,128)(2,1)}, bf16[32,240,128]{2,1,0:T(8,128)(2,1)S(1)}, u32[]{:S(2)}) copy-start(bf16[32,240,128]{2,1,0:T(8,128)(2,1)S(1)} %all-to-all-done) | copy-start | bytes 5898244
  63.2 9.7 %collective-permute-start.6 = (bf16[128,1280]{1,0:T(8,128)(2,1)S(1)}, bf16[128,1280]{1,0:T(8,128)(2,1)S(1)}, u32[]{:S(2)}, u32[]{:S(2)}) collective-permute-start(bf16[128,1280]{1,0:T(8,128)(2,1)S(1)} %slice.15), channel_id=1, source_target_pairs={{3,0},{0,1},{1,2},{2,3},{7,4},{4,5},{5,6},{6,7},{11,8},{8,9},{9,10... | collective-permute-start | bytes 983048 | tf_op jit(solution)/shard_map/ppermute | solution.py:38
  68.8 18.5 %collective-permute-start.11 = (bf16[384,1280]{1,0:T(8,128)(2,1)S(1)}, bf16[384,1280]{1,0:T(8,128)(2,1)S(1)}, u32[]{:S(2)}, u32[]{:S(2)}) collective-permute-start(bf16[384,1280]{1,0:T(8,128)(2,1)S(1)} %slice.17), channel_id=1, source_target_pairs={{1,0},{2,1},{3,2},{0,3},{5,4},{6,5},{7,6},{4,7},{9,8},{10,9},{11,1... | collective-permute-start | bytes 2949128 | tf_op jit(solution)/shard_map/ppermute | solution.py:38
  68.9 12.1 %collective-permute-start.10 = (bf16[256,1280]{1,0:T(8,128)(2,1)S(1)}, bf16[256,1280]{1,0:T(8,128)(2,1)S(1)}, u32[]{:S(2)}, u32[]{:S(2)}) collective-permute-start(bf16[256,1280]{1,0:T(8,128)(2,1)S(1)} %get-tuple-element.24), channel_id=1, source_target_pairs={{8,0},{9,1},{10,2},{11,3},{12,4},{13,5},{14,6},{15,7},{16,8},{17,9... | collective-permute-start | bytes 1966088 | tf_op jit(solution)/shard_map/ppermute | solution.py:38
  70.2 13.9 %collective-permute-start.8 = (bf16[256,1280]{1,0:T(8,128)(2,1)S(1)}, bf16[256,1280]{1,0:T(8,128)(2,1)S(1)}, u32[]{:S(2)}, u32[]{:S(2)}) collective-permute-start(bf16[256,1280]{1,0:T(8,128)(2,1)S(1)} %get-tuple-element.24), channel_id=1, source_target_pairs={{24,0},{25,1},{26,2},{27,3},{28,4},{29,5},{30,6},{31,7},{0,8},{1,9... | collective-permute-start | bytes 1966088 | tf_op jit(solution)/shard_map/ppermute | solution.py:38
  72.4 11.7 %collective-permute-start.7 = (bf16[256,1280]{1,0:T(8,128)(2,1)S(1)}, bf16[256,1280]{1,0:T(8,128)(2,1)S(1)}, u32[]{:S(2)}, u32[]{:S(2)}) collective-permute-start(bf16[256,1280]{1,0:T(8,128)(2,1)S(1)} %get-tuple-element.16), channel_id=1, source_target_pairs={{4,0},{5,1},{6,2},{7,3},{64,4},{65,5},{66,6},{67,7},{12,8},{13,9},... | collective-permute-start | bytes 1966088 | tf_op jit(solution)/shard_map/ppermute | solution.py:38
  72.9 12.2 %collective-permute-start.9 = (bf16[256,1280]{1,0:T(8,128)(2,1)S(1)}, bf16[256,1280]{1,0:T(8,128)(2,1)S(1)}, u32[]{:S(2)}, u32[]{:S(2)}) collective-permute-start(bf16[256,1280]{1,0:T(8,128)(2,1)S(1)} %get-tuple-element.16), channel_id=1, source_target_pairs={{68,0},{69,1},{70,2},{71,3},{0,4},{1,5},{2,6},{3,7},{76,8},{77,9},... | collective-permute-start | bytes 1966088 | tf_op jit(solution)/shard_map/ppermute | solution.py:38
  90.6 19.9 %collective-permute-start.12 = (bf16[64,32,1280]{2,1,0:T(8,128)(2,1)}, bf16[64,32,1280]{2,1,0:T(8,128)(2,1)}, u32[]{:S(2)}, u32[]{:S(2)}) collective-permute-start(bf16[64,32,1280]{2,1,0:T(8,128)(2,1)} %assemble.1), channel_id=1, source_target_pairs={{0,32},{1,33},{2,34},{3,35},{4,36},{5,37},{6,38},{7,39},{8,40},{9,... | collective-permute-start | bytes 15728648 | tf_op jit(solution)/shard_map/ppermute | solution.py:405
  105.1 1.0 copy-start.1
  106.1 31.0 %all-to-all-start.1 = ((bf16[128,32,128]{2,1,0:T(8,128)(2,1)}), bf16[128,32,128]{2,1,0:T(8,128)(2,1)S(1)}, u32[]{:S(2)}, u32[]{:S(2)}) async-start(bf16[128,32,128]{2,1,0:T(8,128)(2,1)} %copy-done.1), calls=%async_computation.1 | async-start | bytes 2097152 | tf_op jit(solution)/shard_map/all_to_all | solution.py:409
  137.1 0.7 copy-start.2

commit v7 on v6

--- a/solution.py
+++ b/solution.py
@@ -46,7 +46,7 @@
 FIRST = [tuple(k * s % 4 for s in STEP) for k in range(4)]
 SECOND = [(0, 0, 0), (1, 1, 3), (0, 2, 0), (3, 3, 1)]
 LEVEL = [vec_add(g, f) for g in SECOND for f in FIRST]
-LAST = [((1, 0, 0), 0, 8), ((0, 0, 3), 8, 16), ((3, 0, 0), 0, 8), ((0, 0, 1), 8, 16), ((0, 1, 0), 0, 12), ((0, 3, 0), 4, 8)]
+LAST = [((1, 0, 0), 0, 8), ((0, 0, 3), 8, 16), ((3, 0, 0), 0, 8), ((0, 0, 1), 8, 16), ((0, 1, 0), 0, 10), ((0, 3, 0), 2, 8)]
 SOURCES = list(LEVEL)
 for away, low, high in LAST:
     SOURCES += [vec_add(away, o) for o in LEVEL[low:high]]
@@ -60,9 +60,11 @@
     level, tiles = lax.optimization_barrier((level, tiles))
     parts = [level[low * ROWS : high * ROWS] for _, low, high in LAST]
     small = take_from(parts[5], LAST[5][0])
+    parts[2], small, early = lax.optimization_barrier((parts[2], small, early))
+    pieces = [take_from(part, last[0]) for part, last in zip(parts[:5], LAST)]
     tiles = tiles.reshape(32, 6, 40, 128).transpose(1, 0, 2, 3).reshape(6, CH, 128)
-    parts[2], small, tiles, early = lax.optimization_barrier((parts[2], small, tiles, early))
-    return [level] + [take_from(part, last[0]) for part, last in zip(parts[:5], LAST)] + [small], tiles, early
+    pieces[0], tiles = lax.optimization_barrier((pieces[0], tiles))
+    return [level] + pieces + [small], tiles, early
 
 
 def assemble_kernel(slots, *refs):
@@ -95,22 +97,21 @@
     return jnp.where(inside, moved, 0.0)
 
 
-def gram_kernel(first_ref, own_hbm, other_hbm, pick_ref, order_ref, scale_ref, out_ref, token_ref, left, acc, staged, pixels_own, pixels_other, sems, loads):
-    own_ref, other_ref = pixels_own, pixels_other
+def gram_kernel(first_ref, own_hbm, other_hbm, pick_ref, order_ref, scale_ref, out_ref, token_ref, left, acc, staged, pixels, sems, loads):
     copies = []
     for group in range(4):
+        source = own_hbm if group < 2 else other_hbm
         rows = pl.ds((group % 2) * LANES, LANES)
-        source, target = (own_hbm, pixels_own) if group < 2 else (other_hbm, pixels_other)
-        copies.append(pltpu.make_async_copy(source.at[rows], target.at[rows], loads.at[group]))
+        target = pixels.at[pl.ds(group * LANES, LANES)]
+        copies.append(pltpu.make_async_copy(source.at[rows], target, loads.at[group]))
         copies[-1].start()
-    token_ref[...] = jnp.zeros_like(token_ref)
+    del token_ref
     pick = pick_ref[...]
     order = order_ref[...]
     for group in range(4):
         copies[group].wait()
-        source = own_ref if group < 2 else other_ref
-        pixels = source[pl.ds((group % 2) * LANES, LANES), :]
-        slab = lax.dot_general(pick, pixels, (((1,), (1,)), ((), ())), preferred_element_type=jnp.float32)
+        rows = pixels[pl.ds(group * LANES, LANES), :]
+        slab = lax.dot_general(pick, rows, (((1,), (1,)), ((), ())), preferred_element_type=jnp.float32)
         shifted = [shift_lanes(slab, t // 3 - 1, t % 3 - 1) for t in range(TAPS)]
         stacked = jnp.concatenate(shifted, axis=0).astype(jnp.bfloat16)
         patch = jnp.dot(order, stacked, preferred_element_type=jnp.float32)
@@ -135,9 +136,9 @@
 
     def multiply(n):
         lanes = pl.ds(n * 256, 256)
-        total = jnp.dot(left[:, pl.ds(0, 2048)], own_ref[:, lanes], preferred_element_type=jnp.float32)
-        total += jnp.dot(left[:, pl.ds(2048, 2048)], other_ref[:, lanes], preferred_element_type=jnp.float32)
-        acc[:, lanes] = total
+
+        for m in range(3):
+            acc[pl.ds(m * 288, 288), lanes] = jnp.dot(left[pl.ds(m * 288, 288), :], pixels[:, lanes], preferred_element_type=jnp.float32)
 
     def interleave(block):
         lanes = pl.ds(block * 128, 128)
@@ -176,13 +177,12 @@
         gram_kernel,
         out_shape=(jax.ShapeDtypeStruct((90, 11520), jnp.float32), jax.ShapeDtypeStruct((8, 128), jnp.float32)),
         in_specs=[pl.BlockSpec(memory_space=pltpu.SMEM), held, held] + [whole] * 3,
-        out_specs=(held, whole),
+        out_specs=(held, held),
         scratch_shapes=[
             pltpu.VMEM((TAPS * MPAD, 4 * LANES), jnp.bfloat16),
             pltpu.VMEM((TAPS * MPAD, CH), jnp.float32),
             pltpu.VMEM((90, 11520), jnp.float32),
-            pltpu.VMEM((2 * LANES, CH), jnp.bfloat16),
-            pltpu.VMEM((2 * LANES, CH), jnp.bfloat16),
+            pltpu.VMEM((4 * LANES, CH), jnp.bfloat16),
             pltpu.SemaphoreType.DMA((10,)),
             pltpu.SemaphoreType.DMA((4,)),
         ],
@@ -357,7 +357,7 @@
     return pl.pallas_call(
         finish_kernel,
         out_shape=jax.ShapeDtypeStruct((90, CH), jnp.float32),
-        in_specs=[whole, whole],
+        in_specs=[whole, pl.BlockSpec(memory_space=pltpu.HBM)],
         out_specs=whole,
         scratch_shapes=[pltpu.VMEM((96, CH), jnp.float32)],
         compiler_params=pltpu.CompilerParams(vmem_limit_bytes=16 * 1024 * 1024),

time: 140 us -> 141 us (level)
  starting transfers between devices: 41.8 us -> 45.2 us
  Pallas kernels: 43.6 us -> 41.5 us
    all_to_all x1, starting transfers between devices: 4.41 us -> 7.02 us  [body(): lax.all_to_all(part, ('blk', 'client'), split_axis=0, concat_axis=0, tile...]
    pallas_call x1, Pallas kernels: 26.6 us -> 24.4 us  [gram(): pl.pallas_call(gram_kernel, out_shape=(jax.ShapeDtypeStruct((90, 11520),...]
  transfers between devices with their start and end apart: 15 -> 15, of which waited for: 7 -> 8; matrix products, arithmetic and copies ran while one was open for 10% -> 10% of each run, Pallas kernels for 28% -> 26%
where the time goes in v7:
time: 141 us
  starting transfers between devices  45.2 us (32%)
  Pallas kernels  41.5 us (29%)
  waiting for transfers between devices  34.5 us (24%)
  local copies, waits for them, and re-layouts  9.98 us (7%)
  other arithmetic  8.56 us (6%)
    ppermute x12, waiting for transfers between devices, take_from(): return lax.ppermute(value, AXES, pairs)  34.5 us
    ppermute x12, starting transfers between devices, take_from(): return lax.ppermute(value, AXES, pairs)  27.1 us
    pallas_call x1, Pallas kernels, gram(): pl.pallas_call(gram_kernel, out_shape=(jax.ShapeDtypeStruct((90, 11520),...  24.4 us
    pallas_call x1, Pallas kernels, rhs_part(): pl.pallas_call(rhs_kernel, out_shape=jax.ShapeDtypeStruct((128, 32, 128),...  8.8 us
    all_to_all x1, starting transfers between devices, body(): lax.all_to_all(part, ('blk', 'client'), split_axis=0, concat_axis=0, tile...  7.02 us
    ppermute x1, starting transfers between devices, body(): other = lax.ppermute(own, AXES, [(d, d ^ 32) for d in range(128)])  6.01 us
    all_to_all x1, starting transfers between devices, gather_chips(): lax.all_to_all(packed, 'blk', split_axis=0, concat_axis=0, tiled=True)  5.06 us
    unnamed x14, local copies, waits for them, and re-layouts  4.13 us
  transfers between devices with their start and end apart: 15, of which 8 were waited for; matrix products, arithmetic and copies ran while one was open for 10% of the time, Pallas kernels for 26%

profile of v7, /device:TPU:1, one launch (start us, length us, event | category | flops | bytes accessed | tf_op | source)
XLA Modules:
  0.0 140.7 jit_solution(12183606544139235062)
XLA Ops:
  2.4 3.5 %collective-permute-start.2 = (bf16[32,1280]{1,0:T(8,128)(2,1)S(1)}, bf16[32,1280]{1,0:T(8,128)(2,1)S(1)}, u32[]{:S(2)}, u32[]{:S(2)}) collective-permute-start(bf16[32,1280]{1,0:T(8,128)(2,1)S(1)} %bitcast.16), channel_id=1, source_target_pairs={{92,0},{93,1},{94,2},{95,3},{24,4},{25,5},{26,6},{27,7},{68,8},{69... | collective-permute-start | bytes 245768 | tf_op jit(solution)/shard_map/ppermute | solution.py:38
  5.9 5.5 %collective-permute-start.1 = (bf16[32,1280]{1,0:T(8,128)(2,1)S(1)}, bf16[32,1280]{1,0:T(8,128)(2,1)S(1)}, u32[]{:S(2)}, u32[]{:S(2)}) collective-permute-start(bf16[32,1280]{1,0:T(8,128)(2,1)S(1)} %bitcast.17), channel_id=1, source_target_pairs={{80,0},{81,1},{82,2},{83,3},{84,4},{85,5},{86,6},{87,7},{88,8},{89... | collective-permute-start | bytes 245768 | tf_op jit(solution)/shard_map/ppermute | solution.py:38
  11.3 1.6 %collective-permute-start = (bf16[32,1280]{1,0:T(8,128)(2,1)S(1)}, bf16[32,1280]{1,0:T(8,128)(2,1)}, u32[]{:S(2)}, u32[]{:S(2)}) collective-permute-start(bf16[32,1280]{1,0:T(8,128)(2,1)S(1)} %bitcast.18), channel_id=1, source_target_pairs={{12,0},{13,1},{14,2},{15,3},{72,4},{73,5},{74,6},{75,7},{20,8},{21... | collective-permute-start | bytes 245768 | tf_op jit(solution)/shard_map/ppermute | solution.py:38
  13.7 1.5 %copy-done = bf16[2,360,1280]{2,1,0:T(8,128)(2,1)S(1)} copy-done((bf16[2,360,1280]{2,1,0:T(8,128)(2,1)S(1)}, bf16[2,360,1280]{2,1,0:T(8,128)(2,1)}, u32[]{:S(2)}) %copy-start) | copy-done | bytes 1843224
  15.2 3.5 %pack.1 = bf16[32,240,128]{2,1,0:T(8,128)(2,1)} custom-call(bf16[2,360,1280]{2,1,0:T(8,128)(2,1)S(1)} %copy-done, bf16[360,360]{1,0:T(8,128)(2,1)S(1)} %fusion.6.order_ref), custom_call_target="tpu_custom_call" | custom-call | flops 1000000000 | bytes 6000000 | tf_op jit(solution)/shard_map/pack/pallas_call | solution.py:217
  18.7 5.1 %all-to-all-start = ((bf16[32,240,128]{2,1,0:T(8,128)(2,1)}), bf16[32,240,128]{2,1,0:T(8,128)(2,1)S(1)}, u32[]{:S(2)}, u32[]{:S(2)}) async-start(bf16[32,240,128]{2,1,0:T(8,128)(2,1)} %pack.1), calls=%async_computation | async-start | bytes 3932160 | tf_op jit(solution)/shard_map/all_to_all | solution.py:57
  27.6 1.4 %fusion.9.order_ref = bf16[96,144]{1,0:T(8,128)(2,1)} fusion(s32[144]{0:T(256)S(1)} %get-tuple-element.36, s32[144]{0:T(256)S(1)} %get-tuple-element.45, s32[96]{0:T(128)} %get-tuple-element.43, s32[96]{0:T(128)} %get-tuple-element.47, s32[144]{0:T(256)S(1)} %get-tuple-element.37, s32[144]{0:T(256)S(1)} %get-tuple-element.44, s32[96]{0:T(128)} %get-tuple-element.42, ...), kind=kLoop, calls=%fused_computation.15 | loop fusion | flops 110592 | bytes 31968 | tf_op jit(solution)/shard_map/convert_element_type | solution.py:392
  31.2 1.5 %broadcast_in_dim.26.scale_ref = f32[4,1024]{1,0:T(4,128)} reshape(f32[4,32,32]{2,1,0:T(8,128)} %broadcast_in_dim.25) | data formatting | bytes 32768 | tf_op jit(solution)/shard_map/broadcast_in_dim | solution.py:395
  33.7 4.4 %collective-permute-start.5 = (bf16[128,1280]{1,0:T(8,128)(2,1)S(1)}, bf16[128,1280]{1,0:T(8,128)(2,1)S(1)}, u32[]{:S(2)}, u32[]{:S(2)}) collective-permute-start(bf16[128,1280]{1,0:T(8,128)(2,1)S(1)} %pad_maximum_fusion), channel_id=1, source_target_pairs={{79,0},{76,1},{77,2},{78,3},{11,4},{8,5},{9,6},{10,7},{87,8},{84,9... | collective-permute-start | bytes 983048 | tf_op jit(solution)/shard_map/ppermute | solution.py:38
  38.1 2.4 %collective-permute-start.4 = (bf16[128,1280]{1,0:T(8,128)(2,1)S(1)}, bf16[128,1280]{1,0:T(8,128)(2,1)S(1)}, u32[]{:S(2)}, u32[]{:S(2)}) collective-permute-start(bf16[128,1280]{1,0:T(8,128)(2,1)S(1)} %pad_maximum_fusion), channel_id=1, source_target_pairs={{2,0},{3,1},{0,2},{1,3},{6,4},{7,5},{4,6},{5,7},{10,8},{11,9},{8,1... | collective-permute-start | bytes 983048 | tf_op jit(solution)/shard_map/ppermute | solution.py:38
  42.5 17.6 %collective-permute-done.3 = bf16[128,1280]{1,0:T(8,128)(2,1)S(1)} collective-permute-done((bf16[128,1280]{1,0:T(8,128)(2,1)S(1)}, bf16[128,1280]{1,0:T(8,128)(2,1)S(1)}, u32[]{:S(2)}, u32[]{:S(2)}) %collective-permute-start.3) | collective-permute-done | bytes 327712 | tf_op jit(solution)/shard_map/ppermute | solution.py:38
  60.1 2.7 %collective-permute-done.4 = bf16[128,1280]{1,0:T(8,128)(2,1)S(1)} collective-permute-done((bf16[128,1280]{1,0:T(8,128)(2,1)S(1)}, bf16[128,1280]{1,0:T(8,128)(2,1)S(1)}, u32[]{:S(2)}, u32[]{:S(2)}) %collective-permute-start.4) | collective-permute-done | bytes 327712 | tf_op jit(solution)/shard_map/ppermute | solution.py:38
  63.0 6.1 %collective-permute-start.6 = (bf16[192,1280]{1,0:T(8,128)(2,1)S(1)}, bf16[192,1280]{1,0:T(8,128)(2,1)S(1)}, u32[]{:S(2)}, u32[]{:S(2)}) collective-permute-start(bf16[192,1280]{1,0:T(8,128)(2,1)S(1)} %slice.15), channel_id=1, source_target_pairs={{3,0},{0,1},{1,2},{2,3},{7,4},{4,5},{5,6},{6,7},{11,8},{8,9},{9,10... | collective-permute-start | bytes 1474568 | tf_op jit(solution)/shard_map/ppermute | solution.py:38
  70.9 4.6 %collective-permute-done.6.refs_6_ = bf16[192,1280]{1,0:T(8,128)(2,1)S(1)} collective-permute-done((bf16[192,1280]{1,0:T(8,128)(2,1)S(1)}, bf16[192,1280]{1,0:T(8,128)(2,1)S(1)}, u32[]{:S(2)}, u32[]{:S(2)}) %collective-permute-start.6) | collective-permute-done | bytes 491552 | tf_op jit(solution)/shard_map/ppermute | solution.py:38
  76.4 1.9 %copy.9 = bf16[32,6,40,128]{3,2,0,1:T(8,128)(2,1)S(1)} copy(bf16[32,6,40,128]{3,2,1,0:T(8,128)(2,1)} %bitcast.15) | data formatting | bytes 3932160 | tf_op jit(solution)/shard_map/reshape | solution.py:65
  78.3 2.5 %collective-permute-done.7.refs_1_ = bf16[256,1280]{1,0:T(8,128)(2,1)S(1)} collective-permute-done((bf16[256,1280]{1,0:T(8,128)(2,1)S(1)}, bf16[256,1280]{1,0:T(8,128)(2,1)S(1)}, u32[]{:S(2)}, u32[]{:S(2)}) %collective-permute-start.7) | collective-permute-done | bytes 655392 | tf_op jit(solution)/shard_map/ppermute | solution.py:38
  80.9 3.1 %collective-permute-done.8.refs_2_ = bf16[256,1280]{1,0:T(8,128)(2,1)S(1)} collective-permute-done((bf16[256,1280]{1,0:T(8,128)(2,1)S(1)}, bf16[256,1280]{1,0:T(8,128)(2,1)S(1)}, u32[]{:S(2)}, u32[]{:S(2)}) %collective-permute-start.8) | collective-permute-done | bytes 655392 | tf_op jit(solution)/shard_map/ppermute | solution.py:38
  84.2 3.7 %collective-permute-done.9.refs_3_ = bf16[256,1280]{1,0:T(8,128)(2,1)S(1)} collective-permute-done((bf16[256,1280]{1,0:T(8,128)(2,1)S(1)}, bf16[256,1280]{1,0:T(8,128)(2,1)S(1)}, u32[]{:S(2)}, u32[]{:S(2)}) %collective-permute-start.9) | collective-permute-done | bytes 655392 | tf_op jit(solution)/shard_map/ppermute | solution.py:38
  87.9 3.2 %assemble.1 = bf16[64,32,1280]{2,1,0:T(8,128)(2,1)} custom-call(s32[64]{0:T(128)S(1)} %fusion.22.slots, bf16[512,1280]{1,0:T(8,128)(2,1)S(1)} %constant_dynamic-update-slice_fusion.refs_0_, bf16[256,1280]{1,0:T(8,128)(2,1)S(1)} %collective-permute-done.7.refs_1_, bf16[256,1280]{1,0:T(8,128)(2,1)S(1)} %collective-permute-done.8.refs_2_, ...), custom_call_target="tpu_custom_call" | custom-call | tf_op jit(solution)/shard_map/assemble/pallas_call | solution.py:80
  91.1 6.0 %collective-permute-start.12 = (bf16[64,32,1280]{2,1,0:T(8,128)(2,1)}, bf16[64,32,1280]{2,1,0:T(8,128)(2,1)}, u32[]{:S(2)}, u32[]{:S(2)}) collective-permute-start(bf16[64,32,1280]{2,1,0:T(8,128)(2,1)} %assemble.1), channel_id=1, source_target_pairs={{0,32},{1,33},{2,34},{3,35},{4,36},{5,37},{6,38},{7,39},{8,40},{9,... | collective-permute-start | bytes 15728648 | tf_op jit(solution)/shard_map/ppermute | solution.py:405
  97.2 8.8 %rhs_part.1 = bf16[128,32,128]{2,1,0:T(8,128)(2,1)S(1)} custom-call(f32[2]{0:T(128)S(1)} %dynamic_slice.7.scale_ref, bf16[2048,1280]{1,0:T(8,128)(2,1)} %bitcast.10.own_hbm.pixels_ref, bf16[6,1280,128]{2,1,0:T(8,128)(2,1)S(1)} %bitcast.14), custom_call_target="tpu_custom_call" | custom-call | flops 4000000000 | bytes 8000000 | tf_op jit(solution)/shard_map/rhs_part/pallas_call | solution.py:307
  107.0 7.0 %all-to-all-start.1 = ((bf16[128,32,128]{2,1,0:T(8,128)(2,1)}), bf16[128,32,128]{2,1,0:T(8,128)(2,1)S(1)}, u32[]{:S(2)}, u32[]{:S(2)}) async-start(bf16[128,32,128]{2,1,0:T(8,128)(2,1)} %copy-done.1), calls=%async_computation.1 | async-start | bytes 2097152 | tf_op jit(solution)/shard_map/all_to_all | solution.py:409
  114.0 24.4 %gram.1 = (f32[90,11520]{1,0:T(8,128)}, f32[8,128]{1,0:T(8,128)}) custom-call(s32[1]{0:T(128)} %bitcast.first_ref, bf16[2048,1280]{1,0:T(8,128)(2,1)} %bitcast.10.own_hbm.pixels_ref, bf16[2048,1280]{1,0:T(8,128)(2,1)} %bitcast.11.other_hbm, bf16[16,1280]{1,0:T(8,128)(2,1)} %fusion.11.pick_ref, bf16[96,144]{1,0:T(8,128)(2,1)} %fusion.9.order_ref, ...), custom_call_target="tpu_custom_call" | custom-call | flops 20000000000 | bytes 20000000 | tf_op jit(solution)/shard_map/gram/pallas_call | solution.py:176
  139.1 1.6 %finish.1 = f32[90,1280]{1,0:T(8,128)} custom-call(bf16[128,32,128]{2,1,0:T(8,128)(2,1)S(1)} %all-to-all-done.1.sent_ref, f32[8,128]{1,0:T(8,128)S(1)} %copy-done.2), custom_call_target="tpu_custom_call" | custom-call | tf_op jit(solution)/shard_map/finish/pallas_call | solution.py:357
  (61 shorter events, 16.1 us)
Async XLA Ops:
  2.4 30.3 %collective-permute-start.2 = (bf16[32,1280]{1,0:T(8,128)(2,1)S(1)}, bf16[32,1280]{1,0:T(8,128)(2,1)S(1)}, u32[]{:S(2)}, u32[]{:S(2)}) collective-permute-start(bf16[32,1280]{1,0:T(8,128)(2,1)S(1)} %bitcast.16), channel_id=1, source_target_pairs={{92,0},{93,1},{94,2},{95,3},{24,4},{25,5},{26,6},{27,7},{68,8},{69... | collective-permute-start | bytes 245768 | tf_op jit(solution)/shard_map/ppermute | solution.py:38
  5.9 26.9 %collective-permute-start.1 = (bf16[32,1280]{1,0:T(8,128)(2,1)S(1)}, bf16[32,1280]{1,0:T(8,128)(2,1)S(1)}, u32[]{:S(2)}, u32[]{:S(2)}) collective-permute-start(bf16[32,1280]{1,0:T(8,128)(2,1)S(1)} %bitcast.17), channel_id=1, source_target_pairs={{80,0},{81,1},{82,2},{83,3},{84,4},{85,5},{86,6},{87,7},{88,8},{89... | collective-permute-start | bytes 245768 | tf_op jit(solution)/shard_map/ppermute | solution.py:38
  11.3 21.4 %collective-permute-start = (bf16[32,1280]{1,0:T(8,128)(2,1)S(1)}, bf16[32,1280]{1,0:T(8,128)(2,1)}, u32[]{:S(2)}, u32[]{:S(2)}) collective-permute-start(bf16[32,1280]{1,0:T(8,128)(2,1)S(1)} %bitcast.18), channel_id=1, source_target_pairs={{12,0},{13,1},{14,2},{15,3},{72,4},{73,5},{74,6},{75,7},{20,8},{21... | collective-permute-start | bytes 245768 | tf_op jit(solution)/shard_map/ppermute | solution.py:38
  13.7 1.5 %copy-start = (bf16[2,360,1280]{2,1,0:T(8,128)(2,1)S(1)}, bf16[2,360,1280]{2,1,0:T(8,128)(2,1)}, u32[]{:S(2)}) copy-start(bf16[2,360,1280]{2,1,0:T(8,128)(2,1)} %weights_ref.1) | copy-start | bytes 5529604
  18.7 44.2 %all-to-all-start = ((bf16[32,240,128]{2,1,0:T(8,128)(2,1)}), bf16[32,240,128]{2,1,0:T(8,128)(2,1)S(1)}, u32[]{:S(2)}, u32[]{:S(2)}) async-start(bf16[32,240,128]{2,1,0:T(8,128)(2,1)} %pack.1), calls=%async_computation | async-start | bytes 3932160 | tf_op jit(solution)/shard_map/all_to_all | solution.py:57
  33.7 29.2 %collective-permute-start.5 = (bf16[128,1280]{1,0:T(8,128)(2,1)S(1)}, bf16[128,1280]{1,0:T(8,128)(2,1)S(1)}, u32[]{:S(2)}, u32[]{:S(2)}) collective-permute-start(bf16[128,1280]{1,0:T(8,128)(2,1)S(1)} %pad_maximum_fusion), channel_id=1, source_target_pairs={{79,0},{76,1},{77,2},{78,3},{11,4},{8,5},{9,6},{10,7},{87,8},{84,9... | collective-permute-start | bytes 983048 | tf_op jit(solution)/shard_map/ppermute | solution.py:38
  38.1 24.8 %collective-permute-start.4 = (bf16[128,1280]{1,0:T(8,128)(2,1)S(1)}, bf16[128,1280]{1,0:T(8,128)(2,1)S(1)}, u32[]{:S(2)}, u32[]{:S(2)}) collective-permute-start(bf16[128,1280]{1,0:T(8,128)(2,1)S(1)} %pad_maximum_fusion), channel_id=1, source_target_pairs={{2,0},{3,1},{0,2},{1,3},{6,4},{7,5},{4,6},{5,7},{10,8},{11,9},{8,1... | collective-permute-start | bytes 983048 | tf_op jit(solution)/shard_map/ppermute | solution.py:38
  40.5 19.6 %collective-permute-start.3 = (bf16[128,1280]{1,0:T(8,128)(2,1)S(1)}, bf16[128,1280]{1,0:T(8,128)(2,1)S(1)}, u32[]{:S(2)}, u32[]{:S(2)}) collective-permute-start(bf16[128,1280]{1,0:T(8,128)(2,1)S(1)} %pad_maximum_fusion), channel_id=1, source_target_pairs={{29,0},{30,1},{31,2},{28,3},{89,4},{90,5},{91,6},{88,7},{5,8},{6,9... | collective-permute-start | bytes 983048 | tf_op jit(solution)/shard_map/ppermute | solution.py:38
  62.9 6.3 %copy-start.3 = (bf16[32,240,128]{2,1,0:T(8,128)(2,1)}, bf16[32,240,128]{2,1,0:T(8,128)(2,1)S(1)}, u32[]{:S(2)}) copy-start(bf16[32,240,128]{2,1,0:T(8,128)(2,1)S(1)} %all-to-all-done) | copy-start | bytes 5898244
  63.0 12.5 %collective-permute-start.6 = (bf16[192,1280]{1,0:T(8,128)(2,1)S(1)}, bf16[192,1280]{1,0:T(8,128)(2,1)S(1)}, u32[]{:S(2)}, u32[]{:S(2)}) collective-permute-start(bf16[192,1280]{1,0:T(8,128)(2,1)S(1)} %slice.15), channel_id=1, source_target_pairs={{3,0},{0,1},{1,2},{2,3},{7,4},{4,5},{5,6},{6,7},{11,8},{8,9},{9,10... | collective-permute-start | bytes 1474568 | tf_op jit(solution)/shard_map/ppermute | solution.py:38
  69.2 15.0 %collective-permute-start.11 = (bf16[320,1280]{1,0:T(8,128)(2,1)S(1)}, bf16[320,1280]{1,0:T(8,128)(2,1)S(1)}, u32[]{:S(2)}, u32[]{:S(2)}) collective-permute-start(bf16[320,1280]{1,0:T(8,128)(2,1)S(1)} %slice.17), channel_id=1, source_target_pairs={{1,0},{2,1},{3,2},{0,3},{5,4},{6,5},{7,6},{4,7},{9,8},{10,9},{11,1... | collective-permute-start | bytes 2457608 | tf_op jit(solution)/shard_map/ppermute | solution.py:38
  69.3 11.6 %collective-permute-start.7 = (bf16[256,1280]{1,0:T(8,128)(2,1)S(1)}, bf16[256,1280]{1,0:T(8,128)(2,1)S(1)}, u32[]{:S(2)}, u32[]{:S(2)}) collective-permute-start(bf16[256,1280]{1,0:T(8,128)(2,1)S(1)} %get-tuple-element.18), channel_id=1, source_target_pairs={{4,0},{5,1},{6,2},{7,3},{64,4},{65,5},{66,6},{67,7},{12,8},{13,9},... | collective-permute-start | bytes 1966088 | tf_op jit(solution)/shard_map/ppermute | solution.py:38
  69.3 11.6 %collective-permute-start.10 = (bf16[256,1280]{1,0:T(8,128)(2,1)S(1)}, bf16[256,1280]{1,0:T(8,128)(2,1)S(1)}, u32[]{:S(2)}, u32[]{:S(2)}) collective-permute-start(bf16[256,1280]{1,0:T(8,128)(2,1)S(1)} %get-tuple-element.26), channel_id=1, source_target_pairs={{8,0},{9,1},{10,2},{11,3},{12,4},{13,5},{14,6},{15,7},{16,8},{17,9... | collective-permute-start | bytes 1966088 | tf_op jit(solution)/shard_map/ppermute | solution.py:38
  70.4 13.6 %collective-permute-start.8 = (bf16[256,1280]{1,0:T(8,128)(2,1)S(1)}, bf16[256,1280]{1,0:T(8,128)(2,1)S(1)}, u32[]{:S(2)}, u32[]{:S(2)}) collective-permute-start(bf16[256,1280]{1,0:T(8,128)(2,1)S(1)} %get-tuple-element.26), channel_id=1, source_target_pairs={{24,0},{25,1},{26,2},{27,3},{28,4},{29,5},{30,6},{31,7},{0,8},{1,9... | collective-permute-start | bytes 1966088 | tf_op jit(solution)/shard_map/ppermute | solution.py:38
  75.5 12.4 %collective-permute-start.9 = (bf16[256,1280]{1,0:T(8,128)(2,1)S(1)}, bf16[256,1280]{1,0:T(8,128)(2,1)S(1)}, u32[]{:S(2)}, u32[]{:S(2)}) collective-permute-start(bf16[256,1280]{1,0:T(8,128)(2,1)S(1)} %get-tuple-element.18), channel_id=1, source_target_pairs={{68,0},{69,1},{70,2},{71,3},{0,4},{1,5},{2,6},{3,7},{76,8},{77,9},... | collective-permute-start | bytes 1966088 | tf_op jit(solution)/shard_map/ppermute | solution.py:38
  91.1 22.9 %collective-permute-start.12 = (bf16[64,32,1280]{2,1,0:T(8,128)(2,1)}, bf16[64,32,1280]{2,1,0:T(8,128)(2,1)}, u32[]{:S(2)}, u32[]{:S(2)}) collective-permute-start(bf16[64,32,1280]{2,1,0:T(8,128)(2,1)} %assemble.1), channel_id=1, source_target_pairs={{0,32},{1,33},{2,34},{3,35},{4,36},{5,37},{6,38},{7,39},{8,40},{9,... | collective-permute-start | bytes 15728648 | tf_op jit(solution)/shard_map/ppermute | solution.py:405
  106.0 1.0 copy-start.1
  107.0 31.5 %all-to-all-start.1 = ((bf16[128,32,128]{2,1,0:T(8,128)(2,1)}), bf16[128,32,128]{2,1,0:T(8,128)(2,1)S(1)}, u32[]{:S(2)}, u32[]{:S(2)}) async-start(bf16[128,32,128]{2,1,0:T(8,128)(2,1)} %copy-done.1), calls=%async_computation.1 | async-start | bytes 2097152 | tf_op jit(solution)/shard_map/all_to_all | solution.py:409
  138.4 0.7 copy-start.2

commit v8 on v7

--- a/solution.py
+++ b/solution.py
@@ -38,29 +38,36 @@
     return lax.ppermute(value, AXES, pairs)
 
 
-def vec_add(*vectors):
-    return tuple(sum(parts) % 4 for parts in zip(*vectors))
-
-
-STEP = (1, 0, 1)
-FIRST = [tuple(k * s % 4 for s in STEP) for k in range(4)]
-SECOND = [(0, 0, 0), (1, 1, 3), (0, 2, 0), (3, 3, 1)]
-LEVEL = [vec_add(g, f) for g in SECOND for f in FIRST]
-LAST = [((1, 0, 0), 0, 8), ((0, 0, 3), 8, 16), ((3, 0, 0), 0, 8), ((0, 0, 1), 8, 16), ((0, 1, 0), 0, 10), ((0, 3, 0), 2, 8)]
-SOURCES = list(LEVEL)
-for away, low, high in LAST:
-    SOURCES += [vec_add(away, o) for o in LEVEL[low:high]]
-assert len(SOURCES) == 64 and len(set(SOURCES)) == 64
+LAST = [((1, 0, 0), 1, 0, 16), ((0, 0, 3), 1, 16, 32), ((3, 0, 0), 3, 0, 16), ((0, 0, 1), 3, 16, 32), ((0, 1, 0), 2, 0, 24), ((0, 3, 0), 2, 24, 32)]
+
+
+def share_kernel(mine_ref, theirs_ref, out_ref):
+    for dest in range(32):
+        z, rest = divmod(dest, 8)
+        x_lo, y = divmod(rest, 4)
+        kind = (x_lo - z + 2 * y) % 4
+        source = mine_ref if kind < 2 else theirs_ref
+        out_ref[dest] = source[pl.ds(kind % 2 * 16, 16), :]
+
+
+def share(mine, theirs):
+    whole = pl.BlockSpec(memory_space=pltpu.VMEM)
+    return pl.pallas_call(
+        share_kernel,
+        out_shape=jax.ShapeDtypeStruct((32, 16, CH), jnp.bfloat16),
+        in_specs=[whole] * 2,
+        out_specs=whole,
+        name="share",
+    )(mine, theirs)
 
 
 def gather_chips(block, packed, early):
+    theirs = lax.ppermute(block, AXES, [(d, d ^ 64) for d in range(128)])
+    level = lax.all_to_all(share(block, theirs), "blk", split_axis=0, concat_axis=0, tiled=True)
     tiles = lax.all_to_all(packed, "blk", split_axis=0, concat_axis=0, tiled=True)
-    level = jnp.concatenate([block] + [take_from(block, o) for o in FIRST[1:]], axis=0)
-    level = jnp.concatenate([level] + [take_from(level, o) for o in SECOND[1:]], axis=0)
-    level, tiles = lax.optimization_barrier((level, tiles))
-    parts = [level[low * ROWS : high * ROWS] for _, low, high in LAST]
+    parts = [level[low:high] for _, _, low, high in LAST]
     small = take_from(parts[5], LAST[5][0])
-    parts[2], small, early = lax.optimization_barrier((parts[2], small, early))
+    parts[2], small, early, tiles = lax.optimization_barrier((parts[2], small, early, tiles))
     pieces = [take_from(part, last[0]) for part, last in zip(parts[:5], LAST)]
     tiles = tiles.reshape(32, 6, 40, 128).transpose(1, 0, 2, 3).reshape(6, CH, 128)
     pieces[0], tiles = lax.optimization_barrier((pieces[0], tiles))
@@ -69,17 +76,17 @@
 
 def assemble_kernel(slots, *refs):
     out = refs[-1]
-    spot = 0
-    for ref in refs[:-1]:
-        for row in range(ref.shape[0] // ROWS):
-            out[slots[spot]] = ref[pl.ds(row * ROWS, ROWS), :]
-            spot += 1
+    for h in range(32):
+        out[slots[0], pl.ds(h * 16, 16), :] = refs[0][h]
+    for ref, (_, kind, low, high) in zip(refs[1:-1], LAST):
+        for h in range(low, high):
+            out[slots[kind], pl.ds(h * 16, 16), :] = ref[h - low]
 
 
 def assemble(slots, pieces):
     return pl.pallas_call(
         assemble_kernel,
-        out_shape=jax.ShapeDtypeStruct((64, ROWS, CH), jnp.bfloat16),
+        out_shape=jax.ShapeDtypeStruct((4, 512, CH), jnp.bfloat16),
         in_specs=[pl.BlockSpec(memory_space=pltpu.SMEM)] + [pl.BlockSpec(memory_space=pltpu.VMEM)] * 7,
         out_specs=pl.BlockSpec(memory_space=pltpu.VMEM),
         compiler_params=pltpu.CompilerParams(vmem_limit_bytes=16 * 1024 * 1024),
@@ -88,10 +95,10 @@
 
 
 def shift_lanes(value, row_off, col_off):
-    amount = 32 * row_off + col_off
+    amount = 16 * row_off + col_off
     moved = pltpu.roll(value, (-amount) % LANES, 1) if amount else value
     lane = lax.broadcasted_iota(jnp.int32, (1, LANES), 1)
-    row = lane // 32 + row_off
+    row = lane // 16 % 32 + row_off
     col = lane % 8 + col_off
     inside = (row >= 0) & (row < 32) & (col >= 0) & (col < 8)
     return jnp.where(inside, moved, 0.0)
@@ -250,7 +257,7 @@
     spread = (tap_row == (tap_lane // 128) * 3 + (tap_lane % 128) // 40).astype(jnp.bfloat16)
     for c in range(2):
         scale = scale_ref[c]
-        pixels = pixels_ref[...].reshape(32, 2, 16, CH)[:, c].reshape(512, CH)
+        pixels = pixels_ref[pl.ds(c * 512, 512), :]
         tiles = jnp.concatenate([tiles_ref[c * 3 + a] for a in range(3)], axis=1)
         taps = jnp.dot(pixels, tiles, preferred_element_type=jnp.float32)
         by_col = shift_rows(taps[:, :128], -16) + taps[:, 128:256] + shift_rows(taps[:, 256:], 16)
@@ -370,7 +377,6 @@
     blk_here = lax.axis_index("blk")
     x_hi, core = client_here // 2, client_here % 2
     z, x_lo, y = blk_here // 8, (blk_here // 4) % 2, blk_here % 4
-    x = x_hi * 2 + x_lo
 
     counts = sample_count.astype(jnp.float32)
     all_scale = 1.0 / (8 * counts * 256)
@@ -392,13 +398,10 @@
     order = ((row // TAPS == col % 16) & (row % TAPS == col // 16)).astype(jnp.bfloat16)
     groups = jnp.stack([client_here, client_here ^ 2, client_here ^ 1, client_here ^ 3])
     group_scale = all_scale.reshape(4, 2)[groups]
-    img_scale = jnp.repeat(jnp.repeat(group_scale, 16, axis=1)[:, None, :], 32, axis=1).reshape(4, LANES)
+    img_scale = jnp.repeat(group_scale, 512, axis=1)
 
     masked = jnp.where(live[:, :, None, None, None], activations, jnp.zeros_like(activations))
-    offs = np.array(SOURCES, np.int32)
-    src_x, src_y, src_z = (x + offs[:, 0]) % 4, (y + offs[:, 1]) % 4, (z + offs[:, 2]) % 4
-    away = (src_x // 2 != x_hi).astype(jnp.int32)
-    slots = (away * 32 + src_z * 8 + (src_x % 2) * 4 + src_y).astype(jnp.int32)
+    slots = ((x_lo - z + 2 * y) % 4 + jnp.arange(4, dtype=jnp.int32)) % 4
     pieces, tiles, early = gather_chips(masked.reshape(ROWS, CH), packed, (pick, order, img_scale, slots))
     pick, order, img_scale, slots = early
     own = assemble(slots, pieces)

time: 141 us -> 143 us (1.014)
  waiting for transfers between devices: 34.5 us -> 45.1 us
  starting transfers between devices: 45.2 us -> 37.7 us
  other arithmetic: 8.56 us -> 4.07 us
  Pallas kernels: 41.5 us -> 44.9 us
    ppermute x12 -> x6, starting transfers between devices: 27.1 us -> 8.31 us  [take_from(): return lax.ppermute(value, AXES, pairs)]
    all_to_all x0 -> x1, waiting for transfers between devices: none -> 12.1 us  [gather_chips(): lax.all_to_all(share(block, theirs), 'blk', split_axis=0, concat_axis=0,...]
    all_to_all x0 -> x1, starting transfers between devices: none -> 9.2 us  [gather_chips(): lax.all_to_all(share(block, theirs), 'blk', split_axis=0, concat_axis=0,...]
    ppermute x0 -> x1, starting transfers between devices: none -> 3.65 us  [gather_chips(): theirs = lax.ppermute(block, AXES, [(d, d ^ 64) for d in range(128)])]
    pallas_call x1 -> x2, Pallas kernels: 3.21 us -> 6.56 us  [the longest x1 4.48 us: assemble(): pl.pallas_call(assemble_kernel, out_shape=jax.ShapeDtypeStruct((4, 512, C...]
    ppermute x1, starting transfers between devices: 6.01 us -> 2.87 us  [body(): other = lax.ppermute(own, AXES, [(d, d ^ 32) for d in range(128)])]
    ppermute x12 -> x6, waiting for transfers between devices: 34.5 us -> 31.9 us  [take_from(): return lax.ppermute(value, AXES, pairs)]
    broadcast_in_dim x3 -> x0, local copies, waits for them, and re-layouts: 2.24 us -> none  [the longest x2 2.17 us: body(): jnp.repeat(jnp.repeat(group_scale, 16, axis=1)[:, None, :], 32, axis=1)]
  transfers between devices with their start and end apart: 15 -> 11, of which waited for: 8 -> 8; matrix products, arithmetic and copies ran while one was open for 10% -> 6% of each run, Pallas kernels for 26% -> 26%
where the time goes in v8:
time: 143 us
  waiting for transfers between devices  45.1 us (32%)
  Pallas kernels  44.9 us (31%)
  starting transfers between devices  37.7 us (26%)
  local copies, waits for them, and re-layouts  9.95 us (7%)
  other arithmetic  4.07 us (3%)
    ppermute x6, waiting for transfers between devices, take_from(): return lax.ppermute(value, AXES, pairs)  31.9 us
    pallas_call x1, Pallas kernels, gram(): pl.pallas_call(gram_kernel, out_shape=(jax.ShapeDtypeStruct((90, 11520),...  24.4 us
    all_to_all x1, waiting for transfers between devices, gather_chips(): lax.all_to_all(share(block, theirs), 'blk', split_axis=0, concat_axis=0,...  12.1 us
    all_to_all x1, starting transfers between devices, gather_chips(): lax.all_to_all(share(block, theirs), 'blk', split_axis=0, concat_axis=0,...  9.2 us
    pallas_call x1, Pallas kernels, rhs_part(): pl.pallas_call(rhs_kernel, out_shape=jax.ShapeDtypeStruct((128, 32, 128),...  8.8 us
    ppermute x6, starting transfers between devices, take_from(): return lax.ppermute(value, AXES, pairs)  8.31 us
    all_to_all x1, starting transfers between devices, gather_chips(): lax.all_to_all(packed, 'blk', split_axis=0, concat_axis=0, tiled=True)  7.21 us
    all_to_all x1, starting transfers between devices, body(): lax.all_to_all(part, ('blk', 'client'), split_axis=0, concat_axis=0, tile...  6.48 us
  transfers between devices with their start and end apart: 11, of which 8 were waited for; matrix products, arithmetic and copies ran while one was open for 6% of the time, Pallas kernels for 26%

profile of v8, /device:TPU:1, one launch (start us, length us, event | category | flops | bytes accessed | tf_op | source)
XLA Modules:
  0.0 142.6 jit_solution(877714029774385920)
XLA Ops:
  2.4 3.7 %collective-permute-start = (bf16[32,1280]{1,0:T(8,128)(2,1)S(1)}, bf16[32,1280]{1,0:T(8,128)(2,1)S(1)}, u32[]{:S(2)}, u32[]{:S(2)}) collective-permute-start(bf16[32,1280]{1,0:T(8,128)(2,1)S(1)} %bitcast.19), channel_id=1, source_target_pairs={{0,64},{1,65},{2,66},{3,67},{4,68},{5,69},{6,70},{7,71},{8,72},{9,... | collective-permute-start | bytes 245768 | tf_op jit(solution)/shard_map/ppermute | solution.py:65
  6.8 1.1 collective-permute-done.theirs_ref
  8.5 2.1 %share.1 = bf16[32,16,1280]{2,1,0:T(8,128)(2,1)} custom-call(bf16[32,1280]{1,0:T(8,128)(2,1)} %bitcast.20, bf16[32,1280]{1,0:T(8,128)(2,1)} %copy-done.7), custom_call_target="tpu_custom_call" | custom-call | tf_op jit(solution)/shard_map/share/pallas_call | solution.py:55
  10.6 9.2 %all-to-all-start = ((bf16[32,16,1280]{2,1,0:T(8,128)(2,1)}), bf16[32,16,1280]{2,1,0:T(8,128)(2,1)S(1)}, u32[]{:S(2)}, u32[]{:S(2)}) async-start(bf16[32,16,1280]{2,1,0:T(8,128)(2,1)} %share.1), calls=%async_computation | async-start | bytes 2621440 | tf_op jit(solution)/shard_map/all_to_all | solution.py:66
  21.3 3.5 %pack.1 = bf16[32,240,128]{2,1,0:T(8,128)(2,1)} custom-call(bf16[2,360,1280]{2,1,0:T(8,128)(2,1)S(1)} %copy-done, bf16[360,360]{1,0:T(8,128)(2,1)S(1)} %fusion.6.order_ref), custom_call_target="tpu_custom_call" | custom-call | flops 1000000000 | bytes 6000000 | tf_op jit(solution)/shard_map/pack/pallas_call | solution.py:224
  24.9 12.1 %all-to-all-done.refs_0_ = bf16[32,16,1280]{2,1,0:T(8,128)(2,1)S(1)} async-done(((bf16[32,16,1280]{2,1,0:T(8,128)(2,1)}), bf16[32,16,1280]{2,1,0:T(8,128)(2,1)S(1)}, u32[]{:S(2)}, u32[]{:S(2)}) %all-to-all-start) | async-done | bytes 1310752 | tf_op jit(solution)/shard_map/all_to_all | solution.py:66
  37.0 7.2 %all-to-all-start.1 = ((bf16[32,240,128]{2,1,0:T(8,128)(2,1)}), bf16[32,240,128]{2,1,0:T(8,128)(2,1)S(1)}, u32[]{:S(2)}, u32[]{:S(2)}) async-start(bf16[32,240,128]{2,1,0:T(8,128)(2,1)} %pack.1), calls=%async_computation.1 | async-start | bytes 3932160 | tf_op jit(solution)/shard_map/all_to_all | solution.py:67
  46.4 1.3 collective-permute-start.1
  47.7 1.0 slice.23
  48.7 1.4 %collective-permute-start.6 = (bf16[24,16,1280]{2,1,0:T(8,128)(2,1)}, bf16[24,16,1280]{2,1,0:T(8,128)(2,1)}, u32[]{:S(2)}, u32[]{:S(2)}) collective-permute-start(bf16[24,16,1280]{2,1,0:T(8,128)(2,1)} %slice.23), channel_id=1, source_target_pairs={{1,0},{2,1},{3,2},{0,3},{5,4},{6,5},{7,6},{4,7},{9,8},{10,9},{11,1... | collective-permute-start | bytes 2949128 | tf_op jit(solution)/shard_map/ppermute | solution.py:38
  50.1 1.2 fusion.24
  51.3 2.5 %collective-permute-start.5 = (bf16[16,16,1280]{2,1,0:T(8,128)(2,1)}, bf16[16,16,1280]{2,1,0:T(8,128)(2,1)}, u32[]{:S(2)}, u32[]{:S(2)}) collective-permute-start(bf16[16,16,1280]{2,1,0:T(8,128)(2,1)} %get-tuple-element.24), channel_id=1, source_target_pairs={{8,0},{9,1},{10,2},{11,3},{12,4},{13,5},{14,6},{15,7},{16,8},{17,9... | collective-permute-start | bytes 1966088 | tf_op jit(solution)/shard_map/ppermute | solution.py:38
  53.8 2.5 %collective-permute-start.2 = (bf16[16,16,1280]{2,1,0:T(8,128)(2,1)}, bf16[16,16,1280]{2,1,0:T(8,128)(2,1)}, u32[]{:S(2)}, u32[]{:S(2)}) collective-permute-start(bf16[16,16,1280]{2,1,0:T(8,128)(2,1)} %get-tuple-element.16), channel_id=1, source_target_pairs={{4,0},{5,1},{6,2},{7,3},{64,4},{65,5},{66,6},{67,7},{12,8},{13,9},... | collective-permute-start | bytes 1966088 | tf_op jit(solution)/shard_map/ppermute | solution.py:38
  56.3 19.4 %collective-permute-done.1.refs_6_ = bf16[8,16,1280]{2,1,0:T(8,128)(2,1)S(1)} collective-permute-done((bf16[8,16,1280]{2,1,0:T(8,128)(2,1)S(1)}, bf16[8,16,1280]{2,1,0:T(8,128)(2,1)S(1)}, u32[]{:S(2)}, u32[]{:S(2)}) %collective-permute-start.1) | collective-permute-done | bytes 327712 | tf_op jit(solution)/shard_map/ppermute | solution.py:38
  77.7 1.9 %copy.6 = bf16[32,6,40,128]{3,2,0,1:T(8,128)(2,1)S(1)} copy(bf16[32,6,40,128]{3,2,1,0:T(8,128)(2,1)} %bitcast.18) | data formatting | bytes 3932160 | tf_op jit(solution)/shard_map/reshape | solution.py:72
  80.5 1.9 %collective-permute-done.5.refs_4_ = bf16[16,16,1280]{2,1,0:T(8,128)(2,1)} collective-permute-done((bf16[16,16,1280]{2,1,0:T(8,128)(2,1)}, bf16[16,16,1280]{2,1,0:T(8,128)(2,1)}, u32[]{:S(2)}, u32[]{:S(2)}) %collective-permute-start.5) | collective-permute-done | bytes 655392 | tf_op jit(solution)/shard_map/ppermute | solution.py:38
  83.1 4.7 %collective-permute-done.6.refs_5_ = bf16[24,16,1280]{2,1,0:T(8,128)(2,1)} collective-permute-done((bf16[24,16,1280]{2,1,0:T(8,128)(2,1)}, bf16[24,16,1280]{2,1,0:T(8,128)(2,1)}, u32[]{:S(2)}, u32[]{:S(2)}) %collective-permute-start.6) | collective-permute-done | bytes 983072 | tf_op jit(solution)/shard_map/ppermute | solution.py:38
  87.8 4.3 %collective-permute-done.4.refs_3_ = bf16[16,16,1280]{2,1,0:T(8,128)(2,1)S(1)} collective-permute-done((bf16[16,16,1280]{2,1,0:T(8,128)(2,1)}, bf16[16,16,1280]{2,1,0:T(8,128)(2,1)S(1)}, u32[]{:S(2)}, u32[]{:S(2)}) %collective-permute-start.4) | collective-permute-done | bytes 655392 | tf_op jit(solution)/shard_map/ppermute | solution.py:38
  92.1 4.5 %assemble.1 = bf16[4,512,1280]{2,1,0:T(8,128)(2,1)} custom-call(s32[4]{0:T(128)S(1)} %and_select_fusion.slots, bf16[32,16,1280]{2,1,0:T(8,128)(2,1)S(1)} %all-to-all-done.refs_0_, bf16[16,16,1280]{2,1,0:T(8,128)(2,1)} %collective-permute-done.2.refs_1_, bf16[16,16,1280]{2,1,0:T(8,128)(2,1)} %collective-permute-done.3.refs_2_, ...), custom_call_target="tpu_custom_call" | custom-call | tf_op jit(solution)/shard_map/assemble/pallas_call | solution.py:87
  96.6 2.9 %collective-permute-start.7 = (bf16[4,512,1280]{2,1,0:T(8,128)(2,1)}, bf16[4,512,1280]{2,1,0:T(8,128)(2,1)}, u32[]{:S(2)}, u32[]{:S(2)}) collective-permute-start(bf16[4,512,1280]{2,1,0:T(8,128)(2,1)} %assemble.1), channel_id=1, source_target_pairs={{0,32},{1,33},{2,34},{3,35},{4,36},{5,37},{6,38},{7,39},{8,40},{9,... | collective-permute-start | bytes 15728648 | tf_op jit(solution)/shard_map/ppermute | solution.py:408
  99.6 8.8 %rhs_part.1 = bf16[128,32,128]{2,1,0:T(8,128)(2,1)S(1)} custom-call(f32[2]{0:T(128)S(1)} %dynamic_slice.7.scale_ref, bf16[2048,1280]{1,0:T(8,128)(2,1)} %bitcast.10.own_hbm.pixels_ref, bf16[6,1280,128]{2,1,0:T(8,128)(2,1)S(1)} %bitcast.17), custom_call_target="tpu_custom_call" | custom-call | flops 4000000000 | bytes 8000000 | tf_op jit(solution)/shard_map/rhs_part/pallas_call | solution.py:314
  109.4 6.5 %all-to-all-start.2 = ((bf16[128,32,128]{2,1,0:T(8,128)(2,1)}), bf16[128,32,128]{2,1,0:T(8,128)(2,1)S(1)}, u32[]{:S(2)}, u32[]{:S(2)}) async-start(bf16[128,32,128]{2,1,0:T(8,128)(2,1)} %copy-done.1), calls=%async_computation.2 | async-start | bytes 2097152 | tf_op jit(solution)/shard_map/all_to_all | solution.py:412
  115.9 24.4 %gram.1 = (f32[90,11520]{1,0:T(8,128)}, f32[8,128]{1,0:T(8,128)}) custom-call(s32[1]{0:T(128)} %bitcast.first_ref, bf16[2048,1280]{1,0:T(8,128)(2,1)} %bitcast.10.own_hbm.pixels_ref, bf16[2048,1280]{1,0:T(8,128)(2,1)} %bitcast.11.other_hbm, bf16[16,1280]{1,0:T(8,128)(2,1)} %fusion.11.pick_ref, bf16[96,144]{1,0:T(8,128)(2,1)} %fusion.9.order_ref, ...), custom_call_target="tpu_custom_call" | custom-call | flops 20000000000 | bytes 20000000 | tf_op jit(solution)/shard_map/gram/pallas_call | solution.py:183
  141.0 1.6 %finish.1 = f32[90,1280]{1,0:T(8,128)} custom-call(bf16[128,32,128]{2,1,0:T(8,128)(2,1)S(1)} %all-to-all-done.2.sent_ref, f32[8,128]{1,0:T(8,128)S(1)} %copy-done.4), custom_call_target="tpu_custom_call" | custom-call | tf_op jit(solution)/shard_map/finish/pallas_call | solution.py:364
  (52 shorter events, 12.1 us)
Async XLA Ops:
  2.4 5.5 %copy-start.6 = (bf16[2,2,1,8,1280]{4,3,2,1,0:T(8,128)(2,1)}, bf16[2,2,1,8,1280]{4,3,2,1,0:T(8,128)(2,1)S(1)}, u32[]{:S(2)}) copy-start(bf16[2,2,1,8,1280]{4,3,2,1,0:T(8,128)(2,1)S(1)} %broadcast_select_fusion) | copy-start | bytes 245764
  2.4 5.5 %collective-permute-start = (bf16[32,1280]{1,0:T(8,128)(2,1)S(1)}, bf16[32,1280]{1,0:T(8,128)(2,1)S(1)}, u32[]{:S(2)}, u32[]{:S(2)}) collective-permute-start(bf16[32,1280]{1,0:T(8,128)(2,1)S(1)} %bitcast.19), channel_id=1, source_target_pairs={{0,64},{1,65},{2,66},{3,67},{4,68},{5,69},{6,70},{7,71},{8,72},{9,... | collective-permute-start | bytes 245768 | tf_op jit(solution)/shard_map/ppermute | solution.py:65
  6.8 14.5 %copy-start = (bf16[2,360,1280]{2,1,0:T(8,128)(2,1)S(1)}, bf16[2,360,1280]{2,1,0:T(8,128)(2,1)}, u32[]{:S(2)}) copy-start(bf16[2,360,1280]{2,1,0:T(8,128)(2,1)} %weights_ref.1) | copy-start | bytes 5529604
  7.9 0.6 copy-start.7
  10.6 26.4 %all-to-all-start = ((bf16[32,16,1280]{2,1,0:T(8,128)(2,1)}), bf16[32,16,1280]{2,1,0:T(8,128)(2,1)S(1)}, u32[]{:S(2)}, u32[]{:S(2)}) async-start(bf16[32,16,1280]{2,1,0:T(8,128)(2,1)} %share.1), calls=%async_computation | async-start | bytes 2621440 | tf_op jit(solution)/shard_map/all_to_all | solution.py:66
  37.0 39.4 %all-to-all-start.1 = ((bf16[32,240,128]{2,1,0:T(8,128)(2,1)}), bf16[32,240,128]{2,1,0:T(8,128)(2,1)S(1)}, u32[]{:S(2)}, u32[]{:S(2)}) async-start(bf16[32,240,128]{2,1,0:T(8,128)(2,1)} %pack.1), calls=%async_computation.1 | async-start | bytes 3932160 | tf_op jit(solution)/shard_map/all_to_all | solution.py:67
  46.4 29.3 %collective-permute-start.1 = (bf16[8,16,1280]{2,1,0:T(8,128)(2,1)S(1)}, bf16[8,16,1280]{2,1,0:T(8,128)(2,1)S(1)}, u32[]{:S(2)}, u32[]{:S(2)}) collective-permute-start(bf16[8,16,1280]{2,1,0:T(8,128)(2,1)S(1)} %slice.21), channel_id=1, source_target_pairs={{3,0},{0,1},{1,2},{2,3},{7,4},{4,5},{5,6},{6,7},{11,8},{8,9},{9,10... | collective-permute-start | bytes 983048 | tf_op jit(solution)/shard_map/ppermute | solution.py:38
  48.7 39.2 %collective-permute-start.6 = (bf16[24,16,1280]{2,1,0:T(8,128)(2,1)}, bf16[24,16,1280]{2,1,0:T(8,128)(2,1)}, u32[]{:S(2)}, u32[]{:S(2)}) collective-permute-start(bf16[24,16,1280]{2,1,0:T(8,128)(2,1)} %slice.23), channel_id=1, source_target_pairs={{1,0},{2,1},{3,2},{0,3},{5,4},{6,5},{7,6},{4,7},{9,8},{10,9},{11,1... | collective-permute-start | bytes 2949128 | tf_op jit(solution)/shard_map/ppermute | solution.py:38
  51.3 31.1 %collective-permute-start.5 = (bf16[16,16,1280]{2,1,0:T(8,128)(2,1)}, bf16[16,16,1280]{2,1,0:T(8,128)(2,1)}, u32[]{:S(2)}, u32[]{:S(2)}) collective-permute-start(bf16[16,16,1280]{2,1,0:T(8,128)(2,1)} %get-tuple-element.24), channel_id=1, source_target_pairs={{8,0},{9,1},{10,2},{11,3},{12,4},{13,5},{14,6},{15,7},{16,8},{17,9... | collective-permute-start | bytes 1966088 | tf_op jit(solution)/shard_map/ppermute | solution.py:38
  53.8 29.3 %collective-permute-start.3 = (bf16[16,16,1280]{2,1,0:T(8,128)(2,1)}, bf16[16,16,1280]{2,1,0:T(8,128)(2,1)}, u32[]{:S(2)}, u32[]{:S(2)}) collective-permute-start(bf16[16,16,1280]{2,1,0:T(8,128)(2,1)} %get-tuple-element.24), channel_id=1, source_target_pairs={{24,0},{25,1},{26,2},{27,3},{28,4},{29,5},{30,6},{31,7},{0,8},{1,9... | collective-permute-start | bytes 1966088 | tf_op jit(solution)/shard_map/ppermute | solution.py:38
  53.8 26.8 %collective-permute-start.2 = (bf16[16,16,1280]{2,1,0:T(8,128)(2,1)}, bf16[16,16,1280]{2,1,0:T(8,128)(2,1)}, u32[]{:S(2)}, u32[]{:S(2)}) collective-permute-start(bf16[16,16,1280]{2,1,0:T(8,128)(2,1)} %get-tuple-element.16), channel_id=1, source_target_pairs={{4,0},{5,1},{6,2},{7,3},{64,4},{65,5},{66,6},{67,7},{12,8},{13,9},... | collective-permute-start | bytes 1966088 | tf_op jit(solution)/shard_map/ppermute | solution.py:38
  75.7 0.7 copy-start.2
  76.4 1.3 copy-start.5
  76.4 15.7 %collective-permute-start.4 = (bf16[16,16,1280]{2,1,0:T(8,128)(2,1)}, bf16[16,16,1280]{2,1,0:T(8,128)(2,1)S(1)}, u32[]{:S(2)}, u32[]{:S(2)}) collective-permute-start(bf16[16,16,1280]{2,1,0:T(8,128)(2,1)} %get-tuple-element.16), channel_id=1, source_target_pairs={{68,0},{69,1},{70,2},{71,3},{0,4},{1,5},{2,6},{3,7},{76,8},{77,9},... | collective-permute-start | bytes 1966088 | tf_op jit(solution)/shard_map/ppermute | solution.py:38
  77.7 14.4 %copy-start.3 = (bf16[8,16,1280]{2,1,0:T(8,128)(2,1)S(1)}, bf16[8,16,1280]{2,1,0:T(8,128)(2,1)}, u32[]{:S(2)}) copy-start(bf16[8,16,1280]{2,1,0:T(8,128)(2,1)} %copy-done.2) | copy-start | bytes 983044
  96.6 19.2 %collective-permute-start.7 = (bf16[4,512,1280]{2,1,0:T(8,128)(2,1)}, bf16[4,512,1280]{2,1,0:T(8,128)(2,1)}, u32[]{:S(2)}, u32[]{:S(2)}) collective-permute-start(bf16[4,512,1280]{2,1,0:T(8,128)(2,1)} %assemble.1), channel_id=1, source_target_pairs={{0,32},{1,33},{2,34},{3,35},{4,36},{5,37},{6,38},{7,39},{8,40},{9,... | collective-permute-start | bytes 15728648 | tf_op jit(solution)/shard_map/ppermute | solution.py:408
  108.4 1.0 copy-start.1
  109.4 30.9 %all-to-all-start.2 = ((bf16[128,32,128]{2,1,0:T(8,128)(2,1)}), bf16[128,32,128]{2,1,0:T(8,128)(2,1)S(1)}, u32[]{:S(2)}, u32[]{:S(2)}) async-start(bf16[128,32,128]{2,1,0:T(8,128)(2,1)} %copy-done.1), calls=%async_computation.2 | async-start | bytes 2097152 | tf_op jit(solution)/shard_map/all_to_all | solution.py:412
  140.3 0.7 copy-start.4

commit v9 on v7

--- a/solution.py
+++ b/solution.py
@@ -46,7 +46,7 @@
 FIRST = [tuple(k * s % 4 for s in STEP) for k in range(4)]
 SECOND = [(0, 0, 0), (1, 1, 3), (0, 2, 0), (3, 3, 1)]
 LEVEL = [vec_add(g, f) for g in SECOND for f in FIRST]
-LAST = [((1, 0, 0), 0, 8), ((0, 0, 3), 8, 16), ((3, 0, 0), 0, 8), ((0, 0, 1), 8, 16), ((0, 1, 0), 0, 10), ((0, 3, 0), 2, 8)]
+LAST = [((1, 0, 0), 0, 8), ((0, 0, 3), 8, 16), ((3, 0, 0), 0, 8), ((0, 0, 1), 8, 16), ((0, 1, 0), 0, 12), ((0, 3, 0), 4, 8)]
 SOURCES = list(LEVEL)
 for away, low, high in LAST:
     SOURCES += [vec_add(away, o) for o in LEVEL[low:high]]
@@ -97,7 +97,7 @@
     return jnp.where(inside, moved, 0.0)
 
 
-def gram_kernel(first_ref, own_hbm, other_hbm, pick_ref, order_ref, scale_ref, out_ref, token_ref, left, acc, staged, pixels, sems, loads):
+def gram_kernel(first_ref, own_hbm, other_hbm, pick_ref, order_ref, scale_ref, out_ref, left, acc, staged, pixels, sems, loads):
     copies = []
     for group in range(4):
         source = own_hbm if group < 2 else other_hbm
@@ -105,7 +105,6 @@
         target = pixels.at[pl.ds(group * LANES, LANES)]
         copies.append(pltpu.make_async_copy(source.at[rows], target, loads.at[group]))
         copies[-1].start()
-    del token_ref
     pick = pick_ref[...]
     order = order_ref[...]
     for group in range(4):
@@ -175,9 +174,9 @@
     held = pl.BlockSpec(memory_space=pltpu.HBM)
     return pl.pallas_call(
         gram_kernel,
-        out_shape=(jax.ShapeDtypeStruct((90, 11520), jnp.float32), jax.ShapeDtypeStruct((8, 128), jnp.float32)),
+        out_shape=jax.ShapeDtypeStruct((90, 11520), jnp.float32),
         in_specs=[pl.BlockSpec(memory_space=pltpu.SMEM), held, held] + [whole] * 3,
-        out_specs=(held, held),
+        out_specs=held,
         scratch_shapes=[
             pltpu.VMEM((TAPS * MPAD, 4 * LANES), jnp.bfloat16),
             pltpu.VMEM((TAPS * MPAD, CH), jnp.float32),
@@ -192,10 +191,17 @@
     )(first, own, other, pick, order, scale)
 
 
-def pack_kernel(weights_ref, order_ref, out_ref, ordered):
+def pack_kernel(weights_hbm, out_ref, weights, ordered, loads):
+    copies = [pltpu.make_async_copy(weights_hbm.at[c], weights.at[c], loads.at[c]) for c in range(2)]
+    for copy in copies:
+        copy.start()
     lane = lax.broadcasted_iota(jnp.int32, (1, 128), 1)
+    row = lax.broadcasted_iota(jnp.int32, (360, 360), 0)
+    col = lax.broadcasted_iota(jnp.int32, (360, 360), 1)
+    order = (col == (row % 40) * TAPS + (row // 40) % 3 * 3 + row // 120).astype(jnp.bfloat16)
     for c in range(2):
-        ordered[...] = jnp.dot(order_ref[...], weights_ref[c], preferred_element_type=jnp.float32)
+        copies[c].wait()
+        ordered[...] = jnp.dot(order, weights[c], preferred_element_type=jnp.float32)
         for dest in range(32):
             tile, off = divmod(dest * 40, 128)
             total = jnp.zeros((120, 128), jnp.float32)
@@ -212,18 +218,21 @@
             out_ref[dest, pl.ds(c * 120, 120), :] = total.astype(jnp.bfloat16)
 
 
-def pack(weights, order):
-    whole = pl.BlockSpec(memory_space=pltpu.VMEM)
+def pack(weights):
     return pl.pallas_call(
         pack_kernel,
         out_shape=jax.ShapeDtypeStruct((32, 240, 128), jnp.bfloat16),
-        in_specs=[whole] * 2,
-        out_specs=whole,
-        scratch_shapes=[pltpu.VMEM((360, CH), jnp.float32)],
-        compiler_params=pltpu.CompilerParams(vmem_limit_bytes=24 * 1024 * 1024),
+        in_specs=[pl.BlockSpec(memory_space=pltpu.HBM)],
+        out_specs=pl.BlockSpec(memory_space=pltpu.VMEM),
+        scratch_shapes=[
+            pltpu.VMEM((2, 360, CH), jnp.bfloat16),
+            pltpu.VMEM((360, CH), jnp.float32),
+            pltpu.SemaphoreType.DMA((2,)),
+        ],
+        compiler_params=pltpu.CompilerParams(vmem_limit_bytes=63 * 1024 * 1024),
         cost_estimate=pl.CostEstimate(flops=1_000_000_000, bytes_accessed=6_000_000, transcendentals=0),
         name="pack",
-    )(weights, order)
+    )(weights)
 
 
 def shift_rows(value, amount):
@@ -284,12 +293,14 @@
             diag.append(jnp.sum(jnp.where(col > 0, kept, 0.0), axis=0, keepdims=True))
         diag = jnp.concatenate(diag + [jnp.zeros((7, CH), jnp.float32)], axis=0)
         diag = diag * (scale * (1.0 - keep_off))
-        wide = None
+        heads = []
         for _ in range(3):
-            head = diag.astype(jnp.bfloat16)
-            part = lax.dot_general(head, spread, (((0,), (0,)), ((), ())), preferred_element_type=jnp.float32)
-            wide = part if wide is None else wide + part
-            diag = diag - head.astype(jnp.float32)
+            heads.append(diag.astype(jnp.bfloat16))
+            diag = diag - heads[-1].astype(jnp.float32)
+        wide = lax.dot_general(
+            jnp.concatenate(heads, axis=0), jnp.concatenate([spread] * 3, axis=0),
+            (((0,), (0,)), ((), ())), preferred_element_type=jnp.float32,
+        )
         value = keep_off * cross + wide * tiles.astype(jnp.float32)
         rhs[...] = value if c == 0 else rhs[...] + value
     zeros = jnp.zeros((2, 128), jnp.float32)
@@ -314,7 +325,7 @@
             pltpu.VMEM((CH, 384), jnp.float32),
             pltpu.VMEM((128, 32, 128), jnp.float32),
         ],
-        compiler_params=pltpu.CompilerParams(vmem_limit_bytes=48 * 1024 * 1024),
+        compiler_params=pltpu.CompilerParams(vmem_limit_bytes=62 * 1024 * 1024),
         cost_estimate=pl.CostEstimate(flops=4_000_000_000, bytes_accessed=8_000_000, transcendentals=0),
         name="rhs_part",
     )(scale, pixels, tiles)
@@ -360,7 +371,7 @@
         in_specs=[whole, pl.BlockSpec(memory_space=pltpu.HBM)],
         out_specs=whole,
         scratch_shapes=[pltpu.VMEM((96, CH), jnp.float32)],
-        compiler_params=pltpu.CompilerParams(vmem_limit_bytes=16 * 1024 * 1024),
+        compiler_params=pltpu.CompilerParams(vmem_limit_bytes=62 * 1024 * 1024),
         name="finish",
     )(sent, after)
 
@@ -377,10 +388,7 @@
     mine = lax.dynamic_slice_in_dim(sample_count, client_here * 2, 2)
     my_scale = lax.dynamic_slice_in_dim(all_scale, client_here * 2, 2)
 
-    row = lax.broadcasted_iota(jnp.int32, (360, 360), 0)
-    col = lax.broadcasted_iota(jnp.int32, (360, 360), 1)
-    tap_order = (col == (row % 40) * TAPS + (row // 40) % 3 * 3 + row // 120).astype(jnp.bfloat16)
-    packed = pack(client_weights, tap_order)
+    packed = pack(client_weights)
 
     live = lax.broadcasted_iota(jnp.int32, (2, 2), 1) < mine[:, None]
     first_channel = blk_here * 40 + client_here * OWN
@@ -408,11 +416,11 @@
     part = rhs_part(my_scale, own_rows, tiles)
     sent = lax.all_to_all(part, ("blk", "client"), split_axis=0, concat_axis=0, tiled=True)
 
-    gram_out, token = gram(
+    gram_out = gram(
         jnp.reshape(first_channel * TAPS, (1,)), own_rows, other.reshape(2048, CH),
         pick, order, img_scale,
     )
-    return gram_out, finish(sent, token)
+    return gram_out, finish(sent, gram_out)
 
 
 def solution(mesh):

time: 141 us -> 138 us (0.979)
  starting transfers between devices: 45.2 us -> 41 us
  Pallas kernels: 41.5 us -> 43.8 us
  local copies, waits for them, and re-layouts: 9.98 us -> 8.11 us
    all_to_all x1, starting transfers between devices: 7.02 us -> 4.25 us  [body(): lax.all_to_all(part, ('blk', 'client'), split_axis=0, concat_axis=0, tile...]
    unnamed x14 -> x8, local copies, waits for them, and re-layouts: 4.13 us -> 1.94 us
    pallas_call x1, Pallas kernels: 3.49 us -> 5.31 us  [pack(): pl.pallas_call(pack_kernel, out_shape=jax.ShapeDtypeStruct((32, 240, 128)...]
  transfers between devices with their start and end apart: 15 -> 15, of which waited for: 8 -> 7; matrix products, arithmetic and copies ran while one was open for 10% -> 10% of each run, Pallas kernels for 26% -> 28%
where the time goes in v9:
time: 138 us; the launch traced here: 137 us
  Pallas kernels  43.8 us (32%)
  starting transfers between devices  41 us (30%)
  waiting for transfers between devices  35.5 us (26%)
  local copies, waits for them, and re-layouts  8.11 us (6%)
  other arithmetic  7.85 us (6%)
    ppermute x12, waiting for transfers between devices, take_from(): return lax.ppermute(value, AXES, pairs)  35.5 us
    ppermute x12, starting transfers between devices, take_from(): return lax.ppermute(value, AXES, pairs)  26.1 us
    pallas_call x1, Pallas kernels, gram(): pl.pallas_call(gram_kernel, out_shape=jax.ShapeDtypeStruct((90, 11520), j...  24.4 us
    pallas_call x1, Pallas kernels, rhs_part(): pl.pallas_call(rhs_kernel, out_shape=jax.ShapeDtypeStruct((128, 32, 128),...  8.03 us
    ppermute x1, starting transfers between devices, body(): other = lax.ppermute(own, AXES, [(d, d ^ 32) for d in range(128)])  5.64 us
    pallas_call x1, Pallas kernels, pack(): pl.pallas_call(pack_kernel, out_shape=jax.ShapeDtypeStruct((32, 240, 128)...  5.31 us
    all_to_all x1, starting transfers between devices, gather_chips(): lax.all_to_all(packed, 'blk', split_axis=0, concat_axis=0, tiled=True)  5.08 us
    all_to_all x1, starting transfers between devices, body(): lax.all_to_all(part, ('blk', 'client'), split_axis=0, concat_axis=0, tile...  4.25 us
  transfers between devices with their start and end apart: 15, of which 7 were waited for; matrix products, arithmetic and copies ran while one was open for 10% of the time, Pallas kernels for 28%

profile of v9, /device:TPU:1, one launch (start us, length us, event | category | flops | bytes accessed | tf_op | source)
XLA Modules:
  0.0 137.2 jit_solution(92641190933140390)
XLA Ops:
  2.4 3.5 %collective-permute-start.2 = (bf16[32,1280]{1,0:T(8,128)(2,1)S(1)}, bf16[32,1280]{1,0:T(8,128)(2,1)S(1)}, u32[]{:S(2)}, u32[]{:S(2)}) collective-permute-start(bf16[32,1280]{1,0:T(8,128)(2,1)S(1)} %bitcast.16), channel_id=1, source_target_pairs={{92,0},{93,1},{94,2},{95,3},{24,4},{25,5},{26,6},{27,7},{68,8},{69... | collective-permute-start | bytes 245768 | tf_op jit(solution)/shard_map/ppermute | solution.py:38
  5.9 5.5 %collective-permute-start.1 = (bf16[32,1280]{1,0:T(8,128)(2,1)S(1)}, bf16[32,1280]{1,0:T(8,128)(2,1)S(1)}, u32[]{:S(2)}, u32[]{:S(2)}) collective-permute-start(bf16[32,1280]{1,0:T(8,128)(2,1)S(1)} %bitcast.17), channel_id=1, source_target_pairs={{80,0},{81,1},{82,2},{83,3},{84,4},{85,5},{86,6},{87,7},{88,8},{89... | collective-permute-start | bytes 245768 | tf_op jit(solution)/shard_map/ppermute | solution.py:38
  11.3 1.6 %collective-permute-start = (bf16[32,1280]{1,0:T(8,128)(2,1)S(1)}, bf16[32,1280]{1,0:T(8,128)(2,1)}, u32[]{:S(2)}, u32[]{:S(2)}) collective-permute-start(bf16[32,1280]{1,0:T(8,128)(2,1)S(1)} %bitcast.18), channel_id=1, source_target_pairs={{12,0},{13,1},{14,2},{15,3},{72,4},{73,5},{74,6},{75,7},{20,8},{21... | collective-permute-start | bytes 245768 | tf_op jit(solution)/shard_map/ppermute | solution.py:38
  12.9 5.3 %pack.1 = bf16[32,240,128]{2,1,0:T(8,128)(2,1)} custom-call(bf16[2,360,1280]{2,1,0:T(8,128)(2,1)} %weights_hbm.1), custom_call_target="tpu_custom_call" | custom-call | flops 1000000000 | bytes 6000000 | tf_op jit(solution)/shard_map/pack/pallas_call | solution.py:222
  18.3 5.1 %all-to-all-start = ((bf16[32,240,128]{2,1,0:T(8,128)(2,1)}), bf16[32,240,128]{2,1,0:T(8,128)(2,1)S(1)}, u32[]{:S(2)}, u32[]{:S(2)}) async-start(bf16[32,240,128]{2,1,0:T(8,128)(2,1)} %pack.1), calls=%async_computation | async-start | bytes 3932160 | tf_op jit(solution)/shard_map/all_to_all | solution.py:57
  27.2 1.5 %fusion.1.order_ref = bf16[96,144]{1,0:T(8,128)(2,1)} fusion(s32[144]{0:T(256)S(1)} %get-tuple-element.24, s32[144]{0:T(256)S(1)} %get-tuple-element.33, s32[96]{0:T(128)} %get-tuple-element.31, s32[96]{0:T(128)} %get-tuple-element.35, s32[144]{0:T(256)S(1)} %get-tuple-element.25, s32[144]{0:T(256)S(1)} %get-tuple-element.32, s32[96]{0:T(128)} %get-tuple-element.30, ...), kind=kLoop, calls=%fused_computation.5 | loop fusion | flops 110592 | bytes 31968 | tf_op jit(solution)/shard_map/convert_element_type | solution.py:400
  30.8 1.5 %broadcast_in_dim.26.scale_ref = f32[4,1024]{1,0:T(4,128)} reshape(f32[4,32,32]{2,1,0:T(8,128)} %broadcast_in_dim.25) | data formatting | bytes 32768 | tf_op jit(solution)/shard_map/broadcast_in_dim | solution.py:403
  33.3 4.4 %collective-permute-start.5 = (bf16[128,1280]{1,0:T(8,128)(2,1)S(1)}, bf16[128,1280]{1,0:T(8,128)(2,1)S(1)}, u32[]{:S(2)}, u32[]{:S(2)}) collective-permute-start(bf16[128,1280]{1,0:T(8,128)(2,1)S(1)} %pad_maximum_fusion), channel_id=1, source_target_pairs={{79,0},{76,1},{77,2},{78,3},{11,4},{8,5},{9,6},{10,7},{87,8},{84,9... | collective-permute-start | bytes 983048 | tf_op jit(solution)/shard_map/ppermute | solution.py:38
  37.7 2.4 %collective-permute-start.4 = (bf16[128,1280]{1,0:T(8,128)(2,1)S(1)}, bf16[128,1280]{1,0:T(8,128)(2,1)S(1)}, u32[]{:S(2)}, u32[]{:S(2)}) collective-permute-start(bf16[128,1280]{1,0:T(8,128)(2,1)S(1)} %pad_maximum_fusion), channel_id=1, source_target_pairs={{2,0},{3,1},{0,2},{1,3},{6,4},{7,5},{4,6},{5,7},{10,8},{11,9},{8,1... | collective-permute-start | bytes 983048 | tf_op jit(solution)/shard_map/ppermute | solution.py:38
  42.1 17.5 %collective-permute-done.3 = bf16[128,1280]{1,0:T(8,128)(2,1)S(1)} collective-permute-done((bf16[128,1280]{1,0:T(8,128)(2,1)S(1)}, bf16[128,1280]{1,0:T(8,128)(2,1)S(1)}, u32[]{:S(2)}, u32[]{:S(2)}) %collective-permute-start.3) | collective-permute-done | bytes 327712 | tf_op jit(solution)/shard_map/ppermute | solution.py:38
  59.6 2.7 %collective-permute-done.4 = bf16[128,1280]{1,0:T(8,128)(2,1)S(1)} collective-permute-done((bf16[128,1280]{1,0:T(8,128)(2,1)S(1)}, bf16[128,1280]{1,0:T(8,128)(2,1)S(1)}, u32[]{:S(2)}, u32[]{:S(2)}) %collective-permute-start.4) | collective-permute-done | bytes 327712 | tf_op jit(solution)/shard_map/ppermute | solution.py:38
  62.5 6.1 %collective-permute-start.6 = (bf16[128,1280]{1,0:T(8,128)(2,1)S(1)}, bf16[128,1280]{1,0:T(8,128)(2,1)S(1)}, u32[]{:S(2)}, u32[]{:S(2)}) collective-permute-start(bf16[128,1280]{1,0:T(8,128)(2,1)S(1)} %slice.15), channel_id=1, source_target_pairs={{3,0},{0,1},{1,2},{2,3},{7,4},{4,5},{5,6},{6,7},{11,8},{8,9},{9,10... | collective-permute-start | bytes 983048 | tf_op jit(solution)/shard_map/ppermute | solution.py:38
  70.3 2.4 %collective-permute-done.6.refs_6_ = bf16[128,1280]{1,0:T(8,128)(2,1)S(1)} collective-permute-done((bf16[128,1280]{1,0:T(8,128)(2,1)S(1)}, bf16[128,1280]{1,0:T(8,128)(2,1)S(1)}, u32[]{:S(2)}, u32[]{:S(2)}) %collective-permute-start.6) | collective-permute-done | bytes 327712 | tf_op jit(solution)/shard_map/ppermute | solution.py:38
  72.6 1.6 %copy.9 = bf16[32,6,40,128]{3,2,0,1:T(8,128)(2,1)} copy(bf16[32,6,40,128]{3,2,1,0:T(8,128)(2,1)S(1)} %bitcast.14) | data formatting | bytes 3932160 | tf_op jit(solution)/shard_map/reshape | solution.py:65
  74.3 8.0 %collective-permute-done.7.refs_1_ = bf16[256,1280]{1,0:T(8,128)(2,1)S(1)} collective-permute-done((bf16[256,1280]{1,0:T(8,128)(2,1)S(1)}, bf16[256,1280]{1,0:T(8,128)(2,1)S(1)}, u32[]{:S(2)}, u32[]{:S(2)}) %collective-permute-start.7) | collective-permute-done | bytes 655392 | tf_op jit(solution)/shard_map/ppermute | solution.py:38
  82.3 1.2 collective-permute-done.8.refs_2_
  83.5 1.3 collective-permute-done.9.refs_3_
  84.8 2.4 %collective-permute-done.11.refs_5_ = bf16[384,1280]{1,0:T(8,128)(2,1)S(1)} collective-permute-done((bf16[384,1280]{1,0:T(8,128)(2,1)S(1)}, bf16[384,1280]{1,0:T(8,128)(2,1)S(1)}, u32[]{:S(2)}, u32[]{:S(2)}) %collective-permute-start.11) | collective-permute-done | bytes 983072 | tf_op jit(solution)/shard_map/ppermute | solution.py:38
  87.2 3.2 %assemble.1 = bf16[64,32,1280]{2,1,0:T(8,128)(2,1)} custom-call(s32[64]{0:T(128)S(1)} %fusion.6.slots, bf16[512,1280]{1,0:T(8,128)(2,1)S(1)} %constant_dynamic-update-slice_fusion.refs_0_, bf16[256,1280]{1,0:T(8,128)(2,1)S(1)} %collective-permute-done.7.refs_1_, bf16[256,1280]{1,0:T(8,128)(2,1)S(1)} %collective-permute-done.8.refs_2_, ...), custom_call_target="tpu_custom_call" | custom-call | tf_op jit(solution)/shard_map/assemble/pallas_call | solution.py:80
  90.4 5.6 %collective-permute-start.12 = (bf16[64,32,1280]{2,1,0:T(8,128)(2,1)}, bf16[64,32,1280]{2,1,0:T(8,128)(2,1)}, u32[]{:S(2)}, u32[]{:S(2)}) collective-permute-start(bf16[64,32,1280]{2,1,0:T(8,128)(2,1)} %assemble.1), channel_id=1, source_target_pairs={{0,32},{1,33},{2,34},{3,35},{4,36},{5,37},{6,38},{7,39},{8,40},{9,... | collective-permute-start | bytes 15728648 | tf_op jit(solution)/shard_map/ppermute | solution.py:413
  96.7 8.0 %rhs_part.1 = bf16[128,32,128]{2,1,0:T(8,128)(2,1)} custom-call(f32[2]{0:T(128)} %dynamic_slice.7.scale_ref, bf16[2048,1280]{1,0:T(8,128)(2,1)} %bitcast.10.own_hbm.pixels_ref, bf16[6,1280,128]{2,1,0:T(8,128)(2,1)} %bitcast.15), custom_call_target="tpu_custom_call" | custom-call | flops 4000000000 | bytes 8000000 | tf_op jit(solution)/shard_map/rhs_part/pallas_call | solution.py:318
  104.7 4.2 %all-to-all-start.1 = ((bf16[128,32,128]{2,1,0:T(8,128)(2,1)}), bf16[128,32,128]{2,1,0:T(8,128)(2,1)S(1)}, u32[]{:S(2)}, u32[]{:S(2)}) async-start(bf16[128,32,128]{2,1,0:T(8,128)(2,1)} %rhs_part.1), calls=%async_computation.1 | async-start | bytes 2097152 | tf_op jit(solution)/shard_map/all_to_all | solution.py:417
  109.0 24.4 %gram.1.after_ref = f32[90,11520]{1,0:T(8,128)} custom-call(s32[1]{0:T(128)} %bitcast.first_ref, bf16[2048,1280]{1,0:T(8,128)(2,1)} %bitcast.10.own_hbm.pixels_ref, bf16[2048,1280]{1,0:T(8,128)(2,1)} %bitcast.11.other_hbm, bf16[16,1280]{1,0:T(8,128)(2,1)} %fusion.3.pick_ref, bf16[96,144]{1,0:T(8,128)(2,1)} %fusion.1.order_ref, ...), custom_call_target="tpu_custom_call" | custom-call | flops 20000000000 | bytes 20000000 | tf_op jit(solution)/shard_map/gram/pallas_call | solution.py:175
  134.4 2.8 %finish.1 = f32[90,1280]{1,0:T(8,128)} custom-call(bf16[128,32,128]{2,1,0:T(8,128)(2,1)} %copy-done, f32[90,11520]{1,0:T(8,128)} %gram.1.after_ref), custom_call_target="tpu_custom_call" | custom-call | tf_op jit(solution)/shard_map/finish/pallas_call | solution.py:368
  (49 shorter events, 14.0 us)
Async XLA Ops:
  2.4 29.9 %collective-permute-start.2 = (bf16[32,1280]{1,0:T(8,128)(2,1)S(1)}, bf16[32,1280]{1,0:T(8,128)(2,1)S(1)}, u32[]{:S(2)}, u32[]{:S(2)}) collective-permute-start(bf16[32,1280]{1,0:T(8,128)(2,1)S(1)} %bitcast.16), channel_id=1, source_target_pairs={{92,0},{93,1},{94,2},{95,3},{24,4},{25,5},{26,6},{27,7},{68,8},{69... | collective-permute-start | bytes 245768 | tf_op jit(solution)/shard_map/ppermute | solution.py:38
  5.9 26.5 %collective-permute-start.1 = (bf16[32,1280]{1,0:T(8,128)(2,1)S(1)}, bf16[32,1280]{1,0:T(8,128)(2,1)S(1)}, u32[]{:S(2)}, u32[]{:S(2)}) collective-permute-start(bf16[32,1280]{1,0:T(8,128)(2,1)S(1)} %bitcast.17), channel_id=1, source_target_pairs={{80,0},{81,1},{82,2},{83,3},{84,4},{85,5},{86,6},{87,7},{88,8},{89... | collective-permute-start | bytes 245768 | tf_op jit(solution)/shard_map/ppermute | solution.py:38
  11.3 21.0 %collective-permute-start = (bf16[32,1280]{1,0:T(8,128)(2,1)S(1)}, bf16[32,1280]{1,0:T(8,128)(2,1)}, u32[]{:S(2)}, u32[]{:S(2)}) collective-permute-start(bf16[32,1280]{1,0:T(8,128)(2,1)S(1)} %bitcast.18), channel_id=1, source_target_pairs={{12,0},{13,1},{14,2},{15,3},{72,4},{73,5},{74,6},{75,7},{20,8},{21... | collective-permute-start | bytes 245768 | tf_op jit(solution)/shard_map/ppermute | solution.py:38
  18.3 44.1 %all-to-all-start = ((bf16[32,240,128]{2,1,0:T(8,128)(2,1)}), bf16[32,240,128]{2,1,0:T(8,128)(2,1)S(1)}, u32[]{:S(2)}, u32[]{:S(2)}) async-start(bf16[32,240,128]{2,1,0:T(8,128)(2,1)} %pack.1), calls=%async_computation | async-start | bytes 3932160 | tf_op jit(solution)/shard_map/all_to_all | solution.py:57
  33.3 29.1 %collective-permute-start.5 = (bf16[128,1280]{1,0:T(8,128)(2,1)S(1)}, bf16[128,1280]{1,0:T(8,128)(2,1)S(1)}, u32[]{:S(2)}, u32[]{:S(2)}) collective-permute-start(bf16[128,1280]{1,0:T(8,128)(2,1)S(1)} %pad_maximum_fusion), channel_id=1, source_target_pairs={{79,0},{76,1},{77,2},{78,3},{11,4},{8,5},{9,6},{10,7},{87,8},{84,9... | collective-permute-start | bytes 983048 | tf_op jit(solution)/shard_map/ppermute | solution.py:38
  37.7 24.7 %collective-permute-start.4 = (bf16[128,1280]{1,0:T(8,128)(2,1)S(1)}, bf16[128,1280]{1,0:T(8,128)(2,1)S(1)}, u32[]{:S(2)}, u32[]{:S(2)}) collective-permute-start(bf16[128,1280]{1,0:T(8,128)(2,1)S(1)} %pad_maximum_fusion), channel_id=1, source_target_pairs={{2,0},{3,1},{0,2},{1,3},{6,4},{7,5},{4,6},{5,7},{10,8},{11,9},{8,1... | collective-permute-start | bytes 983048 | tf_op jit(solution)/shard_map/ppermute | solution.py:38
  40.1 19.5 %collective-permute-start.3 = (bf16[128,1280]{1,0:T(8,128)(2,1)S(1)}, bf16[128,1280]{1,0:T(8,128)(2,1)S(1)}, u32[]{:S(2)}, u32[]{:S(2)}) collective-permute-start(bf16[128,1280]{1,0:T(8,128)(2,1)S(1)} %pad_maximum_fusion), channel_id=1, source_target_pairs={{29,0},{30,1},{31,2},{28,3},{89,4},{90,5},{91,6},{88,7},{5,8},{6,9... | collective-permute-start | bytes 983048 | tf_op jit(solution)/shard_map/ppermute | solution.py:38
  62.5 10.1 %collective-permute-start.6 = (bf16[128,1280]{1,0:T(8,128)(2,1)S(1)}, bf16[128,1280]{1,0:T(8,128)(2,1)S(1)}, u32[]{:S(2)}, u32[]{:S(2)}) collective-permute-start(bf16[128,1280]{1,0:T(8,128)(2,1)S(1)} %slice.15), channel_id=1, source_target_pairs={{3,0},{0,1},{1,2},{2,3},{7,4},{4,5},{5,6},{6,7},{11,8},{8,9},{9,10... | collective-permute-start | bytes 983048 | tf_op jit(solution)/shard_map/ppermute | solution.py:38
  68.6 18.5 %collective-permute-start.11 = (bf16[384,1280]{1,0:T(8,128)(2,1)S(1)}, bf16[384,1280]{1,0:T(8,128)(2,1)S(1)}, u32[]{:S(2)}, u32[]{:S(2)}) collective-permute-start(bf16[384,1280]{1,0:T(8,128)(2,1)S(1)} %slice.17), channel_id=1, source_target_pairs={{1,0},{2,1},{3,2},{0,3},{5,4},{6,5},{7,6},{4,7},{9,8},{10,9},{11,1... | collective-permute-start | bytes 2949128 | tf_op jit(solution)/shard_map/ppermute | solution.py:38
  68.7 13.6 %collective-permute-start.10 = (bf16[256,1280]{1,0:T(8,128)(2,1)S(1)}, bf16[256,1280]{1,0:T(8,128)(2,1)S(1)}, u32[]{:S(2)}, u32[]{:S(2)}) collective-permute-start(bf16[256,1280]{1,0:T(8,128)(2,1)S(1)} %get-tuple-element.22), channel_id=1, source_target_pairs={{8,0},{9,1},{10,2},{11,3},{12,4},{13,5},{14,6},{15,7},{16,8},{17,9... | collective-permute-start | bytes 1966088 | tf_op jit(solution)/shard_map/ppermute | solution.py:38
  69.9 12.4 %collective-permute-start.7 = (bf16[256,1280]{1,0:T(8,128)(2,1)S(1)}, bf16[256,1280]{1,0:T(8,128)(2,1)S(1)}, u32[]{:S(2)}, u32[]{:S(2)}) collective-permute-start(bf16[256,1280]{1,0:T(8,128)(2,1)S(1)} %get-tuple-element.16), channel_id=1, source_target_pairs={{4,0},{5,1},{6,2},{7,3},{64,4},{65,5},{66,6},{67,7},{12,8},{13,9},... | collective-permute-start | bytes 1966088 | tf_op jit(solution)/shard_map/ppermute | solution.py:38
  69.9 13.6 %collective-permute-start.8 = (bf16[256,1280]{1,0:T(8,128)(2,1)S(1)}, bf16[256,1280]{1,0:T(8,128)(2,1)S(1)}, u32[]{:S(2)}, u32[]{:S(2)}) collective-permute-start(bf16[256,1280]{1,0:T(8,128)(2,1)S(1)} %get-tuple-element.22), channel_id=1, source_target_pairs={{24,0},{25,1},{26,2},{27,3},{28,4},{29,5},{30,6},{31,7},{0,8},{1,9... | collective-permute-start | bytes 1966088 | tf_op jit(solution)/shard_map/ppermute | solution.py:38
  72.6 12.1 %collective-permute-start.9 = (bf16[256,1280]{1,0:T(8,128)(2,1)S(1)}, bf16[256,1280]{1,0:T(8,128)(2,1)S(1)}, u32[]{:S(2)}, u32[]{:S(2)}) collective-permute-start(bf16[256,1280]{1,0:T(8,128)(2,1)S(1)} %get-tuple-element.16), channel_id=1, source_target_pairs={{68,0},{69,1},{70,2},{71,3},{0,4},{1,5},{2,6},{3,7},{76,8},{77,9},... | collective-permute-start | bytes 1966088 | tf_op jit(solution)/shard_map/ppermute | solution.py:38
  90.4 18.6 %collective-permute-start.12 = (bf16[64,32,1280]{2,1,0:T(8,128)(2,1)}, bf16[64,32,1280]{2,1,0:T(8,128)(2,1)}, u32[]{:S(2)}, u32[]{:S(2)}) collective-permute-start(bf16[64,32,1280]{2,1,0:T(8,128)(2,1)} %assemble.1), channel_id=1, source_target_pairs={{0,32},{1,33},{2,34},{3,35},{4,36},{5,37},{6,38},{7,39},{8,40},{9,... | collective-permute-start | bytes 15728648 | tf_op jit(solution)/shard_map/ppermute | solution.py:413
  104.7 28.7 %all-to-all-start.1 = ((bf16[128,32,128]{2,1,0:T(8,128)(2,1)}), bf16[128,32,128]{2,1,0:T(8,128)(2,1)S(1)}, u32[]{:S(2)}, u32[]{:S(2)}) async-start(bf16[128,32,128]{2,1,0:T(8,128)(2,1)} %rhs_part.1), calls=%async_computation.1 | async-start | bytes 2097152 | tf_op jit(solution)/shard_map/all_to_all | solution.py:417
  133.4 1.0 copy-start

commit v10 on v9

--- a/solution.py
+++ b/solution.py
@@ -371,7 +371,7 @@
         in_specs=[whole, pl.BlockSpec(memory_space=pltpu.HBM)],
         out_specs=whole,
         scratch_shapes=[pltpu.VMEM((96, CH), jnp.float32)],
-        compiler_params=pltpu.CompilerParams(vmem_limit_bytes=62 * 1024 * 1024),
+        compiler_params=pltpu.CompilerParams(vmem_limit_bytes=57 * 1024 * 1024),
         name="finish",
     )(sent, after)
 
@@ -407,8 +407,8 @@
     src_x, src_y, src_z = (x + offs[:, 0]) % 4, (y + offs[:, 1]) % 4, (z + offs[:, 2]) % 4
     away = (src_x // 2 != x_hi).astype(jnp.int32)
     slots = (away * 32 + src_z * 8 + (src_x % 2) * 4 + src_y).astype(jnp.int32)
-    pieces, tiles, early = gather_chips(masked.reshape(ROWS, CH), packed, (pick, order, img_scale, slots))
-    pick, order, img_scale, slots = early
+    pieces, tiles, early = gather_chips(masked.reshape(ROWS, CH), packed, (pick, order, img_scale, slots, my_scale))
+    pick, order, img_scale, slots, my_scale = early
     own = assemble(slots, pieces)
     other = lax.ppermute(own, AXES, [(d, d ^ 32) for d in range(128)])
 

time: 138 us -> 137 us (level)
  no operation moved by 1% of the time
where the time goes in v10:
time: 137 us; the launch traced here: 136 us
  Pallas kernels  43.8 us (32%)
  starting transfers between devices  40.4 us (29%)
  waiting for transfers between devices  35.1 us (26%)
  local copies, waits for them, and re-layouts  8.11 us (6%)
  other arithmetic  7.85 us (6%)
    ppermute x12, waiting for transfers between devices, take_from(): return lax.ppermute(value, AXES, pairs)  35.1 us
    ppermute x12, starting transfers between devices, take_from(): return lax.ppermute(value, AXES, pairs)  25.5 us
    pallas_call x1, Pallas kernels, gram(): pl.pallas_call(gram_kernel, out_shape=jax.ShapeDtypeStruct((90, 11520), j...  24.4 us
    pallas_call x1, Pallas kernels, rhs_part(): pl.pallas_call(rhs_kernel, out_shape=jax.ShapeDtypeStruct((128, 32, 128),...  8.02 us
    ppermute x1, starting transfers between devices, body(): other = lax.ppermute(own, AXES, [(d, d ^ 32) for d in range(128)])  5.63 us
    pallas_call x1, Pallas kernels, pack(): pl.pallas_call(pack_kernel, out_shape=jax.ShapeDtypeStruct((32, 240, 128)...  5.31 us
    all_to_all x1, starting transfers between devices, gather_chips(): lax.all_to_all(packed, 'blk', split_axis=0, concat_axis=0, tiled=True)  5.08 us
    all_to_all x1, starting transfers between devices, body(): lax.all_to_all(part, ('blk', 'client'), split_axis=0, concat_axis=0, tile...  4.12 us
  transfers between devices with their start and end apart: 15, of which 7 were waited for; matrix products, arithmetic and copies ran while one was open for 10% of the time, Pallas kernels for 28%

profile of v10, /device:TPU:1, one launch (start us, length us, event | category | flops | bytes accessed | tf_op | source)
XLA Modules:
  0.0 136.1 jit_solution(8872719820300620102)
XLA Ops:
  2.4 3.5 %collective-permute-start.2 = (bf16[32,1280]{1,0:T(8,128)(2,1)S(1)}, bf16[32,1280]{1,0:T(8,128)(2,1)S(1)}, u32[]{:S(2)}, u32[]{:S(2)}) collective-permute-start(bf16[32,1280]{1,0:T(8,128)(2,1)S(1)} %bitcast.16), channel_id=1, source_target_pairs={{92,0},{93,1},{94,2},{95,3},{24,4},{25,5},{26,6},{27,7},{68,8},{69... | collective-permute-start | bytes 245768 | tf_op jit(solution)/shard_map/ppermute | solution.py:38
  5.9 5.5 %collective-permute-start.1 = (bf16[32,1280]{1,0:T(8,128)(2,1)S(1)}, bf16[32,1280]{1,0:T(8,128)(2,1)S(1)}, u32[]{:S(2)}, u32[]{:S(2)}) collective-permute-start(bf16[32,1280]{1,0:T(8,128)(2,1)S(1)} %bitcast.17), channel_id=1, source_target_pairs={{80,0},{81,1},{82,2},{83,3},{84,4},{85,5},{86,6},{87,7},{88,8},{89... | collective-permute-start | bytes 245768 | tf_op jit(solution)/shard_map/ppermute | solution.py:38
  11.3 1.6 %collective-permute-start = (bf16[32,1280]{1,0:T(8,128)(2,1)S(1)}, bf16[32,1280]{1,0:T(8,128)(2,1)}, u32[]{:S(2)}, u32[]{:S(2)}) collective-permute-start(bf16[32,1280]{1,0:T(8,128)(2,1)S(1)} %bitcast.18), channel_id=1, source_target_pairs={{12,0},{13,1},{14,2},{15,3},{72,4},{73,5},{74,6},{75,7},{20,8},{21... | collective-permute-start | bytes 245768 | tf_op jit(solution)/shard_map/ppermute | solution.py:38
  12.9 5.3 %pack.1 = bf16[32,240,128]{2,1,0:T(8,128)(2,1)} custom-call(bf16[2,360,1280]{2,1,0:T(8,128)(2,1)} %weights_hbm.1), custom_call_target="tpu_custom_call" | custom-call | flops 1000000000 | bytes 6000000 | tf_op jit(solution)/shard_map/pack/pallas_call | solution.py:222
  18.3 5.1 %all-to-all-start = ((bf16[32,240,128]{2,1,0:T(8,128)(2,1)}), bf16[32,240,128]{2,1,0:T(8,128)(2,1)S(1)}, u32[]{:S(2)}, u32[]{:S(2)}) async-start(bf16[32,240,128]{2,1,0:T(8,128)(2,1)} %pack.1), calls=%async_computation | async-start | bytes 3932160 | tf_op jit(solution)/shard_map/all_to_all | solution.py:57
  27.2 1.5 %fusion.1.order_ref = bf16[96,144]{1,0:T(8,128)(2,1)} fusion(s32[144]{0:T(256)S(1)} %get-tuple-element.26, s32[144]{0:T(256)S(1)} %get-tuple-element.35, s32[96]{0:T(128)} %get-tuple-element.33, s32[96]{0:T(128)} %get-tuple-element.37, s32[144]{0:T(256)S(1)} %get-tuple-element.27, s32[144]{0:T(256)S(1)} %get-tuple-element.34, s32[96]{0:T(128)} %get-tuple-element.32, ...), kind=kLoop, calls=%fused_computation.5 | loop fusion | flops 110592 | bytes 31968 | tf_op jit(solution)/shard_map/convert_element_type | solution.py:400
  31.5 1.5 %broadcast_in_dim.26.scale_ref = f32[4,1024]{1,0:T(4,128)} reshape(f32[4,32,32]{2,1,0:T(8,128)} %broadcast_in_dim.25) | data formatting | bytes 32768 | tf_op jit(solution)/shard_map/broadcast_in_dim | solution.py:403
  33.9 4.4 %collective-permute-start.5 = (bf16[128,1280]{1,0:T(8,128)(2,1)S(1)}, bf16[128,1280]{1,0:T(8,128)(2,1)S(1)}, u32[]{:S(2)}, u32[]{:S(2)}) collective-permute-start(bf16[128,1280]{1,0:T(8,128)(2,1)S(1)} %pad_maximum_fusion), channel_id=1, source_target_pairs={{79,0},{76,1},{77,2},{78,3},{11,4},{8,5},{9,6},{10,7},{87,8},{84,9... | collective-permute-start | bytes 983048 | tf_op jit(solution)/shard_map/ppermute | solution.py:38
  38.3 2.4 %collective-permute-start.4 = (bf16[128,1280]{1,0:T(8,128)(2,1)S(1)}, bf16[128,1280]{1,0:T(8,128)(2,1)S(1)}, u32[]{:S(2)}, u32[]{:S(2)}) collective-permute-start(bf16[128,1280]{1,0:T(8,128)(2,1)S(1)} %pad_maximum_fusion), channel_id=1, source_target_pairs={{2,0},{3,1},{0,2},{1,3},{6,4},{7,5},{4,6},{5,7},{10,8},{11,9},{8,1... | collective-permute-start | bytes 983048 | tf_op jit(solution)/shard_map/ppermute | solution.py:38
  42.7 16.6 %collective-permute-done.3 = bf16[128,1280]{1,0:T(8,128)(2,1)S(1)} collective-permute-done((bf16[128,1280]{1,0:T(8,128)(2,1)S(1)}, bf16[128,1280]{1,0:T(8,128)(2,1)S(1)}, u32[]{:S(2)}, u32[]{:S(2)}) %collective-permute-start.3) | collective-permute-done | bytes 327712 | tf_op jit(solution)/shard_map/ppermute | solution.py:38
  59.3 3.3 %collective-permute-done.4 = bf16[128,1280]{1,0:T(8,128)(2,1)S(1)} collective-permute-done((bf16[128,1280]{1,0:T(8,128)(2,1)S(1)}, bf16[128,1280]{1,0:T(8,128)(2,1)S(1)}, u32[]{:S(2)}, u32[]{:S(2)}) %collective-permute-start.4) | collective-permute-done | bytes 327712 | tf_op jit(solution)/shard_map/ppermute | solution.py:38
  62.8 5.5 %collective-permute-start.6 = (bf16[128,1280]{1,0:T(8,128)(2,1)S(1)}, bf16[128,1280]{1,0:T(8,128)(2,1)S(1)}, u32[]{:S(2)}, u32[]{:S(2)}) collective-permute-start(bf16[128,1280]{1,0:T(8,128)(2,1)S(1)} %slice.15), channel_id=1, source_target_pairs={{3,0},{0,1},{1,2},{2,3},{7,4},{4,5},{5,6},{6,7},{11,8},{8,9},{9,10... | collective-permute-start | bytes 983048 | tf_op jit(solution)/shard_map/ppermute | solution.py:38
  68.4 1.3 collective-permute-start.10
  70.0 2.4 %collective-permute-done.6.refs_6_ = bf16[128,1280]{1,0:T(8,128)(2,1)S(1)} collective-permute-done((bf16[128,1280]{1,0:T(8,128)(2,1)S(1)}, bf16[128,1280]{1,0:T(8,128)(2,1)S(1)}, u32[]{:S(2)}, u32[]{:S(2)}) %collective-permute-start.6) | collective-permute-done | bytes 327712 | tf_op jit(solution)/shard_map/ppermute | solution.py:38
  72.4 1.6 %copy.9 = bf16[32,6,40,128]{3,2,0,1:T(8,128)(2,1)} copy(bf16[32,6,40,128]{3,2,1,0:T(8,128)(2,1)S(1)} %bitcast.14) | data formatting | bytes 3932160 | tf_op jit(solution)/shard_map/reshape | solution.py:65
  74.0 8.4 %collective-permute-done.7.refs_1_ = bf16[256,1280]{1,0:T(8,128)(2,1)S(1)} collective-permute-done((bf16[256,1280]{1,0:T(8,128)(2,1)S(1)}, bf16[256,1280]{1,0:T(8,128)(2,1)S(1)}, u32[]{:S(2)}, u32[]{:S(2)}) %collective-permute-start.7) | collective-permute-done | bytes 655392 | tf_op jit(solution)/shard_map/ppermute | solution.py:38
  82.4 1.1 collective-permute-done.8.refs_2_
  84.5 2.4 %collective-permute-done.11.refs_5_ = bf16[384,1280]{1,0:T(8,128)(2,1)S(1)} collective-permute-done((bf16[384,1280]{1,0:T(8,128)(2,1)S(1)}, bf16[384,1280]{1,0:T(8,128)(2,1)S(1)}, u32[]{:S(2)}, u32[]{:S(2)}) %collective-permute-start.11) | collective-permute-done | bytes 983072 | tf_op jit(solution)/shard_map/ppermute | solution.py:38
  86.9 3.2 %assemble.1 = bf16[64,32,1280]{2,1,0:T(8,128)(2,1)} custom-call(s32[64]{0:T(128)S(1)} %fusion.6.slots, bf16[512,1280]{1,0:T(8,128)(2,1)S(1)} %constant_dynamic-update-slice_fusion.refs_0_, bf16[256,1280]{1,0:T(8,128)(2,1)S(1)} %collective-permute-done.7.refs_1_, bf16[256,1280]{1,0:T(8,128)(2,1)S(1)} %collective-permute-done.8.refs_2_, ...), custom_call_target="tpu_custom_call" | custom-call | tf_op jit(solution)/shard_map/assemble/pallas_call | solution.py:80
  90.1 5.6 %collective-permute-start.12 = (bf16[64,32,1280]{2,1,0:T(8,128)(2,1)}, bf16[64,32,1280]{2,1,0:T(8,128)(2,1)}, u32[]{:S(2)}, u32[]{:S(2)}) collective-permute-start(bf16[64,32,1280]{2,1,0:T(8,128)(2,1)} %assemble.1), channel_id=1, source_target_pairs={{0,32},{1,33},{2,34},{3,35},{4,36},{5,37},{6,38},{7,39},{8,40},{9,... | collective-permute-start | bytes 15728648 | tf_op jit(solution)/shard_map/ppermute | solution.py:413
  95.7 8.0 %rhs_part.1 = bf16[128,32,128]{2,1,0:T(8,128)(2,1)} custom-call(f32[2]{0:T(128)} %dynamic_slice.7.scale_ref, bf16[2048,1280]{1,0:T(8,128)(2,1)} %bitcast.10.own_hbm.pixels_ref, bf16[6,1280,128]{2,1,0:T(8,128)(2,1)} %bitcast.15), custom_call_target="tpu_custom_call" | custom-call | flops 4000000000 | bytes 8000000 | tf_op jit(solution)/shard_map/rhs_part/pallas_call | solution.py:318
  103.8 4.1 %all-to-all-start.1 = ((bf16[128,32,128]{2,1,0:T(8,128)(2,1)}), bf16[128,32,128]{2,1,0:T(8,128)(2,1)S(1)}, u32[]{:S(2)}, u32[]{:S(2)}) async-start(bf16[128,32,128]{2,1,0:T(8,128)(2,1)} %rhs_part.1), calls=%async_computation.1 | async-start | bytes 2097152 | tf_op jit(solution)/shard_map/all_to_all | solution.py:417
  107.9 24.4 %gram.1.after_ref = f32[90,11520]{1,0:T(8,128)} custom-call(s32[1]{0:T(128)} %bitcast.first_ref, bf16[2048,1280]{1,0:T(8,128)(2,1)} %bitcast.10.own_hbm.pixels_ref, bf16[2048,1280]{1,0:T(8,128)(2,1)} %bitcast.11.other_hbm, bf16[16,1280]{1,0:T(8,128)(2,1)} %fusion.3.pick_ref, bf16[96,144]{1,0:T(8,128)(2,1)} %fusion.1.order_ref, ...), custom_call_target="tpu_custom_call" | custom-call | flops 20000000000 | bytes 20000000 | tf_op jit(solution)/shard_map/gram/pallas_call | solution.py:175
  133.3 2.8 %finish.1 = f32[90,1280]{1,0:T(8,128)} custom-call(bf16[128,32,128]{2,1,0:T(8,128)(2,1)} %copy-done, f32[90,11520]{1,0:T(8,128)} %gram.1.after_ref), custom_call_target="tpu_custom_call" | custom-call | tf_op jit(solution)/shard_map/finish/pallas_call | solution.py:368
  (49 shorter events, 13.7 us)
Async XLA Ops:
  2.4 30.6 %collective-permute-start.2 = (bf16[32,1280]{1,0:T(8,128)(2,1)S(1)}, bf16[32,1280]{1,0:T(8,128)(2,1)S(1)}, u32[]{:S(2)}, u32[]{:S(2)}) collective-permute-start(bf16[32,1280]{1,0:T(8,128)(2,1)S(1)} %bitcast.16), channel_id=1, source_target_pairs={{92,0},{93,1},{94,2},{95,3},{24,4},{25,5},{26,6},{27,7},{68,8},{69... | collective-permute-start | bytes 245768 | tf_op jit(solution)/shard_map/ppermute | solution.py:38
  5.9 27.1 %collective-permute-start.1 = (bf16[32,1280]{1,0:T(8,128)(2,1)S(1)}, bf16[32,1280]{1,0:T(8,128)(2,1)S(1)}, u32[]{:S(2)}, u32[]{:S(2)}) collective-permute-start(bf16[32,1280]{1,0:T(8,128)(2,1)S(1)} %bitcast.17), channel_id=1, source_target_pairs={{80,0},{81,1},{82,2},{83,3},{84,4},{85,5},{86,6},{87,7},{88,8},{89... | collective-permute-start | bytes 245768 | tf_op jit(solution)/shard_map/ppermute | solution.py:38
  11.3 21.7 %collective-permute-start = (bf16[32,1280]{1,0:T(8,128)(2,1)S(1)}, bf16[32,1280]{1,0:T(8,128)(2,1)}, u32[]{:S(2)}, u32[]{:S(2)}) collective-permute-start(bf16[32,1280]{1,0:T(8,128)(2,1)S(1)} %bitcast.18), channel_id=1, source_target_pairs={{12,0},{13,1},{14,2},{15,3},{72,4},{73,5},{74,6},{75,7},{20,8},{21... | collective-permute-start | bytes 245768 | tf_op jit(solution)/shard_map/ppermute | solution.py:38
  18.3 44.4 %all-to-all-start = ((bf16[32,240,128]{2,1,0:T(8,128)(2,1)}), bf16[32,240,128]{2,1,0:T(8,128)(2,1)S(1)}, u32[]{:S(2)}, u32[]{:S(2)}) async-start(bf16[32,240,128]{2,1,0:T(8,128)(2,1)} %pack.1), calls=%async_computation | async-start | bytes 3932160 | tf_op jit(solution)/shard_map/all_to_all | solution.py:57
  33.9 28.7 %collective-permute-start.5 = (bf16[128,1280]{1,0:T(8,128)(2,1)S(1)}, bf16[128,1280]{1,0:T(8,128)(2,1)S(1)}, u32[]{:S(2)}, u32[]{:S(2)}) collective-permute-start(bf16[128,1280]{1,0:T(8,128)(2,1)S(1)} %pad_maximum_fusion), channel_id=1, source_target_pairs={{79,0},{76,1},{77,2},{78,3},{11,4},{8,5},{9,6},{10,7},{87,8},{84,9... | collective-permute-start | bytes 983048 | tf_op jit(solution)/shard_map/ppermute | solution.py:38
  38.3 24.3 %collective-permute-start.4 = (bf16[128,1280]{1,0:T(8,128)(2,1)S(1)}, bf16[128,1280]{1,0:T(8,128)(2,1)S(1)}, u32[]{:S(2)}, u32[]{:S(2)}) collective-permute-start(bf16[128,1280]{1,0:T(8,128)(2,1)S(1)} %pad_maximum_fusion), channel_id=1, source_target_pairs={{2,0},{3,1},{0,2},{1,3},{6,4},{7,5},{4,6},{5,7},{10,8},{11,9},{8,1... | collective-permute-start | bytes 983048 | tf_op jit(solution)/shard_map/ppermute | solution.py:38
  40.7 18.6 %collective-permute-start.3 = (bf16[128,1280]{1,0:T(8,128)(2,1)S(1)}, bf16[128,1280]{1,0:T(8,128)(2,1)S(1)}, u32[]{:S(2)}, u32[]{:S(2)}) collective-permute-start(bf16[128,1280]{1,0:T(8,128)(2,1)S(1)} %pad_maximum_fusion), channel_id=1, source_target_pairs={{29,0},{30,1},{31,2},{28,3},{89,4},{90,5},{91,6},{88,7},{5,8},{6,9... | collective-permute-start | bytes 983048 | tf_op jit(solution)/shard_map/ppermute | solution.py:38
  62.8 9.6 %collective-permute-start.6 = (bf16[128,1280]{1,0:T(8,128)(2,1)S(1)}, bf16[128,1280]{1,0:T(8,128)(2,1)S(1)}, u32[]{:S(2)}, u32[]{:S(2)}) collective-permute-start(bf16[128,1280]{1,0:T(8,128)(2,1)S(1)} %slice.15), channel_id=1, source_target_pairs={{3,0},{0,1},{1,2},{2,3},{7,4},{4,5},{5,6},{6,7},{11,8},{8,9},{9,10... | collective-permute-start | bytes 983048 | tf_op jit(solution)/shard_map/ppermute | solution.py:38
  68.3 18.5 %collective-permute-start.11 = (bf16[384,1280]{1,0:T(8,128)(2,1)S(1)}, bf16[384,1280]{1,0:T(8,128)(2,1)S(1)}, u32[]{:S(2)}, u32[]{:S(2)}) collective-permute-start(bf16[384,1280]{1,0:T(8,128)(2,1)S(1)} %slice.17), channel_id=1, source_target_pairs={{1,0},{2,1},{3,2},{0,3},{5,4},{6,5},{7,6},{4,7},{9,8},{10,9},{11,1... | collective-permute-start | bytes 2949128 | tf_op jit(solution)/shard_map/ppermute | solution.py:38
  68.4 14.0 %collective-permute-start.10 = (bf16[256,1280]{1,0:T(8,128)(2,1)S(1)}, bf16[256,1280]{1,0:T(8,128)(2,1)S(1)}, u32[]{:S(2)}, u32[]{:S(2)}) collective-permute-start(bf16[256,1280]{1,0:T(8,128)(2,1)S(1)} %get-tuple-element.24), channel_id=1, source_target_pairs={{8,0},{9,1},{10,2},{11,3},{12,4},{13,5},{14,6},{15,7},{16,8},{17,9... | collective-permute-start | bytes 1966088 | tf_op jit(solution)/shard_map/ppermute | solution.py:38
  69.8 12.7 %collective-permute-start.7 = (bf16[256,1280]{1,0:T(8,128)(2,1)S(1)}, bf16[256,1280]{1,0:T(8,128)(2,1)S(1)}, u32[]{:S(2)}, u32[]{:S(2)}) collective-permute-start(bf16[256,1280]{1,0:T(8,128)(2,1)S(1)} %get-tuple-element.17), channel_id=1, source_target_pairs={{4,0},{5,1},{6,2},{7,3},{64,4},{65,5},{66,6},{67,7},{12,8},{13,9},... | collective-permute-start | bytes 1966088 | tf_op jit(solution)/shard_map/ppermute | solution.py:38
  69.8 13.8 %collective-permute-start.8 = (bf16[256,1280]{1,0:T(8,128)(2,1)S(1)}, bf16[256,1280]{1,0:T(8,128)(2,1)S(1)}, u32[]{:S(2)}, u32[]{:S(2)}) collective-permute-start(bf16[256,1280]{1,0:T(8,128)(2,1)S(1)} %get-tuple-element.24), channel_id=1, source_target_pairs={{24,0},{25,1},{26,2},{27,3},{28,4},{29,5},{30,6},{31,7},{0,8},{1,9... | collective-permute-start | bytes 1966088 | tf_op jit(solution)/shard_map/ppermute | solution.py:38
  72.4 12.1 %collective-permute-start.9 = (bf16[256,1280]{1,0:T(8,128)(2,1)S(1)}, bf16[256,1280]{1,0:T(8,128)(2,1)S(1)}, u32[]{:S(2)}, u32[]{:S(2)}) collective-permute-start(bf16[256,1280]{1,0:T(8,128)(2,1)S(1)} %get-tuple-element.17), channel_id=1, source_target_pairs={{68,0},{69,1},{70,2},{71,3},{0,4},{1,5},{2,6},{3,7},{76,8},{77,9},... | collective-permute-start | bytes 1966088 | tf_op jit(solution)/shard_map/ppermute | solution.py:38
  90.1 17.8 %collective-permute-start.12 = (bf16[64,32,1280]{2,1,0:T(8,128)(2,1)}, bf16[64,32,1280]{2,1,0:T(8,128)(2,1)}, u32[]{:S(2)}, u32[]{:S(2)}) collective-permute-start(bf16[64,32,1280]{2,1,0:T(8,128)(2,1)} %assemble.1), channel_id=1, source_target_pairs={{0,32},{1,33},{2,34},{3,35},{4,36},{5,37},{6,38},{7,39},{8,40},{9,... | collective-permute-start | bytes 15728648 | tf_op jit(solution)/shard_map/ppermute | solution.py:413
  103.8 28.5 %all-to-all-start.1 = ((bf16[128,32,128]{2,1,0:T(8,128)(2,1)}), bf16[128,32,128]{2,1,0:T(8,128)(2,1)S(1)}, u32[]{:S(2)}, u32[]{:S(2)}) async-start(bf16[128,32,128]{2,1,0:T(8,128)(2,1)} %rhs_part.1), calls=%async_computation.1 | async-start | bytes 2097152 | tf_op jit(solution)/shard_map/all_to_all | solution.py:417
  132.3 1.0 copy-start

commit v11 on v10

--- a/solution.py
+++ b/solution.py
@@ -371,7 +371,7 @@
         in_specs=[whole, pl.BlockSpec(memory_space=pltpu.HBM)],
         out_specs=whole,
         scratch_shapes=[pltpu.VMEM((96, CH), jnp.float32)],
-        compiler_params=pltpu.CompilerParams(vmem_limit_bytes=57 * 1024 * 1024),
+        compiler_params=pltpu.CompilerParams(vmem_limit_bytes=50 * 1024 * 1024),
         name="finish",
     )(sent, after)
 

time: 137 us -> 134 us (0.978)
  no operation moved by 1% of the time
where the time goes in v11:
time: 134 us
  Pallas kernels  42.5 us (32%)
  starting transfers between devices  40.4 us (30%)
  waiting for transfers between devices  35.1 us (26%)
  other arithmetic  7.92 us (6%)
  local copies, waits for them, and re-layouts  7.12 us (5%)
    ppermute x12, waiting for transfers between devices, take_from(): return lax.ppermute(value, AXES, pairs)  35 us
    ppermute x12, starting transfers between devices, take_from(): return lax.ppermute(value, AXES, pairs)  25.5 us
    pallas_call x1, Pallas kernels, gram(): pl.pallas_call(gram_kernel, out_shape=jax.ShapeDtypeStruct((90, 11520), j...  24.4 us
    pallas_call x1, Pallas kernels, rhs_part(): pl.pallas_call(rhs_kernel, out_shape=jax.ShapeDtypeStruct((128, 32, 128),...  8.02 us
    ppermute x1, starting transfers between devices, body(): other = lax.ppermute(own, AXES, [(d, d ^ 32) for d in range(128)])  5.63 us
    pallas_call x1, Pallas kernels, pack(): pl.pallas_call(pack_kernel, out_shape=jax.ShapeDtypeStruct((32, 240, 128)...  5.31 us
    all_to_all x1, starting transfers between devices, gather_chips(): lax.all_to_all(packed, 'blk', split_axis=0, concat_axis=0, tiled=True)  5.08 us
    all_to_all x1, starting transfers between devices, body(): lax.all_to_all(part, ('blk', 'client'), split_axis=0, concat_axis=0, tile...  4.2 us
  transfers between devices with their start and end apart: 15, of which 7 were waited for; matrix products, arithmetic and copies ran while one was open for 10% of the time, Pallas kernels for 28%

profile of v11, /device:TPU:1, one launch (start us, length us, event | category | flops | bytes accessed | tf_op | source)
XLA Modules:
  0.0 133.9 jit_solution(4779773750462040198)
XLA Ops:
  2.4 3.5 %collective-permute-start.2 = (bf16[32,1280]{1,0:T(8,128)(2,1)S(1)}, bf16[32,1280]{1,0:T(8,128)(2,1)S(1)}, u32[]{:S(2)}, u32[]{:S(2)}) collective-permute-start(bf16[32,1280]{1,0:T(8,128)(2,1)S(1)} %bitcast.16), channel_id=1, source_target_pairs={{92,0},{93,1},{94,2},{95,3},{24,4},{25,5},{26,6},{27,7},{68,8},{69... | collective-permute-start | bytes 245768 | tf_op jit(solution)/shard_map/ppermute | solution.py:38
  5.9 5.5 %collective-permute-start.1 = (bf16[32,1280]{1,0:T(8,128)(2,1)S(1)}, bf16[32,1280]{1,0:T(8,128)(2,1)S(1)}, u32[]{:S(2)}, u32[]{:S(2)}) collective-permute-start(bf16[32,1280]{1,0:T(8,128)(2,1)S(1)} %bitcast.17), channel_id=1, source_target_pairs={{80,0},{81,1},{82,2},{83,3},{84,4},{85,5},{86,6},{87,7},{88,8},{89... | collective-permute-start | bytes 245768 | tf_op jit(solution)/shard_map/ppermute | solution.py:38
  11.3 1.6 %collective-permute-start = (bf16[32,1280]{1,0:T(8,128)(2,1)S(1)}, bf16[32,1280]{1,0:T(8,128)(2,1)}, u32[]{:S(2)}, u32[]{:S(2)}) collective-permute-start(bf16[32,1280]{1,0:T(8,128)(2,1)S(1)} %bitcast.18), channel_id=1, source_target_pairs={{12,0},{13,1},{14,2},{15,3},{72,4},{73,5},{74,6},{75,7},{20,8},{21... | collective-permute-start | bytes 245768 | tf_op jit(solution)/shard_map/ppermute | solution.py:38
  12.9 5.3 %pack.1 = bf16[32,240,128]{2,1,0:T(8,128)(2,1)} custom-call(bf16[2,360,1280]{2,1,0:T(8,128)(2,1)} %weights_hbm.1), custom_call_target="tpu_custom_call" | custom-call | flops 1000000000 | bytes 6000000 | tf_op jit(solution)/shard_map/pack/pallas_call | solution.py:222
  18.3 5.1 %all-to-all-start = ((bf16[32,240,128]{2,1,0:T(8,128)(2,1)}), bf16[32,240,128]{2,1,0:T(8,128)(2,1)S(1)}, u32[]{:S(2)}, u32[]{:S(2)}) async-start(bf16[32,240,128]{2,1,0:T(8,128)(2,1)} %pack.1), calls=%async_computation | async-start | bytes 3932160 | tf_op jit(solution)/shard_map/all_to_all | solution.py:57
  27.2 1.5 %fusion.1.order_ref = bf16[96,144]{1,0:T(8,128)(2,1)} fusion(s32[144]{0:T(256)S(1)} %get-tuple-element.26, s32[144]{0:T(256)S(1)} %get-tuple-element.35, s32[96]{0:T(128)} %get-tuple-element.33, s32[96]{0:T(128)} %get-tuple-element.37, s32[144]{0:T(256)S(1)} %get-tuple-element.27, s32[144]{0:T(256)S(1)} %get-tuple-element.34, s32[96]{0:T(128)} %get-tuple-element.32, ...), kind=kLoop, calls=%fused_computation.5 | loop fusion | flops 110592 | bytes 31968 | tf_op jit(solution)/shard_map/convert_element_type | solution.py:400
  31.5 1.5 %broadcast_in_dim.26.scale_ref = f32[4,1024]{1,0:T(4,128)} reshape(f32[4,32,32]{2,1,0:T(8,128)} %broadcast_in_dim.25) | data formatting | bytes 32768 | tf_op jit(solution)/shard_map/broadcast_in_dim | solution.py:403
  34.0 4.4 %collective-permute-start.5 = (bf16[128,1280]{1,0:T(8,128)(2,1)S(1)}, bf16[128,1280]{1,0:T(8,128)(2,1)S(1)}, u32[]{:S(2)}, u32[]{:S(2)}) collective-permute-start(bf16[128,1280]{1,0:T(8,128)(2,1)S(1)} %pad_maximum_fusion), channel_id=1, source_target_pairs={{79,0},{76,1},{77,2},{78,3},{11,4},{8,5},{9,6},{10,7},{87,8},{84,9... | collective-permute-start | bytes 983048 | tf_op jit(solution)/shard_map/ppermute | solution.py:38
  38.4 2.4 %collective-permute-start.4 = (bf16[128,1280]{1,0:T(8,128)(2,1)S(1)}, bf16[128,1280]{1,0:T(8,128)(2,1)S(1)}, u32[]{:S(2)}, u32[]{:S(2)}) collective-permute-start(bf16[128,1280]{1,0:T(8,128)(2,1)S(1)} %pad_maximum_fusion), channel_id=1, source_target_pairs={{2,0},{3,1},{0,2},{1,3},{6,4},{7,5},{4,6},{5,7},{10,8},{11,9},{8,1... | collective-permute-start | bytes 983048 | tf_op jit(solution)/shard_map/ppermute | solution.py:38
  42.8 16.5 %collective-permute-done.3 = bf16[128,1280]{1,0:T(8,128)(2,1)S(1)} collective-permute-done((bf16[128,1280]{1,0:T(8,128)(2,1)S(1)}, bf16[128,1280]{1,0:T(8,128)(2,1)S(1)}, u32[]{:S(2)}, u32[]{:S(2)}) %collective-permute-start.3) | collective-permute-done | bytes 327712 | tf_op jit(solution)/shard_map/ppermute | solution.py:38
  59.3 3.3 %collective-permute-done.4 = bf16[128,1280]{1,0:T(8,128)(2,1)S(1)} collective-permute-done((bf16[128,1280]{1,0:T(8,128)(2,1)S(1)}, bf16[128,1280]{1,0:T(8,128)(2,1)S(1)}, u32[]{:S(2)}, u32[]{:S(2)}) %collective-permute-start.4) | collective-permute-done | bytes 327712 | tf_op jit(solution)/shard_map/ppermute | solution.py:38
  62.8 5.5 %collective-permute-start.6 = (bf16[128,1280]{1,0:T(8,128)(2,1)S(1)}, bf16[128,1280]{1,0:T(8,128)(2,1)S(1)}, u32[]{:S(2)}, u32[]{:S(2)}) collective-permute-start(bf16[128,1280]{1,0:T(8,128)(2,1)S(1)} %slice.15), channel_id=1, source_target_pairs={{3,0},{0,1},{1,2},{2,3},{7,4},{4,5},{5,6},{6,7},{11,8},{8,9},{9,10... | collective-permute-start | bytes 983048 | tf_op jit(solution)/shard_map/ppermute | solution.py:38
  68.4 1.4 %collective-permute-start.10 = (bf16[256,1280]{1,0:T(8,128)(2,1)S(1)}, bf16[256,1280]{1,0:T(8,128)(2,1)S(1)}, u32[]{:S(2)}, u32[]{:S(2)}) collective-permute-start(bf16[256,1280]{1,0:T(8,128)(2,1)S(1)} %get-tuple-element.24), channel_id=1, source_target_pairs={{8,0},{9,1},{10,2},{11,3},{12,4},{13,5},{14,6},{15,7},{16,8},{17,9... | collective-permute-start | bytes 1966088 | tf_op jit(solution)/shard_map/ppermute | solution.py:38
  69.9 2.4 %collective-permute-done.6.refs_6_ = bf16[128,1280]{1,0:T(8,128)(2,1)S(1)} collective-permute-done((bf16[128,1280]{1,0:T(8,128)(2,1)S(1)}, bf16[128,1280]{1,0:T(8,128)(2,1)S(1)}, u32[]{:S(2)}, u32[]{:S(2)}) %collective-permute-start.6) | collective-permute-done | bytes 327712 | tf_op jit(solution)/shard_map/ppermute | solution.py:38
  72.4 1.6 %copy.9 = bf16[32,6,40,128]{3,2,0,1:T(8,128)(2,1)} copy(bf16[32,6,40,128]{3,2,1,0:T(8,128)(2,1)S(1)} %bitcast.14) | data formatting | bytes 3932160 | tf_op jit(solution)/shard_map/reshape | solution.py:65
  74.0 8.4 %collective-permute-done.7.refs_1_ = bf16[256,1280]{1,0:T(8,128)(2,1)S(1)} collective-permute-done((bf16[256,1280]{1,0:T(8,128)(2,1)S(1)}, bf16[256,1280]{1,0:T(8,128)(2,1)S(1)}, u32[]{:S(2)}, u32[]{:S(2)}) %collective-permute-start.7) | collective-permute-done | bytes 655392 | tf_op jit(solution)/shard_map/ppermute | solution.py:38
  82.4 1.2 collective-permute-done.8.refs_2_
  84.5 2.4 %collective-permute-done.11.refs_5_ = bf16[384,1280]{1,0:T(8,128)(2,1)S(1)} collective-permute-done((bf16[384,1280]{1,0:T(8,128)(2,1)S(1)}, bf16[384,1280]{1,0:T(8,128)(2,1)S(1)}, u32[]{:S(2)}, u32[]{:S(2)}) %collective-permute-start.11) | collective-permute-done | bytes 983072 | tf_op jit(solution)/shard_map/ppermute | solution.py:38
  86.8 3.2 %assemble.1 = bf16[64,32,1280]{2,1,0:T(8,128)(2,1)} custom-call(s32[64]{0:T(128)S(1)} %fusion.6.slots, bf16[512,1280]{1,0:T(8,128)(2,1)S(1)} %constant_dynamic-update-slice_fusion.refs_0_, bf16[256,1280]{1,0:T(8,128)(2,1)S(1)} %collective-permute-done.7.refs_1_, bf16[256,1280]{1,0:T(8,128)(2,1)S(1)} %collective-permute-done.8.refs_2_, ...), custom_call_target="tpu_custom_call" | custom-call | tf_op jit(solution)/shard_map/assemble/pallas_call | solution.py:80
  90.1 5.6 %collective-permute-start.12 = (bf16[64,32,1280]{2,1,0:T(8,128)(2,1)}, bf16[64,32,1280]{2,1,0:T(8,128)(2,1)}, u32[]{:S(2)}, u32[]{:S(2)}) collective-permute-start(bf16[64,32,1280]{2,1,0:T(8,128)(2,1)} %assemble.1), channel_id=1, source_target_pairs={{0,32},{1,33},{2,34},{3,35},{4,36},{5,37},{6,38},{7,39},{8,40},{9,... | collective-permute-start | bytes 15728648 | tf_op jit(solution)/shard_map/ppermute | solution.py:413
  95.7 8.0 %rhs_part.1 = bf16[128,32,128]{2,1,0:T(8,128)(2,1)} custom-call(f32[2]{0:T(128)} %dynamic_slice.7.scale_ref, bf16[2048,1280]{1,0:T(8,128)(2,1)} %bitcast.10.own_hbm.pixels_ref, bf16[6,1280,128]{2,1,0:T(8,128)(2,1)} %bitcast.15), custom_call_target="tpu_custom_call" | custom-call | flops 4000000000 | bytes 8000000 | tf_op jit(solution)/shard_map/rhs_part/pallas_call | solution.py:318
  103.7 4.2 %all-to-all-start.1 = ((bf16[128,32,128]{2,1,0:T(8,128)(2,1)}), bf16[128,32,128]{2,1,0:T(8,128)(2,1)S(1)}, u32[]{:S(2)}, u32[]{:S(2)}) async-start(bf16[128,32,128]{2,1,0:T(8,128)(2,1)} %rhs_part.1), calls=%async_computation.1 | async-start | bytes 2097152 | tf_op jit(solution)/shard_map/all_to_all | solution.py:417
  107.9 24.4 %gram.1.after_ref = f32[90,11520]{1,0:T(8,128)} custom-call(s32[1]{0:T(128)} %bitcast.first_ref, bf16[2048,1280]{1,0:T(8,128)(2,1)} %bitcast.10.own_hbm.pixels_ref, bf16[2048,1280]{1,0:T(8,128)(2,1)} %bitcast.11.other_hbm, bf16[16,1280]{1,0:T(8,128)(2,1)} %fusion.3.pick_ref, bf16[96,144]{1,0:T(8,128)(2,1)} %fusion.1.order_ref, ...), custom_call_target="tpu_custom_call" | custom-call | flops 20000000000 | bytes 20000000 | tf_op jit(solution)/shard_map/gram/pallas_call | solution.py:175
  132.3 1.6 %finish.1 = f32[90,1280]{1,0:T(8,128)} custom-call(bf16[128,32,128]{2,1,0:T(8,128)(2,1)S(1)} %all-to-all-done.1.sent_ref, f32[90,11520]{1,0:T(8,128)} %gram.1.after_ref), custom_call_target="tpu_custom_call" | custom-call | tf_op jit(solution)/shard_map/finish/pallas_call | solution.py:368
  (47 shorter events, 12.7 us)
Async XLA Ops:
  2.4 30.7 %collective-permute-start.2 = (bf16[32,1280]{1,0:T(8,128)(2,1)S(1)}, bf16[32,1280]{1,0:T(8,128)(2,1)S(1)}, u32[]{:S(2)}, u32[]{:S(2)}) collective-permute-start(bf16[32,1280]{1,0:T(8,128)(2,1)S(1)} %bitcast.16), channel_id=1, source_target_pairs={{92,0},{93,1},{94,2},{95,3},{24,4},{25,5},{26,6},{27,7},{68,8},{69... | collective-permute-start | bytes 245768 | tf_op jit(solution)/shard_map/ppermute | solution.py:38
  5.9 27.2 %collective-permute-start.1 = (bf16[32,1280]{1,0:T(8,128)(2,1)S(1)}, bf16[32,1280]{1,0:T(8,128)(2,1)S(1)}, u32[]{:S(2)}, u32[]{:S(2)}) collective-permute-start(bf16[32,1280]{1,0:T(8,128)(2,1)S(1)} %bitcast.17), channel_id=1, source_target_pairs={{80,0},{81,1},{82,2},{83,3},{84,4},{85,5},{86,6},{87,7},{88,8},{89... | collective-permute-start | bytes 245768 | tf_op jit(solution)/shard_map/ppermute | solution.py:38
  11.3 21.7 %collective-permute-start = (bf16[32,1280]{1,0:T(8,128)(2,1)S(1)}, bf16[32,1280]{1,0:T(8,128)(2,1)}, u32[]{:S(2)}, u32[]{:S(2)}) collective-permute-start(bf16[32,1280]{1,0:T(8,128)(2,1)S(1)} %bitcast.18), channel_id=1, source_target_pairs={{12,0},{13,1},{14,2},{15,3},{72,4},{73,5},{74,6},{75,7},{20,8},{21... | collective-permute-start | bytes 245768 | tf_op jit(solution)/shard_map/ppermute | solution.py:38
  18.3 44.4 %all-to-all-start = ((bf16[32,240,128]{2,1,0:T(8,128)(2,1)}), bf16[32,240,128]{2,1,0:T(8,128)(2,1)S(1)}, u32[]{:S(2)}, u32[]{:S(2)}) async-start(bf16[32,240,128]{2,1,0:T(8,128)(2,1)} %pack.1), calls=%async_computation | async-start | bytes 3932160 | tf_op jit(solution)/shard_map/all_to_all | solution.py:57
  34.0 28.7 %collective-permute-start.5 = (bf16[128,1280]{1,0:T(8,128)(2,1)S(1)}, bf16[128,1280]{1,0:T(8,128)(2,1)S(1)}, u32[]{:S(2)}, u32[]{:S(2)}) collective-permute-start(bf16[128,1280]{1,0:T(8,128)(2,1)S(1)} %pad_maximum_fusion), channel_id=1, source_target_pairs={{79,0},{76,1},{77,2},{78,3},{11,4},{8,5},{9,6},{10,7},{87,8},{84,9... | collective-permute-start | bytes 983048 | tf_op jit(solution)/shard_map/ppermute | solution.py:38
  38.4 24.3 %collective-permute-start.4 = (bf16[128,1280]{1,0:T(8,128)(2,1)S(1)}, bf16[128,1280]{1,0:T(8,128)(2,1)S(1)}, u32[]{:S(2)}, u32[]{:S(2)}) collective-permute-start(bf16[128,1280]{1,0:T(8,128)(2,1)S(1)} %pad_maximum_fusion), channel_id=1, source_target_pairs={{2,0},{3,1},{0,2},{1,3},{6,4},{7,5},{4,6},{5,7},{10,8},{11,9},{8,1... | collective-permute-start | bytes 983048 | tf_op jit(solution)/shard_map/ppermute | solution.py:38
  40.8 18.5 %collective-permute-start.3 = (bf16[128,1280]{1,0:T(8,128)(2,1)S(1)}, bf16[128,1280]{1,0:T(8,128)(2,1)S(1)}, u32[]{:S(2)}, u32[]{:S(2)}) collective-permute-start(bf16[128,1280]{1,0:T(8,128)(2,1)S(1)} %pad_maximum_fusion), channel_id=1, source_target_pairs={{29,0},{30,1},{31,2},{28,3},{89,4},{90,5},{91,6},{88,7},{5,8},{6,9... | collective-permute-start | bytes 983048 | tf_op jit(solution)/shard_map/ppermute | solution.py:38
  62.8 9.5 %collective-permute-start.6 = (bf16[128,1280]{1,0:T(8,128)(2,1)S(1)}, bf16[128,1280]{1,0:T(8,128)(2,1)S(1)}, u32[]{:S(2)}, u32[]{:S(2)}) collective-permute-start(bf16[128,1280]{1,0:T(8,128)(2,1)S(1)} %slice.15), channel_id=1, source_target_pairs={{3,0},{0,1},{1,2},{2,3},{7,4},{4,5},{5,6},{6,7},{11,8},{8,9},{9,10... | collective-permute-start | bytes 983048 | tf_op jit(solution)/shard_map/ppermute | solution.py:38
  68.3 18.5 %collective-permute-start.11 = (bf16[384,1280]{1,0:T(8,128)(2,1)S(1)}, bf16[384,1280]{1,0:T(8,128)(2,1)S(1)}, u32[]{:S(2)}, u32[]{:S(2)}) collective-permute-start(bf16[384,1280]{1,0:T(8,128)(2,1)S(1)} %slice.17), channel_id=1, source_target_pairs={{1,0},{2,1},{3,2},{0,3},{5,4},{6,5},{7,6},{4,7},{9,8},{10,9},{11,1... | collective-permute-start | bytes 2949128 | tf_op jit(solution)/shard_map/ppermute | solution.py:38
  68.4 14.0 %collective-permute-start.10 = (bf16[256,1280]{1,0:T(8,128)(2,1)S(1)}, bf16[256,1280]{1,0:T(8,128)(2,1)S(1)}, u32[]{:S(2)}, u32[]{:S(2)}) collective-permute-start(bf16[256,1280]{1,0:T(8,128)(2,1)S(1)} %get-tuple-element.24), channel_id=1, source_target_pairs={{8,0},{9,1},{10,2},{11,3},{12,4},{13,5},{14,6},{15,7},{16,8},{17,9... | collective-permute-start | bytes 1966088 | tf_op jit(solution)/shard_map/ppermute | solution.py:38
  69.8 12.6 %collective-permute-start.7 = (bf16[256,1280]{1,0:T(8,128)(2,1)S(1)}, bf16[256,1280]{1,0:T(8,128)(2,1)S(1)}, u32[]{:S(2)}, u32[]{:S(2)}) collective-permute-start(bf16[256,1280]{1,0:T(8,128)(2,1)S(1)} %get-tuple-element.17), channel_id=1, source_target_pairs={{4,0},{5,1},{6,2},{7,3},{64,4},{65,5},{66,6},{67,7},{12,8},{13,9},... | collective-permute-start | bytes 1966088 | tf_op jit(solution)/shard_map/ppermute | solution.py:38
  69.8 13.8 %collective-permute-start.8 = (bf16[256,1280]{1,0:T(8,128)(2,1)S(1)}, bf16[256,1280]{1,0:T(8,128)(2,1)S(1)}, u32[]{:S(2)}, u32[]{:S(2)}) collective-permute-start(bf16[256,1280]{1,0:T(8,128)(2,1)S(1)} %get-tuple-element.24), channel_id=1, source_target_pairs={{24,0},{25,1},{26,2},{27,3},{28,4},{29,5},{30,6},{31,7},{0,8},{1,9... | collective-permute-start | bytes 1966088 | tf_op jit(solution)/shard_map/ppermute | solution.py:38
  72.3 12.1 %collective-permute-start.9 = (bf16[256,1280]{1,0:T(8,128)(2,1)S(1)}, bf16[256,1280]{1,0:T(8,128)(2,1)S(1)}, u32[]{:S(2)}, u32[]{:S(2)}) collective-permute-start(bf16[256,1280]{1,0:T(8,128)(2,1)S(1)} %get-tuple-element.17), channel_id=1, source_target_pairs={{68,0},{69,1},{70,2},{71,3},{0,4},{1,5},{2,6},{3,7},{76,8},{77,9},... | collective-permute-start | bytes 1966088 | tf_op jit(solution)/shard_map/ppermute | solution.py:38
  90.1 17.9 %collective-permute-start.12 = (bf16[64,32,1280]{2,1,0:T(8,128)(2,1)}, bf16[64,32,1280]{2,1,0:T(8,128)(2,1)}, u32[]{:S(2)}, u32[]{:S(2)}) collective-permute-start(bf16[64,32,1280]{2,1,0:T(8,128)(2,1)} %assemble.1), channel_id=1, source_target_pairs={{0,32},{1,33},{2,34},{3,35},{4,36},{5,37},{6,38},{7,39},{8,40},{9,... | collective-permute-start | bytes 15728648 | tf_op jit(solution)/shard_map/ppermute | solution.py:413
  103.7 28.6 %all-to-all-start.1 = ((bf16[128,32,128]{2,1,0:T(8,128)(2,1)}), bf16[128,32,128]{2,1,0:T(8,128)(2,1)S(1)}, u32[]{:S(2)}, u32[]{:S(2)}) async-start(bf16[128,32,128]{2,1,0:T(8,128)(2,1)} %rhs_part.1), calls=%async_computation.1 | async-start | bytes 2097152 | tf_op jit(solution)/shard_map/all_to_all | solution.py:417

commit v12 on v11

--- a/solution.py
+++ b/solution.py
@@ -46,7 +46,7 @@
 FIRST = [tuple(k * s % 4 for s in STEP) for k in range(4)]
 SECOND = [(0, 0, 0), (1, 1, 3), (0, 2, 0), (3, 3, 1)]
 LEVEL = [vec_add(g, f) for g in SECOND for f in FIRST]
-LAST = [((1, 0, 0), 0, 8), ((0, 0, 3), 8, 16), ((3, 0, 0), 0, 8), ((0, 0, 1), 8, 16), ((0, 1, 0), 0, 12), ((0, 3, 0), 4, 8)]
+LAST = [((1, 0, 0), 0, 8), ((0, 0, 3), 8, 16), ((3, 0, 0), 0, 8), ((0, 0, 1), 8, 16), ((0, 1, 0), 0, 11), ((0, 3, 0), 3, 8)]
 SOURCES = list(LEVEL)
 for away, low, high in LAST:
     SOURCES += [vec_add(away, o) for o in LEVEL[low:high]]
@@ -136,8 +136,8 @@
     def multiply(n):
         lanes = pl.ds(n * 256, 256)
 
-        for m in range(3):
-            acc[pl.ds(m * 288, 288), lanes] = jnp.dot(left[pl.ds(m * 288, 288), :], pixels[:, lanes], preferred_element_type=jnp.float32)
+        for m in range(6):
+            acc[pl.ds(m * 144, 144), lanes] = jnp.dot(left[pl.ds(m * 144, 144), :], pixels[:, lanes], preferred_element_type=jnp.float32)
 
     def interleave(block):
         lanes = pl.ds(block * 128, 128)

time: 134 us -> 136 us (1.015)
  starting transfers between devices: 40.4 us -> 44.5 us
  waiting for transfers between devices: 35.1 us -> 32.6 us
    all_to_all x1, starting transfers between devices: 4.2 us -> 6.73 us  [body(): lax.all_to_all(part, ('blk', 'client'), split_axis=0, concat_axis=0, tile...]
    ppermute x12, waiting for transfers between devices: 35 us -> 32.6 us  [take_from(): return lax.ppermute(value, AXES, pairs)]
  transfers between devices with their start and end apart: 15 -> 15, of which waited for: 7 -> 8; matrix products, arithmetic and copies ran while one was open for 10% -> 10% of each run, Pallas kernels for 28% -> 28%
where the time goes in v12:
time: 136 us; the launch traced here: 135 us
  starting transfers between devices  44.5 us (33%)
  Pallas kernels  42.2 us (31%)
  waiting for transfers between devices  32.6 us (24%)
  other arithmetic  7.92 us (6%)
  local copies, waits for them, and re-layouts  7.12 us (5%)
    ppermute x12, waiting for transfers between devices, take_from(): return lax.ppermute(value, AXES, pairs)  32.6 us
    ppermute x12, starting transfers between devices, take_from(): return lax.ppermute(value, AXES, pairs)  26.5 us
    pallas_call x1, Pallas kernels, gram(): pl.pallas_call(gram_kernel, out_shape=jax.ShapeDtypeStruct((90, 11520), j...  24.1 us
    pallas_call x1, Pallas kernels, rhs_part(): pl.pallas_call(rhs_kernel, out_shape=jax.ShapeDtypeStruct((128, 32, 128),...  8.02 us
    all_to_all x1, starting transfers between devices, body(): lax.all_to_all(part, ('blk', 'client'), split_axis=0, concat_axis=0, tile...  6.73 us
    ppermute x1, starting transfers between devices, body(): other = lax.ppermute(own, AXES, [(d, d ^ 32) for d in range(128)])  6.21 us
    pallas_call x1, Pallas kernels, pack(): pl.pallas_call(pack_kernel, out_shape=jax.ShapeDtypeStruct((32, 240, 128)...  5.31 us
    all_to_all x1, starting transfers between devices, gather_chips(): lax.all_to_all(packed, 'blk', split_axis=0, concat_axis=0, tiled=True)  5.08 us
  transfers between devices with their start and end apart: 15, of which 8 were waited for; matrix products, arithmetic and copies ran while one was open for 10% of the time, Pallas kernels for 28%

profile of v12, /device:TPU:1, one launch (start us, length us, event | category | flops | bytes accessed | tf_op | source)
XLA Modules:
  0.0 135.2 jit_solution(15495138421958564818)
XLA Ops:
  2.4 3.5 %collective-permute-start.2 = (bf16[32,1280]{1,0:T(8,128)(2,1)S(1)}, bf16[32,1280]{1,0:T(8,128)(2,1)S(1)}, u32[]{:S(2)}, u32[]{:S(2)}) collective-permute-start(bf16[32,1280]{1,0:T(8,128)(2,1)S(1)} %bitcast.16), channel_id=1, source_target_pairs={{92,0},{93,1},{94,2},{95,3},{24,4},{25,5},{26,6},{27,7},{68,8},{69... | collective-permute-start | bytes 245768 | tf_op jit(solution)/shard_map/ppermute | solution.py:38
  5.9 5.5 %collective-permute-start.1 = (bf16[32,1280]{1,0:T(8,128)(2,1)S(1)}, bf16[32,1280]{1,0:T(8,128)(2,1)S(1)}, u32[]{:S(2)}, u32[]{:S(2)}) collective-permute-start(bf16[32,1280]{1,0:T(8,128)(2,1)S(1)} %bitcast.17), channel_id=1, source_target_pairs={{80,0},{81,1},{82,2},{83,3},{84,4},{85,5},{86,6},{87,7},{88,8},{89... | collective-permute-start | bytes 245768 | tf_op jit(solution)/shard_map/ppermute | solution.py:38
  11.3 1.6 %collective-permute-start = (bf16[32,1280]{1,0:T(8,128)(2,1)S(1)}, bf16[32,1280]{1,0:T(8,128)(2,1)}, u32[]{:S(2)}, u32[]{:S(2)}) collective-permute-start(bf16[32,1280]{1,0:T(8,128)(2,1)S(1)} %bitcast.18), channel_id=1, source_target_pairs={{12,0},{13,1},{14,2},{15,3},{72,4},{73,5},{74,6},{75,7},{20,8},{21... | collective-permute-start | bytes 245768 | tf_op jit(solution)/shard_map/ppermute | solution.py:38
  12.9 5.3 %pack.1 = bf16[32,240,128]{2,1,0:T(8,128)(2,1)} custom-call(bf16[2,360,1280]{2,1,0:T(8,128)(2,1)} %weights_hbm.1), custom_call_target="tpu_custom_call" | custom-call | flops 1000000000 | bytes 6000000 | tf_op jit(solution)/shard_map/pack/pallas_call | solution.py:222
  18.3 5.1 %all-to-all-start = ((bf16[32,240,128]{2,1,0:T(8,128)(2,1)}), bf16[32,240,128]{2,1,0:T(8,128)(2,1)S(1)}, u32[]{:S(2)}, u32[]{:S(2)}) async-start(bf16[32,240,128]{2,1,0:T(8,128)(2,1)} %pack.1), calls=%async_computation | async-start | bytes 3932160 | tf_op jit(solution)/shard_map/all_to_all | solution.py:57
  27.2 1.5 %fusion.1.order_ref = bf16[96,144]{1,0:T(8,128)(2,1)} fusion(s32[144]{0:T(256)S(1)} %get-tuple-element.26, s32[144]{0:T(256)S(1)} %get-tuple-element.35, s32[96]{0:T(128)} %get-tuple-element.33, s32[96]{0:T(128)} %get-tuple-element.37, s32[144]{0:T(256)S(1)} %get-tuple-element.27, s32[144]{0:T(256)S(1)} %get-tuple-element.34, s32[96]{0:T(128)} %get-tuple-element.32, ...), kind=kLoop, calls=%fused_computation.5 | loop fusion | flops 110592 | bytes 31968 | tf_op jit(solution)/shard_map/convert_element_type | solution.py:400
  31.5 1.5 %broadcast_in_dim.26.scale_ref = f32[4,1024]{1,0:T(4,128)} reshape(f32[4,32,32]{2,1,0:T(8,128)} %broadcast_in_dim.25) | data formatting | bytes 32768 | tf_op jit(solution)/shard_map/broadcast_in_dim | solution.py:403
  34.0 4.4 %collective-permute-start.5 = (bf16[128,1280]{1,0:T(8,128)(2,1)S(1)}, bf16[128,1280]{1,0:T(8,128)(2,1)S(1)}, u32[]{:S(2)}, u32[]{:S(2)}) collective-permute-start(bf16[128,1280]{1,0:T(8,128)(2,1)S(1)} %pad_maximum_fusion), channel_id=1, source_target_pairs={{79,0},{76,1},{77,2},{78,3},{11,4},{8,5},{9,6},{10,7},{87,8},{84,9... | collective-permute-start | bytes 983048 | tf_op jit(solution)/shard_map/ppermute | solution.py:38
  38.4 2.4 %collective-permute-start.4 = (bf16[128,1280]{1,0:T(8,128)(2,1)S(1)}, bf16[128,1280]{1,0:T(8,128)(2,1)S(1)}, u32[]{:S(2)}, u32[]{:S(2)}) collective-permute-start(bf16[128,1280]{1,0:T(8,128)(2,1)S(1)} %pad_maximum_fusion), channel_id=1, source_target_pairs={{2,0},{3,1},{0,2},{1,3},{6,4},{7,5},{4,6},{5,7},{10,8},{11,9},{8,1... | collective-permute-start | bytes 983048 | tf_op jit(solution)/shard_map/ppermute | solution.py:38
  42.8 16.5 %collective-permute-done.3 = bf16[128,1280]{1,0:T(8,128)(2,1)S(1)} collective-permute-done((bf16[128,1280]{1,0:T(8,128)(2,1)S(1)}, bf16[128,1280]{1,0:T(8,128)(2,1)S(1)}, u32[]{:S(2)}, u32[]{:S(2)}) %collective-permute-start.3) | collective-permute-done | bytes 327712 | tf_op jit(solution)/shard_map/ppermute | solution.py:38
  59.3 3.3 %collective-permute-done.4 = bf16[128,1280]{1,0:T(8,128)(2,1)S(1)} collective-permute-done((bf16[128,1280]{1,0:T(8,128)(2,1)S(1)}, bf16[128,1280]{1,0:T(8,128)(2,1)S(1)}, u32[]{:S(2)}, u32[]{:S(2)}) %collective-permute-start.4) | collective-permute-done | bytes 327712 | tf_op jit(solution)/shard_map/ppermute | solution.py:38
  62.8 5.5 %collective-permute-start.6 = (bf16[160,1280]{1,0:T(8,128)(2,1)S(1)}, bf16[160,1280]{1,0:T(8,128)(2,1)S(1)}, u32[]{:S(2)}, u32[]{:S(2)}) collective-permute-start(bf16[160,1280]{1,0:T(8,128)(2,1)S(1)} %slice.15), channel_id=1, source_target_pairs={{3,0},{0,1},{1,2},{2,3},{7,4},{4,5},{5,6},{6,7},{11,8},{8,9},{9,10... | collective-permute-start | bytes 1228808 | tf_op jit(solution)/shard_map/ppermute | solution.py:38
  68.5 1.4 %collective-permute-start.10 = (bf16[256,1280]{1,0:T(8,128)(2,1)S(1)}, bf16[256,1280]{1,0:T(8,128)(2,1)S(1)}, u32[]{:S(2)}, u32[]{:S(2)}) collective-permute-start(bf16[256,1280]{1,0:T(8,128)(2,1)S(1)} %get-tuple-element.24), channel_id=1, source_target_pairs={{8,0},{9,1},{10,2},{11,3},{12,4},{13,5},{14,6},{15,7},{16,8},{17,9... | collective-permute-start | bytes 1966088 | tf_op jit(solution)/shard_map/ppermute | solution.py:38
  70.0 3.2 %collective-permute-done.6.refs_6_ = bf16[160,1280]{1,0:T(8,128)(2,1)S(1)} collective-permute-done((bf16[160,1280]{1,0:T(8,128)(2,1)S(1)}, bf16[160,1280]{1,0:T(8,128)(2,1)S(1)}, u32[]{:S(2)}, u32[]{:S(2)}) %collective-permute-start.6) | collective-permute-done | bytes 409632 | tf_op jit(solution)/shard_map/ppermute | solution.py:38
  74.2 1.6 %copy.9 = bf16[32,6,40,128]{3,2,0,1:T(8,128)(2,1)} copy(bf16[32,6,40,128]{3,2,1,0:T(8,128)(2,1)S(1)} %bitcast.14) | data formatting | bytes 3932160 | tf_op jit(solution)/shard_map/reshape | solution.py:65
  75.8 4.2 %collective-permute-done.7.refs_1_ = bf16[256,1280]{1,0:T(8,128)(2,1)S(1)} collective-permute-done((bf16[256,1280]{1,0:T(8,128)(2,1)S(1)}, bf16[256,1280]{1,0:T(8,128)(2,1)S(1)}, u32[]{:S(2)}, u32[]{:S(2)}) %collective-permute-start.7) | collective-permute-done | bytes 655392 | tf_op jit(solution)/shard_map/ppermute | solution.py:38
  80.6 3.1 %collective-permute-done.8.refs_2_ = bf16[256,1280]{1,0:T(8,128)(2,1)S(1)} collective-permute-done((bf16[256,1280]{1,0:T(8,128)(2,1)S(1)}, bf16[256,1280]{1,0:T(8,128)(2,1)S(1)}, u32[]{:S(2)}, u32[]{:S(2)}) %collective-permute-start.8) | collective-permute-done | bytes 655392 | tf_op jit(solution)/shard_map/ppermute | solution.py:38
  83.7 1.4 %collective-permute-done.11.refs_5_ = bf16[352,1280]{1,0:T(8,128)(2,1)S(1)} collective-permute-done((bf16[352,1280]{1,0:T(8,128)(2,1)S(1)}, bf16[352,1280]{1,0:T(8,128)(2,1)S(1)}, u32[]{:S(2)}, u32[]{:S(2)}) %collective-permute-start.11) | collective-permute-done | bytes 901152 | tf_op jit(solution)/shard_map/ppermute | solution.py:38
  85.4 3.2 %assemble.1 = bf16[64,32,1280]{2,1,0:T(8,128)(2,1)} custom-call(s32[64]{0:T(128)S(1)} %fusion.6.slots, bf16[512,1280]{1,0:T(8,128)(2,1)S(1)} %constant_dynamic-update-slice_fusion.refs_0_, bf16[256,1280]{1,0:T(8,128)(2,1)S(1)} %collective-permute-done.7.refs_1_, bf16[256,1280]{1,0:T(8,128)(2,1)S(1)} %collective-permute-done.8.refs_2_, ...), custom_call_target="tpu_custom_call" | custom-call | tf_op jit(solution)/shard_map/assemble/pallas_call | solution.py:80
  88.6 6.2 %collective-permute-start.12 = (bf16[64,32,1280]{2,1,0:T(8,128)(2,1)}, bf16[64,32,1280]{2,1,0:T(8,128)(2,1)}, u32[]{:S(2)}, u32[]{:S(2)}) collective-permute-start(bf16[64,32,1280]{2,1,0:T(8,128)(2,1)} %assemble.1), channel_id=1, source_target_pairs={{0,32},{1,33},{2,34},{3,35},{4,36},{5,37},{6,38},{7,39},{8,40},{9,... | collective-permute-start | bytes 15728648 | tf_op jit(solution)/shard_map/ppermute | solution.py:413
  94.8 8.0 %rhs_part.1 = bf16[128,32,128]{2,1,0:T(8,128)(2,1)} custom-call(f32[2]{0:T(128)} %dynamic_slice.7.scale_ref, bf16[2048,1280]{1,0:T(8,128)(2,1)} %bitcast.10.own_hbm.pixels_ref, bf16[6,1280,128]{2,1,0:T(8,128)(2,1)} %bitcast.15), custom_call_target="tpu_custom_call" | custom-call | flops 4000000000 | bytes 8000000 | tf_op jit(solution)/shard_map/rhs_part/pallas_call | solution.py:318
  102.8 6.7 %all-to-all-start.1 = ((bf16[128,32,128]{2,1,0:T(8,128)(2,1)}), bf16[128,32,128]{2,1,0:T(8,128)(2,1)S(1)}, u32[]{:S(2)}, u32[]{:S(2)}) async-start(bf16[128,32,128]{2,1,0:T(8,128)(2,1)} %rhs_part.1), calls=%async_computation.1 | async-start | bytes 2097152 | tf_op jit(solution)/shard_map/all_to_all | solution.py:417
  109.5 24.1 %gram.1.after_ref = f32[90,11520]{1,0:T(8,128)} custom-call(s32[1]{0:T(128)} %bitcast.first_ref, bf16[2048,1280]{1,0:T(8,128)(2,1)} %bitcast.10.own_hbm.pixels_ref, bf16[2048,1280]{1,0:T(8,128)(2,1)} %bitcast.11.other_hbm, bf16[16,1280]{1,0:T(8,128)(2,1)} %fusion.3.pick_ref, bf16[96,144]{1,0:T(8,128)(2,1)} %fusion.1.order_ref, ...), custom_call_target="tpu_custom_call" | custom-call | flops 20000000000 | bytes 20000000 | tf_op jit(solution)/shard_map/gram/pallas_call | solution.py:175
  133.6 1.6 %finish.1 = f32[90,1280]{1,0:T(8,128)} custom-call(bf16[128,32,128]{2,1,0:T(8,128)(2,1)S(1)} %all-to-all-done.1.sent_ref, f32[90,11520]{1,0:T(8,128)} %gram.1.after_ref), custom_call_target="tpu_custom_call" | custom-call | tf_op jit(solution)/shard_map/finish/pallas_call | solution.py:368
  (47 shorter events, 13.6 us)
Async XLA Ops:
  2.4 30.7 %collective-permute-start.2 = (bf16[32,1280]{1,0:T(8,128)(2,1)S(1)}, bf16[32,1280]{1,0:T(8,128)(2,1)S(1)}, u32[]{:S(2)}, u32[]{:S(2)}) collective-permute-start(bf16[32,1280]{1,0:T(8,128)(2,1)S(1)} %bitcast.16), channel_id=1, source_target_pairs={{92,0},{93,1},{94,2},{95,3},{24,4},{25,5},{26,6},{27,7},{68,8},{69... | collective-permute-start | bytes 245768 | tf_op jit(solution)/shard_map/ppermute | solution.py:38
  5.9 27.2 %collective-permute-start.1 = (bf16[32,1280]{1,0:T(8,128)(2,1)S(1)}, bf16[32,1280]{1,0:T(8,128)(2,1)S(1)}, u32[]{:S(2)}, u32[]{:S(2)}) collective-permute-start(bf16[32,1280]{1,0:T(8,128)(2,1)S(1)} %bitcast.17), channel_id=1, source_target_pairs={{80,0},{81,1},{82,2},{83,3},{84,4},{85,5},{86,6},{87,7},{88,8},{89... | collective-permute-start | bytes 245768 | tf_op jit(solution)/shard_map/ppermute | solution.py:38
  11.3 21.7 %collective-permute-start = (bf16[32,1280]{1,0:T(8,128)(2,1)S(1)}, bf16[32,1280]{1,0:T(8,128)(2,1)}, u32[]{:S(2)}, u32[]{:S(2)}) collective-permute-start(bf16[32,1280]{1,0:T(8,128)(2,1)S(1)} %bitcast.18), channel_id=1, source_target_pairs={{12,0},{13,1},{14,2},{15,3},{72,4},{73,5},{74,6},{75,7},{20,8},{21... | collective-permute-start | bytes 245768 | tf_op jit(solution)/shard_map/ppermute | solution.py:38
  18.3 44.4 %all-to-all-start = ((bf16[32,240,128]{2,1,0:T(8,128)(2,1)}), bf16[32,240,128]{2,1,0:T(8,128)(2,1)S(1)}, u32[]{:S(2)}, u32[]{:S(2)}) async-start(bf16[32,240,128]{2,1,0:T(8,128)(2,1)} %pack.1), calls=%async_computation | async-start | bytes 3932160 | tf_op jit(solution)/shard_map/all_to_all | solution.py:57
  34.0 28.7 %collective-permute-start.5 = (bf16[128,1280]{1,0:T(8,128)(2,1)S(1)}, bf16[128,1280]{1,0:T(8,128)(2,1)S(1)}, u32[]{:S(2)}, u32[]{:S(2)}) collective-permute-start(bf16[128,1280]{1,0:T(8,128)(2,1)S(1)} %pad_maximum_fusion), channel_id=1, source_target_pairs={{79,0},{76,1},{77,2},{78,3},{11,4},{8,5},{9,6},{10,7},{87,8},{84,9... | collective-permute-start | bytes 983048 | tf_op jit(solution)/shard_map/ppermute | solution.py:38
  38.4 24.3 %collective-permute-start.4 = (bf16[128,1280]{1,0:T(8,128)(2,1)S(1)}, bf16[128,1280]{1,0:T(8,128)(2,1)S(1)}, u32[]{:S(2)}, u32[]{:S(2)}) collective-permute-start(bf16[128,1280]{1,0:T(8,128)(2,1)S(1)} %pad_maximum_fusion), channel_id=1, source_target_pairs={{2,0},{3,1},{0,2},{1,3},{6,4},{7,5},{4,6},{5,7},{10,8},{11,9},{8,1... | collective-permute-start | bytes 983048 | tf_op jit(solution)/shard_map/ppermute | solution.py:38
  40.8 18.5 %collective-permute-start.3 = (bf16[128,1280]{1,0:T(8,128)(2,1)S(1)}, bf16[128,1280]{1,0:T(8,128)(2,1)S(1)}, u32[]{:S(2)}, u32[]{:S(2)}) collective-permute-start(bf16[128,1280]{1,0:T(8,128)(2,1)S(1)} %pad_maximum_fusion), channel_id=1, source_target_pairs={{29,0},{30,1},{31,2},{28,3},{89,4},{90,5},{91,6},{88,7},{5,8},{6,9... | collective-permute-start | bytes 983048 | tf_op jit(solution)/shard_map/ppermute | solution.py:38
  62.8 10.4 %collective-permute-start.6 = (bf16[160,1280]{1,0:T(8,128)(2,1)S(1)}, bf16[160,1280]{1,0:T(8,128)(2,1)S(1)}, u32[]{:S(2)}, u32[]{:S(2)}) collective-permute-start(bf16[160,1280]{1,0:T(8,128)(2,1)S(1)} %slice.15), channel_id=1, source_target_pairs={{3,0},{0,1},{1,2},{2,3},{7,4},{4,5},{5,6},{6,7},{11,8},{8,9},{9,10... | collective-permute-start | bytes 1228808 | tf_op jit(solution)/shard_map/ppermute | solution.py:38
  68.3 16.8 %collective-permute-start.11 = (bf16[352,1280]{1,0:T(8,128)(2,1)S(1)}, bf16[352,1280]{1,0:T(8,128)(2,1)S(1)}, u32[]{:S(2)}, u32[]{:S(2)}) collective-permute-start(bf16[352,1280]{1,0:T(8,128)(2,1)S(1)} %slice.17), channel_id=1, source_target_pairs={{1,0},{2,1},{3,2},{0,3},{5,4},{6,5},{7,6},{4,7},{9,8},{10,9},{11,1... | collective-permute-start | bytes 2703368 | tf_op jit(solution)/shard_map/ppermute | solution.py:38
  68.4 11.6 %collective-permute-start.7 = (bf16[256,1280]{1,0:T(8,128)(2,1)S(1)}, bf16[256,1280]{1,0:T(8,128)(2,1)S(1)}, u32[]{:S(2)}, u32[]{:S(2)}) collective-permute-start(bf16[256,1280]{1,0:T(8,128)(2,1)S(1)} %get-tuple-element.17), channel_id=1, source_target_pairs={{4,0},{5,1},{6,2},{7,3},{64,4},{65,5},{66,6},{67,7},{12,8},{13,9},... | collective-permute-start | bytes 1966088 | tf_op jit(solution)/shard_map/ppermute | solution.py:38
  68.5 12.1 %collective-permute-start.10 = (bf16[256,1280]{1,0:T(8,128)(2,1)S(1)}, bf16[256,1280]{1,0:T(8,128)(2,1)S(1)}, u32[]{:S(2)}, u32[]{:S(2)}) collective-permute-start(bf16[256,1280]{1,0:T(8,128)(2,1)S(1)} %get-tuple-element.24), channel_id=1, source_target_pairs={{8,0},{9,1},{10,2},{11,3},{12,4},{13,5},{14,6},{15,7},{16,8},{17,9... | collective-permute-start | bytes 1966088 | tf_op jit(solution)/shard_map/ppermute | solution.py:38
  69.8 13.8 %collective-permute-start.8 = (bf16[256,1280]{1,0:T(8,128)(2,1)S(1)}, bf16[256,1280]{1,0:T(8,128)(2,1)S(1)}, u32[]{:S(2)}, u32[]{:S(2)}) collective-permute-start(bf16[256,1280]{1,0:T(8,128)(2,1)S(1)} %get-tuple-element.24), channel_id=1, source_target_pairs={{24,0},{25,1},{26,2},{27,3},{28,4},{29,5},{30,6},{31,7},{0,8},{1,9... | collective-permute-start | bytes 1966088 | tf_op jit(solution)/shard_map/ppermute | solution.py:38
  73.2 12.1 %collective-permute-start.9 = (bf16[256,1280]{1,0:T(8,128)(2,1)S(1)}, bf16[256,1280]{1,0:T(8,128)(2,1)S(1)}, u32[]{:S(2)}, u32[]{:S(2)}) collective-permute-start(bf16[256,1280]{1,0:T(8,128)(2,1)S(1)} %get-tuple-element.17), channel_id=1, source_target_pairs={{68,0},{69,1},{70,2},{71,3},{0,4},{1,5},{2,6},{3,7},{76,8},{77,9},... | collective-permute-start | bytes 1966088 | tf_op jit(solution)/shard_map/ppermute | solution.py:38
  88.6 21.0 %collective-permute-start.12 = (bf16[64,32,1280]{2,1,0:T(8,128)(2,1)}, bf16[64,32,1280]{2,1,0:T(8,128)(2,1)}, u32[]{:S(2)}, u32[]{:S(2)}) collective-permute-start(bf16[64,32,1280]{2,1,0:T(8,128)(2,1)} %assemble.1), channel_id=1, source_target_pairs={{0,32},{1,33},{2,34},{3,35},{4,36},{5,37},{6,38},{7,39},{8,40},{9,... | collective-permute-start | bytes 15728648 | tf_op jit(solution)/shard_map/ppermute | solution.py:413
  102.8 30.8 %all-to-all-start.1 = ((bf16[128,32,128]{2,1,0:T(8,128)(2,1)}), bf16[128,32,128]{2,1,0:T(8,128)(2,1)S(1)}, u32[]{:S(2)}, u32[]{:S(2)}) async-start(bf16[128,32,128]{2,1,0:T(8,128)(2,1)} %rhs_part.1), calls=%async_computation.1 | async-start | bytes 2097152 | tf_op jit(solution)/shard_map/all_to_all | solution.py:417
